TPU v7x, 32 devices: a whole 2x2x4 slice. The times are simulated.
32 devices in a mesh: table: 4 (over y, x), ctx: 8 (over z, core).
Axes of the slice: x: 2, y: 2, z: 4, core: 2. Of those that a mesh axis runs over, the one named last changes fastest.
Arguments:
- item_local: int32 [4, 2048], P('table', 'ctx'), may hold values from 0 to 511
- item_owner: int32 [4, 2048, 1], P('table', 'ctx'), may hold values from 0 to 3; in each aligned block of 256 rows (0 to 255, 256 to 511, ..., all dimensions but the last counted through in order) at most 128 rows name the same one
- hist_len: int32 [4], P('table'), may hold values from 512 to 2048, as said below
- table: bfloat16 [2048, 512], P('table'), may hold values from -6 to 6
- gain: float32 [512], replicated, may hold values from 0.1 to 1.9
- w_query: bfloat16 [512, 512], replicated, may hold values from -0.25 to 0.25
- w_key: bfloat16 [512, 512], replicated, may hold values from -0.25 to 0.25
- w_value: bfloat16 [512, 512], replicated, may hold values from -0.25 to 0.25
- w_out: bfloat16 [512, 512], replicated, may hold values from -0.25 to 0.25
- rate: float32 [8], replicated, may hold values from 0.0009765625 to 0.05
- d_out: bfloat16 [4, 2048, 512], P('table', 'ctx'), may hold values from -6 to 6
Outputs:
- output: bfloat16 [4, 2048, 512], P('table', 'ctx')
- table_grad: bfloat16 [2048, 512], P('table')
Inputs may be any that keep to these rules, and one draw needn't show every extreme that they name: `item_owner`: among the 256 positions of one device at most 128 name the same owner, and some device's positions reach 128. `hist_len`: each length is a multiple of 64; some user's history fills all 2048 positions.
All inputs are finite; a program needn't handle non-finite values.
Results may differ from a plain program's by a relative error of at most 0.009.
Values may be sent and summed in bfloat16 or wider, within the bound.
No kernel may reach another device: no remote copies, remote signals or barrier semaphores. Data moves between devices by JAX's collectives and lax.ppermute only.
A program may use at most 64 MiB of HBM per device.

v0:
```python
import math

import jax
import jax.numpy as jnp
from jax import lax
from jax.sharding import PartitionSpec as P

EPS = 1e-06
HIGHEST = lax.Precision.HIGHEST


def inv_rms(tensor):
    return lax.rsqrt(jnp.mean(tensor * tensor, axis=-1, keepdims=True) + EPS)


def norm_back(tensor, factor, upstream, scale):
    return (
        scale
        * factor
        * (
            upstream
            - tensor * factor * factor * jnp.mean(tensor * upstream, axis=-1, keepdims=True)
        )
    )


def precise(form, left, right):
    return jnp.einsum(form, left, right, precision=HIGHEST)


def back_dot(upstream, matrix):
    return lax.dot_general(
        upstream, matrix, (((1,), (1,)), ((), ())), preferred_element_type=jnp.float32
    )


def decay_tables(rate, length):
    position = jnp.arange(length, dtype=jnp.float32)
    distance = position[:, None] - position[None, :]
    within = jnp.where(
        distance[None] >= 0.0, jnp.exp(-rate[:, None, None] * jnp.maximum(distance, 0.0)[None]), 0.0
    )
    entering = jnp.exp(-rate[None, :] * (position[:, None] + 1.0))
    leaving = jnp.exp(-rate[None, :] * (length - 1.0 - position[:, None]))
    return (within, entering, leaving)


def attention_pass(
    queries, keys_unit, values_in, grad_out, state_in, adjoint_in, within, entering, leaving
):
    scores = precise("thd,shd->hts", queries, keys_unit) * within
    attended = precise("hts,shd->thd", scores, values_in) + entering[:, :, None] * precise(
        "thi,hij->thj", queries, state_in
    )
    pair_grads = precise("thd,shd->hts", grad_out, values_in) * within
    grad_queries = precise("hts,shd->thd", pair_grads, keys_unit) + entering[:, :, None] * precise(
        "thj,hij->thi", grad_out, state_in
    )
    grad_keys = precise("hts,thd->shd", pair_grads, queries) + leaving[:, :, None] * precise(
        "shj,hij->shi", values_in, adjoint_in
    )
    grad_values = precise("hts,thd->shd", scores, grad_out) + leaving[:, :, None] * precise(
        "shi,hij->shj", keys_unit, adjoint_in
    )
    return (attended, grad_queries, grad_keys, grad_values)


def group_states(queries, keys_unit, values_in, grad_out, entering, leaving):
    carried = precise("shi,shj->hij", keys_unit * leaving[:, :, None], values_in)
    adjoint = precise("thi,thj->hij", queries * entering[:, :, None], grad_out)
    return (carried, adjoint)


def local(
    item_local, item_owner, hist_len, table, gain, w_query, w_key, w_value, w_out, rate, d_out
):
    tables = lax.axis_size("table")
    length = item_local.shape[1]
    width = table.shape[1]
    heads = rate.shape[0]
    head_size = width // heads
    capacity = 2 * length // tables
    key_scale = 1.0 / math.sqrt(head_size)
    owners = item_owner[0, :, 0]
    local_ids = item_local[0]
    row_ids = owners * table.shape[0] + local_ids
    order = jnp.arange(length, dtype=jnp.int32)
    same = row_ids[:, None] == row_ids[None, :]
    earlier = jnp.any(same & (order[None, :] < order[:, None]), axis=1)
    leading = jnp.logical_not(earlier)
    hits = (owners[:, None] == jnp.arange(tables, dtype=jnp.int32)[None, :]).astype(jnp.int32)
    slots = jnp.sum((jnp.cumsum(hits, axis=0) - 1) * hits, axis=1)
    requests = (
        jnp.full((tables, capacity), -1, jnp.int32).at[owners, slots].set(local_ids, mode="drop")
    )
    asked = lax.all_to_all(requests, "table", split_axis=0, concat_axis=0, tiled=True)
    found = jnp.take(table, jnp.maximum(asked, 0), axis=0)
    found = jnp.where((asked >= 0)[:, :, None], found, jnp.zeros_like(found))
    fetched = lax.all_to_all(found, "table", split_axis=0, concat_axis=0, tiled=True)
    embedded = fetched[owners, slots]
    position = lax.axis_index("ctx") * length + order
    validity = (position < hist_len[0]).astype(jnp.float32)[:, None]
    mask_heads = validity[:, :, None]
    inputs_f = embedded.astype(jnp.float32)
    rstd = inv_rms(inputs_f)
    normed = (inputs_f * rstd * gain).astype(jnp.bfloat16)
    query_raw = jnp.dot(normed, w_query, preferred_element_type=jnp.float32).reshape(
        length, heads, head_size
    )
    key_raw = jnp.dot(normed, w_key, preferred_element_type=jnp.float32).reshape(
        length, heads, head_size
    )
    value_raw = jnp.dot(normed, w_value, preferred_element_type=jnp.float32).reshape(
        length, heads, head_size
    )
    query_rms = inv_rms(query_raw)
    key_rms = inv_rms(key_raw)
    queries = query_raw * query_rms / head_size
    keys_unit = key_raw * key_rms * key_scale * mask_heads
    values_in = value_raw * mask_heads
    grad_masked = d_out[0] * validity.astype(jnp.bfloat16)
    grad_out = back_dot(grad_masked, w_out).reshape(length, heads, head_size)
    within, entering, leaving = decay_tables(rate, length)
    carried, adjoint = group_states(queries, keys_unit, values_in, grad_out, entering, leaving)
    flat_shape = (heads, head_size * head_size)
    own_index = lax.axis_index("ctx").astype(jnp.float32)
    pieces = (
        lax.all_gather(carried.reshape((1,) + flat_shape), "ctx", axis=0, tiled=True),
        lax.all_gather(adjoint.reshape((1,) + flat_shape), "ctx", axis=0, tiled=True),
    )
    count = pieces[0].shape[0]
    block_index = jnp.arange(count, dtype=jnp.int32).astype(jnp.float32)
    before = own_index - 1.0 - block_index
    after = block_index - own_index - 1.0
    weight_before = jnp.where(
        before[:, None] >= 0.0,
        jnp.exp(-rate[None, :] * length * jnp.maximum(before, 0.0)[:, None]),
        0.0,
    )
    weight_after = jnp.where(
        after[:, None] >= 0.0,
        jnp.exp(-rate[None, :] * length * jnp.maximum(after, 0.0)[:, None]),
        0.0,
    )
    state_flat = jnp.sum(weight_before[:, :, None] * pieces[0], axis=0)
    adjoint_flat = jnp.sum(weight_after[:, :, None] * pieces[1], axis=0)
    state_in = state_flat.reshape(heads, head_size, head_size)
    adjoint_in = adjoint_flat.reshape(heads, head_size, head_size)
    attended, grad_queries, grad_keys, grad_values = attention_pass(
        queries, keys_unit, values_in, grad_out, state_in, adjoint_in, within, entering, leaving
    )
    attended_b = attended.reshape(length, width).astype(jnp.bfloat16)
    output = (inputs_f + jnp.dot(attended_b, w_out, preferred_element_type=jnp.float32)).astype(
        jnp.bfloat16
    )
    d_query = (
        norm_back(query_raw, query_rms, grad_queries, 1.0 / head_size)
        .reshape(length, width)
        .astype(jnp.bfloat16)
    )
    d_key = (
        (mask_heads * norm_back(key_raw, key_rms, grad_keys, key_scale))
        .reshape(length, width)
        .astype(jnp.bfloat16)
    )
    d_value = (mask_heads * grad_values).reshape(length, width).astype(jnp.bfloat16)
    d_normed = back_dot(d_query, w_query) + back_dot(d_key, w_key) + back_dot(d_value, w_value)
    row_grad = grad_masked.astype(jnp.float32) + norm_back(inputs_f, rstd, d_normed * gain, 1.0)
    summed = jnp.dot(same.astype(jnp.float32), row_grad, precision=HIGHEST)
    sending = jnp.where(leading[:, None], summed, jnp.zeros_like(summed))
    outgoing = (
        jnp.zeros((tables, capacity, width), jnp.float32)
        .at[owners, slots]
        .set(sending, mode="drop")
    )
    arrived = lax.all_to_all(outgoing, "table", split_axis=0, concat_axis=0, tiled=True)
    selector = (
        asked.reshape(-1)[None, :] == jnp.arange(table.shape[0], dtype=jnp.int32)[:, None]
    ).astype(jnp.float32)
    owner_rows = jnp.dot(selector, arrived.reshape(-1, width), precision=HIGHEST)
    table_grad = lax.psum(owner_rows, "ctx").astype(jnp.bfloat16)
    return (output[None], table_grad)


def solution(mesh):
    return jax.shard_map(
        local,
        mesh=mesh,
        in_specs=(
            P("table", "ctx"),
            P("table", "ctx", None),
            P("table"),
            P("table", None),
            P(),
            P(),
            P(),
            P(),
            P(),
            P(),
            P("table", "ctx", None),
        ),
        out_specs=(P("table", "ctx", None), P("table", None)),
        check_vma=False,
    )
```

profile of v0, /device:TPU:0, one launch (start us, length us, event | category | flops | bytes accessed | tf_op | source)
XLA Modules:
  0.0 262.1 jit_solution(5084500324281298224)
XLA Ops:
  11.5 38.3 %scatter_fusion = s32[4,128]{1,0:T(4,128)} fusion(s32[4,128]{1,0:T(4,128)} %broadcast_in_dim.63, s32[256]{0:T(256)S(1)} %bitcast.146, s32[256]{0:T(256)} %bitcast.166), kind=kCustom, calls=%fused_computation.2 | custom fusion | bytes 5120 | tf_op jit(solution)/shard_map/scatter | solution.py:94
  49.8 5.2 %all-to-all-start = ((s32[4,1,128]{2,1,0:T(1,128)}), s32[4,1,128]{2,1,0:T(1,128)S(1)}, u32[]{:S(2)}, u32[]{:S(2)}) async-start(s32[4,1,128]{2,1,0:T(1,128)} %bitcast.9), calls=%async_computation | async-start | bytes 4096 | tf_op jit(solution)/shard_map/all_to_all | solution.py:96
  55.5 4.1 %all-to-all-done = s32[4,1,128]{2,1,0:T(1,128)S(1)} async-done(((s32[4,1,128]{2,1,0:T(1,128)}), s32[4,1,128]{2,1,0:T(1,128)S(1)}, u32[]{:S(2)}, u32[]{:S(2)}) %all-to-all-start) | async-done | bytes 2080 | tf_op jit(solution)/shard_map/all_to_all | solution.py:96
  59.6 2.0 gather_fusion
  62.6 3.5 %all-to-all-start.1 = ((bf16[4,128,512]{2,1,0:T(8,128)(2,1)}), bf16[4,128,512]{2,1,0:T(8,128)(2,1)S(1)}, u32[]{:S(2)}, u32[]{:S(2)}) async-start(bf16[4,128,512]{2,1,0:T(8,128)(2,1)} %select_select_fusion), calls=%async_computation.1 | async-start | bytes 1048576 | tf_op jit(solution)/shard_map/all_to_all | solution.py:99
  67.4 5.6 %all-to-all-done.1 = bf16[4,128,512]{2,1,0:T(8,128)(2,1)S(1)} async-done(((bf16[4,128,512]{2,1,0:T(8,128)(2,1)}), bf16[4,128,512]{2,1,0:T(8,128)(2,1)S(1)}, u32[]{:S(2)}, u32[]{:S(2)}) %all-to-all-start.1) | async-done | bytes 524320 | tf_op jit(solution)/shard_map/all_to_all | solution.py:99
  73.0 2.1 gather_fusion.1
  78.8 1.5 fusion.95
  80.3 3.6 %fusion = f32[8,256,256]{2,1,0:T(8,128)} fusion(f32[256,8,64]{0,2,1:T(8,128)S(1)} %fusion.45, f32[256,256]{1,0:T(8,128)S(1)} %fusion.51, f32[8]{0:T(128)S(1)} %get-tuple-element.18, pred[256,256]{1,0:T(8,128)(4,1)S(1)} %fusion.52, f32[256,8,64]{0,2,1:T(8,128)S(1)} %bitcast.153, f32[256]{0:T(256)S(1)} %fusion.82), kind=kOutput, calls=%fused_computation.5 | convolution fusion | flops 404357120 | bytes 3474464 | tf_op jit(solution)/shard_map/thd,shd->hts/dot_general | solution.py:28
  83.9 15.9 %all-gather.5.cloned.1.call-done = f32[8,8,4096]{2,1,0:T(8,128)} async-done(((f32[1,8,4096]{2,1,0:T(8,128)}), f32[8,8,4096]{2,1,0:T(8,128)}) %all-gather.5.cloned.1.call-update) | async-done | bytes 1048592 | tf_op jit(solution)/shard_map/all_gather | solution.py:129
  99.7 2.0 multiply_reduce_fusion
  103.4 3.9 %multiply_reduce_fusion.2 = (f32[256,8]{0,1:T(8,128)S(1)}, f32[256,8]{0,1:T(8,128)S(1)}, f32[256,8,64]{0,2,1:T(8,128)}) fusion(f32[256,512]{0,1:T(8,128)S(1)} %fusion.91, f32[256,8,64]{0,2,1:T(8,128)S(1)} %fusion.9, f32[8,256,256]{2,1,0:T(8,128)} %fusion, f32[256,8,64]{0,2,1:T(8,128)S(1)} %bitcast.149, f32[256,8]{0,1:T(8,128)S(1)} %get-tuple-element.9), kind=kOutput, calls=%fused_computation.50 | convolution fusion | flops 403566592 | bytes 4218880 | tf_op jit(solution)/shard_map/hts,thd->shd/dot_general | solution.py:28
  108.6 1.7 reshape.418
  113.1 1.9 multiply_convert_fusion
  115.1 2.9 %fusion.1 = f32[8,256,256]{2,1,0:T(8,128)S(1)} fusion(f32[256,256]{1,0:T(8,128)S(1)} %fusion.51, f32[8]{0:T(128)} %copy-done.19, pred[256,256]{1,0:T(8,128)(4,1)S(1)} %fusion.52, f32[256,8,64]{0,2,1:T(8,128)S(1)} %bitcast.150, f32[256,512]{0,1:T(8,128)S(1)} %fusion.91, f32[256]{0:T(256)S(1)} %fusion.81, f32[256,8]{0,1:T(8,128)S(1)} %get-tuple-element.7, ...), kind=kOutput, calls=%fused_computation.6 | convolution fusion | flops 404750336 | bytes 3490848 | tf_op jit(solution)/shard_map/thd,shd->hts/dot_general | solution.py:28
  120.7 11.6 %all-gather.3.cloned.1.call-done = f32[8,8,4096]{2,1,0:T(8,128)} async-done(((f32[1,8,4096]{2,1,0:T(8,128)}), f32[8,8,4096]{2,1,0:T(8,128)}) %all-gather.3.cloned.1.call-update) | async-done | bytes 1048592 | tf_op jit(solution)/shard_map/all_gather | solution.py:128
  134.4 3.9 %multiply_reduce_fusion.3 = (f32[256,8]{0,1:T(8,128)S(1)}, f32[256,8,64]{0,2,1:T(8,128)S(1)}) fusion(f32[256,512]{0,1:T(8,128)S(1)} %get-tuple-element.20, f32[256,8,64]{0,2,1:T(8,128)S(1)} %fusion.8, f32[8,256,256]{2,1,0:T(8,128)} %fusion, f32[256,512]{0,1:T(8,128)S(1)} %fusion.91, f32[256]{0:T(256)S(1)} %fusion.81, f32[256,8]{0,1:T(8,128)S(1)} %get-tuple-element.7), kind=kOutput, calls=%fused_computation.54 | convolution fusion | flops 403306496 | bytes 4211712 | tf_op jit(solution)/shard_map/hts,shd->thd/dot_general | solution.py:28
  142.1 33.9 %scatter_fusion.1 = f32[4,128,512]{2,1,0:T(8,128)} fusion(f32[4,128,512]{2,1,0:T(8,128)} %broadcast_in_dim.73, s32[256]{0:T(256)S(1)} %bitcast.147, f32[256,512]{1,0:T(8,128)S(1)} %convolution_select_fusion), kind=kCustom, calls=%fused_computation.3 | custom fusion | bytes 1574912 | tf_op jit(solution)/shard_map/scatter | solution.py:174
  176.0 4.4 %all-to-all-start.2 = ((f32[4,128,512]{2,1,0:T(8,128)}), f32[4,128,512]{2,1,0:T(8,128)}, u32[]{:S(2)}, u32[]{:S(2)}) async-start(f32[4,128,512]{2,1,0:T(8,128)} %scatter_fusion.1), calls=%async_computation.2 | async-start | bytes 2097152 | tf_op jit(solution)/shard_map/all_to_all | solution.py:176
  180.4 1.6 fusion.7
  182.0 3.1 %fusion.14 = bf16[256,8,64]{0,2,1:T(8,128)(2,1)S(1)} fusion(f32[256,8,64]{0,2,1:T(8,128)S(1)} %fusion.7, f32[8,256,256]{2,1,0:T(8,128)S(1)} %copy-done.3, f32[256,8,64]{0,2,1:T(8,128)} %bitcast.156, f32[256]{0:T(256)S(1)} %fusion.82), kind=kOutput, calls=%fused_computation.31 | convolution fusion | flops 403046400 | bytes 3408896 | tf_op jit(solution)/shard_map/hts,shd->thd/dot_general | solution.py:28
  186.2 8.8 %all-to-all-done.2 = f32[4,128,512]{2,1,0:T(8,128)} async-done(((f32[4,128,512]{2,1,0:T(8,128)}), f32[4,128,512]{2,1,0:T(8,128)}, u32[]{:S(2)}, u32[]{:S(2)}) %all-to-all-start.2) | async-done | bytes 1048608 | tf_op jit(solution)/shard_map/all_to_all | solution.py:176
  195.0 2.3 fusion.16
  197.3 58.0 %all-reduce.1 = bf16[512,512]{1,0:T(8,128)(2,1)} all-reduce(f32[512,512]{1,0:T(8,128)S(1)} %fusion.16), channel_id=1, replica_groups=mesh['table'=4,'ctx'=8] {'ctx'}, use_global_device_ids=true, to_apply=%region_14.15 | all-reduce | flops 262144 | bytes 1572864 | tf_op jit(solution)/shard_map/psum | solution.py:181
  (120 shorter events, 25.2 us)
Async XLA Ops:
  7.2 59.8 %copy-start = (bf16[512,512]{1,0:T(8,128)(2,1)S(1)}, bf16[512,512]{1,0:T(8,128)(2,1)}, u32[]{:S(2)}) copy-start(bf16[512,512]{1,0:T(8,128)(2,1)} %param.19) | copy-start | bytes 1572868
  7.2 47.8 %copy-start.27 = (f32[8]{0:T(128)S(1)}, f32[8]{0:T(128)}, u32[]{:S(2)}) copy-start(f32[8]{0:T(128)} %param.20) | copy-start | bytes 100
  7.2 52.4 %copy-start.1 = (bf16[512,512]{1,0:T(8,128)(2,1)S(1)}, bf16[512,512]{1,0:T(8,128)(2,1)}, u32[]{:S(2)}) copy-start(bf16[512,512]{1,0:T(8,128)(2,1)} %param.14) | copy-start | bytes 1572868
  49.8 9.7 %all-to-all-start = ((s32[4,1,128]{2,1,0:T(1,128)}), s32[4,1,128]{2,1,0:T(1,128)S(1)}, u32[]{:S(2)}, u32[]{:S(2)}) async-start(s32[4,1,128]{2,1,0:T(1,128)} %bitcast.9), calls=%async_computation | async-start | bytes 4096 | tf_op jit(solution)/shard_map/all_to_all | solution.py:96
  55.5 24.8 %copy-start.19 = (f32[8]{0:T(128)}, f32[8]{0:T(128)S(1)}, u32[]{:S(2)}) copy-start(f32[8]{0:T(128)S(1)} %get-tuple-element.18) | copy-start | bytes 100
  61.6 5.4 %copy-start.12 = (bf16[1,256,512]{2,1,0:T(8,128)(2,1)S(1)}, bf16[1,256,512]{2,1,0:T(8,128)(2,1)}, u32[]{:S(2)}) copy-start(bf16[1,256,512]{2,1,0:T(8,128)(2,1)} %param.21) | copy-start | bytes 786436
  62.6 10.4 %all-to-all-start.1 = ((bf16[4,128,512]{2,1,0:T(8,128)(2,1)}), bf16[4,128,512]{2,1,0:T(8,128)(2,1)S(1)}, u32[]{:S(2)}, u32[]{:S(2)}) async-start(bf16[4,128,512]{2,1,0:T(8,128)(2,1)} %select_select_fusion), calls=%async_computation.1 | async-start | bytes 1048576 | tf_op jit(solution)/shard_map/all_to_all | solution.py:99
  66.1 9.1 %copy-start.9 = (bf16[512,512]{1,0:T(8,128)(2,1)S(1)}, bf16[512,512]{1,0:T(8,128)(2,1)}, u32[]{:S(2)}) copy-start(bf16[512,512]{1,0:T(8,128)(2,1)} %param.16) | copy-start | bytes 1572868
  66.1 9.1 %copy-start.14 = (f32[512]{0:T(512)S(1)}, f32[512]{0:T(512)}, u32[]{:S(2)}) copy-start(f32[512]{0:T(512)} %param.15) | copy-start | bytes 6148
  66.1 33.6 %all-gather.5.cloned.1.call-start = ((), (), s32[]{:S(2)}) async-start(), calls=%async_computation.4 | async-start | bytes 1179648 | tf_op jit(solution)/shard_map/all_gather | solution.py:129
  67.0 6.0 %copy-start.24 = (bf16[256]{0:T(256)(128)(2,1)}, bf16[256]{0:T(256)(128)(2,1)S(1)}, u32[]{:S(2)}) copy-start(bf16[256]{0:T(256)(128)(2,1)S(1)} %fusion.90) | copy-start | bytes 1540
  75.1 2.6 copy-start.26
  75.1 3.2 %copy-start.6 = (bf16[512,512]{1,0:T(8,128)(2,1)S(1)}, bf16[512,512]{1,0:T(8,128)(2,1)}, u32[]{:S(2)}) copy-start(bf16[512,512]{1,0:T(8,128)(2,1)} %param.17) | copy-start | bytes 1572868
  75.3 3.5 %copy-start.17 = (f32[256]{0:T(256)}, f32[256]{0:T(256)S(1)}, u32[]{:S(2)}) copy-start(f32[256]{0:T(256)S(1)} %add_rsqrt_fusion.2) | copy-start | bytes 3076
  77.2 55.1 %all-gather.3.cloned.1.call-start = ((), (), s32[]{:S(2)}) async-start(), calls=%async_computation.3 | async-start | bytes 1179648 | tf_op jit(solution)/shard_map/all_gather | solution.py:128
  80.2 27.0 %copy-start.4 = (f32[256,512]{0,1:T(8,128)}, f32[256,512]{0,1:T(8,128)S(1)}, u32[]{:S(2)}) copy-start(f32[256,512]{0,1:T(8,128)S(1)} %fusion.95) | copy-start | bytes 1572868
  103.3 7.0 %copy-start.15 = (s32[1,256,1]{1,2,0:T(1,128)S(1)}, s32[1,256,1]{1,2,0:T(1,128)}, u32[]{:S(2)}) copy-start(s32[1,256,1]{1,2,0:T(1,128)} %param.12) | copy-start | bytes 3076
  111.1 1.4 copy-start.20
  119.3 13.0 %copy-start.16 = (f32[8,8]{1,0:T(8,128)S(1)}, f32[8,8]{1,0:T(8,128)}, u32[]{:S(2)}) copy-start(f32[8,8]{1,0:T(8,128)} %get-tuple-element.15) | copy-start | bytes 772
  133.8 4.5 %copy-start.5 = (f32[8,64,64]{2,1,0:T(8,128)}, f32[8,64,64]{2,1,0:T(8,128)S(1)}, u32[]{:S(2)}) copy-start(f32[8,64,64]{2,1,0:T(8,128)S(1)} %reshape.419) | copy-start | bytes 393220
  134.4 4.1 %copy-start.10 = (bf16[512,512]{1,0:T(8,128)(2,1)S(1)}, bf16[512,512]{1,0:T(8,128)(2,1)}, u32[]{:S(2)}) copy-start(bf16[512,512]{1,0:T(8,128)(2,1)} %param.16) | copy-start | bytes 1572868
  138.3 1.4 copy-start.8
  176.0 6.0 %copy-start.3 = (f32[8,256,256]{2,1,0:T(8,128)S(1)}, f32[8,256,256]{2,1,0:T(8,128)}, u32[]{:S(2)}) copy-start(f32[8,256,256]{2,1,0:T(8,128)} %copy-done.2) | copy-start | bytes 6291460
  176.0 18.9 %all-to-all-start.2 = ((f32[4,128,512]{2,1,0:T(8,128)}), f32[4,128,512]{2,1,0:T(8,128)}, u32[]{:S(2)}, u32[]{:S(2)}) async-start(f32[4,128,512]{2,1,0:T(8,128)} %scatter_fusion.1), calls=%async_computation.2 | async-start | bytes 2097152 | tf_op jit(solution)/shard_map/all_to_all | solution.py:176
  (10 other events, 12.6 us)
Sparse Core Ops, SparseCore 0:
  77.3 22.3 all-gather.4
  110.5 21.7 all-gather.2
where the time goes:
time: 265 us; the launch traced here: 262 us
  local copies, waits for them, and re-layouts  83.8 us (32%)
  blocking collectives  58 us (22%)
  waiting for transfers between devices  45.9 us (17%)
  matrix products  32.2 us (12%)
  between operations  15.3 us (6%)
  other arithmetic  13.6 us (5%)
  starting transfers between devices  13.3 us (5%)
    psum x1, blocking collectives, local(): table_grad = lax.psum(owner_rows, 'ctx').astype(jnp.bfloat16)  58 us
    scatter x1, local copies, waits for them, and re-layouts, local(): jnp.full((tables, capacity), -1, jnp.int32).at[owners, slots]  38.3 us
    scatter x1, local copies, waits for them, and re-layouts, local(): outgoing = jnp.zeros((tables, capacity, width), jnp.float32).at[owners, s...  33.9 us
    dot_general x12, matrix products, precise(): return jnp.einsum(form, left, right, precision=HIGHEST)  24.3 us
    all_gather x1, waiting for transfers between devices, local(): lax.all_gather(adjoint.reshape((1,) + flat_shape), 'ctx', axis=0, tiled=T...  15.9 us
    all_gather x1, waiting for transfers between devices, local(): lax.all_gather(carried.reshape((1,) + flat_shape), 'ctx', axis=0, tiled=T...  11.6 us
    all_to_all x1, waiting for transfers between devices, local(): lax.all_to_all(outgoing, 'table', split_axis=0, concat_axis=0, tiled=True)  8.78 us
    all_to_all x1, waiting for transfers between devices, local(): lax.all_to_all(found, 'table', split_axis=0, concat_axis=0, tiled=True)  5.59 us
  transfers between devices with their start and end apart: 5, of which 5 were waited for; matrix products, arithmetic and copies ran while one was open for 8% of the time, Pallas kernels for 0%

commit v1 on v0

v1 whole, which is shorter than its diff:
```python
import functools
import math

import jax
import jax.numpy as jnp
from jax import lax
from jax.experimental import pallas as pl
from jax.experimental.pallas import tpu as pltpu
from jax.sharding import PartitionSpec as P

EPS = 1e-06
F32 = jnp.float32
BF16 = jnp.bfloat16
MIB = 1 << 20


def dot(left, right, ways=(1, 0)):
    return lax.dot_general(
        left, right, (((ways[0],), (ways[1],)), ((), ())), preferred_element_type=F32
    )


def dot_nt(left, right):
    return dot(left, right, (1, 1))


def dot_tn(left, right):
    return dot(left, right, (0, 0))


def call(body, info, operands, specs, outs, flops, name):
    whole = [
        pl.BlockSpec(x.shape, functools.partial(lambda n, i, s: (0,) * n, x.ndim))
        if spec is None
        else spec
        for x, spec in zip(operands, specs)
    ]
    moved = sum(math.prod(x.shape) * x.dtype.itemsize for x in (*operands, *outs))
    return pl.pallas_call(
        body,
        grid_spec=pltpu.PrefetchScalarGridSpec(
            num_scalar_prefetch=1,
            grid=(1,),
            in_specs=whole,
            out_specs=[
                pl.BlockSpec(o.shape, functools.partial(lambda n, i, s: (0,) * n, len(o.shape)))
                for o in outs
            ],
        ),
        out_shape=outs,
        compiler_params=pltpu.CompilerParams(vmem_limit_bytes=56 * MIB),
        cost_estimate=pl.CostEstimate(flops=flops, bytes_accessed=moved, transcendentals=0),
        name=name,
    )(info, *operands)


def iota(shape, dim):
    return lax.broadcasted_iota(jnp.int32, shape, dim)


def head_of(shape, dim, size):
    return iota(shape, dim) // size


def valid_col(info, offset, length):
    position = offset + iota((length, 1), 0)
    return (position < info[3]).astype(F32)


def decay(rate, offset, length, chip):
    centre = (chip - 1) / 2.0
    moment = (offset + iota((length, rate.shape[1]), 0)).astype(F32) - centre
    return jnp.exp(-rate * moment), jnp.exp(rate * moment)


def prepare(length, tables, rows, cap, info, d_own, d_oth, w_out, ids_col, ids_row, g, dest, meta):
    mine, core, z = info[0], info[1], info[2]
    for j, d_ref in enumerate((d_own, d_oth)):
        side = core if j == 0 else 1 - core
        valid = valid_col(info, (2 * z + side) * length, length)
        g[j] = (dot_nt(d_ref[...], w_out[...]) * valid).astype(BF16)
        column = ids_col[j]
        row = ids_row[j : j + 1, :]
        owner_row = row // rows
        local_row = row - owner_row * rows
        order = iota((length, length), 0) < iota((length, length), 1)
        same = jnp.where((column // rows == owner_row) & order, 1.0, 0.0)
        slot = jnp.sum(same, axis=0, keepdims=True).astype(jnp.int32)
        where_to = (owner_row ^ mine) * cap + slot
        dest[j : j + 1, :] = where_to
        high = local_row // 32
        pick = iota((16, length), 0)
        coded = jnp.where(
            pick == 0, high + 1, jnp.where(pick == 1, local_row - high * 32, 0)
        )
        coded = coded.astype(F32).astype(BF16)
        for m in range(tables):
            hit = iota((cap, length), 0) + m * cap == where_to
            hit = jnp.where(hit, 1.0, 0.0).astype(BF16)
            meta[m, j] = dot_nt(coded, hit).astype(BF16)


def project(
    length, tables, rows, size, chips, info, ids_col, gain, w_q, w_k, w_v, g, rate, table, *refs
):
    parts, outs = refs[: 2 * (tables - 1)], refs[2 * (tables - 1) :]
    emb, q_raw, k_raw, v_out = outs[:4]
    sends = outs[4:]
    mine, core, z = info[0], info[1], info[2]
    half = w_q.shape[1]
    part = rows // 2
    blocks = [(table, mine * rows)]
    for m in range(1, tables):
        blocks.append((parts[m - 1], (mine ^ m) * rows + core * part))
        blocks.append((parts[tables - 1 + m - 1], (mine ^ m) * rows + (1 - core) * part))
    mean_of = jnp.where(
        head_of((half, half), 0, size) == head_of((half, half), 1, size), 1.0 / size, 0.0
    ).astype(BF16)
    carried = jnp.zeros((half, half), F32)
    adjoint = jnp.zeros((half, half), F32)
    for j in range(2):
        side = core if j == 0 else 1 - core
        column = ids_col[j]
        x = jnp.zeros((length, table.shape[1]), F32)
        for ref, base in blocks:
            count = ref.shape[0]
            hit = column - base == iota((length, count), 1)
            x = x + dot(jnp.where(hit, 1.0, 0.0).astype(BF16), ref[...])
        emb[j] = x.astype(BF16)
        rstd = lax.rsqrt(jnp.mean(x * x, axis=1, keepdims=True) + EPS)
        normed = (x * rstd * gain[...]).astype(BF16)
        valid = valid_col(info, (2 * z + side) * length, length)
        qr = dot(normed, w_q[...])
        kr = dot(normed, w_k[...])
        v = (dot(normed, w_v[...]) * valid).astype(BF16)
        q_raw[j] = qr.astype(BF16)
        k_raw[j] = kr.astype(BF16)
        v_out[j] = v
        falling, rising = decay(rate[...], side * length, length, 2 * length)
        q_rms = lax.rsqrt(dot((qr * qr).astype(BF16), mean_of) + EPS)
        k_rms = lax.rsqrt(dot((kr * kr).astype(BF16), mean_of) + EPS)
        qa = (qr * q_rms * falling / size).astype(BF16)
        kb = (kr * k_rms * rising * (valid / math.sqrt(size))).astype(BF16)
        carried = carried + dot_tn(kb, v)
        adjoint = adjoint + dot_tn(qa, g[j])
    lane_head = head_of((size, half), 1, size)

    def packed(full):
        return sum(
            jnp.where(lane_head == h, full[h * size : (h + 1) * size, :], 0.0)
            for h in range(half // size)
        )

    carried, adjoint = packed(carried), packed(adjoint)
    for bit, ref in enumerate(sends):
        low = ((z >> bit) & 1) == 0
        ref[...] = jnp.where(low, carried, adjoint).astype(BF16)


def scaled_inputs(length, size, info, j, rate, mean_of, q_raw, k_raw, v, g):
    core, z = info[1], info[2]
    side = core if j == 0 else 1 - core
    valid = valid_col(info, (2 * z + side) * length, length)
    falling, rising = decay(rate[...], side * length, length, 2 * length)
    qr = q_raw[j].astype(F32)
    kr = k_raw[j].astype(F32)
    q_rms = lax.rsqrt(dot((qr * qr).astype(BF16), mean_of) + EPS)
    k_rms = lax.rsqrt(dot((kr * kr).astype(BF16), mean_of) + EPS)
    qn = qr * q_rms
    kn = kr * k_rms * valid
    q = qn / size
    k = kn / math.sqrt(size)
    qa = (q * falling).astype(BF16)
    kb = (k * rising).astype(BF16)
    ga = (g[j].astype(F32) * falling).astype(BF16)
    vb = (v[j].astype(F32) * rising).astype(BF16)
    return qn, kn, q_rms, k_rms, q, k, qa, kb, ga, vb, valid


def attend(length, size, info, rate, q_raw, k_raw, v_in, g_in, att, gq, gk, gv):
    core = info[1]
    half = q_raw.shape[2]
    same_head = head_of((half, half), 0, size) == head_of((half, half), 1, size)
    mean_of = jnp.where(same_head, 1.0 / size, 0.0).astype(BF16)
    lane_head = head_of((length, half), 1, size)
    causal = iota((length, length), 0) >= iota((length, length), 1)
    anti = iota((length, length), 0) <= iota((length, length), 1)
    kept, states = [], []
    for j in range(2):
        _, _, _, _, q, k, qa, kb, ga, vb, _ = scaled_inputs(
            length, size, info, j, rate, mean_of, q_raw, k_raw, v_in, g_in
        )
        v, g = v_in[j], g_in[j]
        q, k = q.astype(BF16), k.astype(BF16)
        kept.append((qa, kb, ga, vb))
        states.append(
            (
                jnp.where(same_head, dot_tn(kb, v), 0.0),
                jnp.where(same_head, dot_tn(qa, g), 0.0),
            )
        )
        zero = jnp.zeros_like(v)
        sums = [jnp.zeros((length, half), F32) for _ in range(4)]
        for h in range(half // size):
            mine = lane_head == h

            def only(tensor):
                return jnp.where(mine, tensor, zero)

            def pairs(left, right, mask):
                return jnp.where(mask, dot_nt(only(left), right), 0.0).astype(BF16)

            sums[0] += dot(pairs(qa, kb, causal), only(v))
            sums[1] += dot(pairs(ga, vb, causal), only(k))
            sums[2] += dot(pairs(vb, ga, anti), only(q))
            sums[3] += dot(pairs(kb, qa, anti), only(g))
        kept[j] += (sums,)
    for j in range(2):
        qa, kb, ga, vb, sums = kept[j]
        later = (core if j == 0 else 1 - core).astype(F32)
        state = (states[1 - j][0] * later).astype(BF16)
        back = (states[1 - j][1] * (1.0 - later)).astype(BF16)
        att[j] = (sums[0] + dot(qa, state)).astype(BF16)
        gq[j] = (sums[1] + dot_nt(ga, state)).astype(BF16)
        gk[j] = (sums[2] + dot_nt(vb, back)).astype(BF16)
        gv[j] = (sums[3] + dot(kb, back)).astype(BF16)


def finish(
    length, size, chips, info, rate, q_raw, k_raw, v_in, g_in, att, gq, gk, gv,
    emb, gain, w_q, w_k, w_v, d_own, d_oth, *refs
):
    came, (att_own, att_oth, row_keep, row_send) = refs[: chips - 1], refs[chips - 1 :]
    core, z = info[1], info[2]
    half = q_raw.shape[2]
    same_head = head_of((half, half), 0, size) == head_of((half, half), 1, size)
    mean_of = jnp.where(same_head, 1.0 / size, 0.0).astype(BF16)
    state = jnp.zeros((size, half), F32)
    back = jnp.zeros((size, half), F32)
    for m in range(1, chips):
        peer = z ^ m
        apart = jnp.abs(peer - z).astype(F32) * (2.0 * length)
        piece = came[m - 1][...].astype(F32) * jnp.exp(-rate[...] * apart)
        before = peer < z
        state = state + jnp.where(before, piece, 0.0)
        back = back + jnp.where(before, 0.0, piece)

    def spread(packed):
        return jnp.where(same_head, jnp.concatenate([packed] * (half // size), 0), 0.0).astype(BF16)

    state, back = spread(state), spread(back)
    keep_at = pl.multiple_of(core * half, half)
    send_at = pl.multiple_of((1 - core) * half, half)
    for j, d_ref in enumerate((d_own, d_oth)):
        qn, kn, q_rms, k_rms, _, _, qa, kb, ga, vb, valid = scaled_inputs(
            length, size, info, j, rate, mean_of, q_raw, k_raw, v_in, g_in
        )
        attended = (att[j].astype(F32) + dot(qa, state)).astype(BF16)
        (att_own if j == 0 else att_oth)[...] = attended
        grad_q = gq[j].astype(F32) + dot_nt(ga, state)
        grad_k = gk[j].astype(F32) + dot_nt(vb, back)
        grad_v = gv[j].astype(F32) + dot(kb, back)
        d_q = q_rms / size * (grad_q - qn * dot((qn * grad_q).astype(BF16), mean_of))
        d_k = k_rms * (valid / math.sqrt(size)) * (
            grad_k - kn * dot((kn * grad_k).astype(BF16), mean_of)
        )
        d_q, d_k, d_v = d_q.astype(BF16), d_k.astype(BF16), (grad_v * valid).astype(BF16)
        x = emb[j].astype(F32)
        rstd = lax.rsqrt(jnp.mean(x * x, axis=1, keepdims=True) + EPS)
        scaled = []
        total = jnp.zeros((length, 1), F32)
        for at in (keep_at, send_at):
            rows = pl.ds(at, half)
            d_normed = dot_nt(d_q, w_q[rows, :]) + dot_nt(d_k, w_k[rows, :]) + dot_nt(d_v, w_v[rows, :])
            d_normed = d_normed * gain[:, rows]
            part = emb[j, :, rows].astype(F32)
            scaled.append((d_normed, part))
            total = total + jnp.sum(d_normed * part, axis=1, keepdims=True)
        pull = total * (rstd * rstd / (2 * half))
        kept = rstd * (scaled[0][0] - scaled[0][1] * pull)
        row_keep[j] = kept + d_ref[:, pl.ds(keep_at, half)].astype(F32) * valid
        row_send[1 - j] = (rstd * (scaled[1][0] - scaled[1][1] * pull)).astype(BF16)


def compact(length, tables, cap, info, row_keep, row_came, dest, meta, *outs):
    for j in range(2):
        grads = (row_keep[j] + row_came[j].astype(F32)).astype(BF16)
        where_to = dest[j : j + 1, :]
        for m in range(tables):
            hit = iota((cap, length), 0) + m * cap == where_to
            hit = jnp.where(hit, 1.0, 0.0).astype(BF16)
            outs[m][j * cap : (j + 1) * cap, :] = dot(hit, grads).astype(BF16)
    for m in range(tables):
        for j in range(2):
            base = 2 * cap + 16 * j
            outs[m][base : base + 16, :] = jnp.zeros((16, outs[m].shape[1]), BF16)
            outs[m][base : base + 16, 0:cap] = meta[m, j]


def result(info, emb, att_own, att_came, w_out, out):
    core = info[1]
    half = att_own.shape[1]
    own = pl.ds(pl.multiple_of(core * half, half), half)
    other = pl.ds(pl.multiple_of((1 - core) * half, half), half)
    total = dot(att_own[...], w_out[own, :]) + dot(att_came[...], w_out[other, :])
    out[...] = (emb[0].astype(F32) + total).astype(BF16)


def owner_sum(tables, rows, cap, chips, info, *refs):
    came, outs, acc = refs[:tables], refs[tables : tables + chips], refs[tables + chips]
    z = info[2]
    total = None
    for m in range(tables):
        for j in range(2):
            base = 2 * cap + 16 * j
            coded = came[m][base : base + 16, 0:cap].astype(F32)
            number = ((coded[0:1, :] - 1.0) * 32.0 + coded[1:2, :]).astype(jnp.int32)
            hit = jnp.where(iota((rows, cap), 0) == number, 1.0, 0.0).astype(BF16)
            part = dot(hit, came[m][j * cap : (j + 1) * cap, :])
            total = part if total is None else total + part
    acc[...] = total
    share = rows // chips
    for m in range(chips):
        at = pl.multiple_of((z ^ m) * share, share)
        outs[m][...] = acc[pl.ds(at, share), :].astype(BF16)


def add_up(chips, info, *refs):
    total = refs[0][...].astype(F32)
    for m in range(1, chips):
        total = total + refs[m][...].astype(F32)
    refs[chips][...] = total.astype(BF16)


def assemble(chips, share, half, info, *refs):
    own, other, out, sem = refs[:chips], refs[chips : 2 * chips], refs[2 * chips], refs[2 * chips + 1]
    core, z = info[1], info[2]
    copies = []
    for m in range(chips):
        rows = pl.ds(pl.multiple_of((z ^ m) * share, share), share)
        for n, (ref, side) in enumerate(((own[m], core), (other[m], 1 - core))):
            columns = pl.ds(pl.multiple_of(side * half, half), half)
            copies.append(
                pltpu.make_async_copy(ref, out.at[rows, columns], sem.at[2 * m + n])
            )
    for copy in copies:
        copy.start()
    for copy in copies:
        copy.wait()


def local(
    item_local, item_owner, hist_len, table, gain, w_query, w_key, w_value, w_out, rate, d_out
):
    tables = lax.axis_size("table")
    count = lax.axis_size("ctx")
    length = item_local.shape[1]
    rows, width = table.shape
    heads = rate.shape[0]
    size = width // heads
    half = width // 2
    chips = count // 2
    cap = 2 * length // tables
    mine = lax.axis_index("table")
    block = lax.axis_index("ctx")
    core = block % 2
    z = block // 2

    def over_table(x, m):
        return lax.ppermute(x, "table", [(i, i ^ m) for i in range(tables)])

    def over_z(x, m):
        return lax.ppermute(x, "ctx", [(i, i ^ (2 * m)) for i in range(count)])

    def swap(x):
        return lax.ppermute(x, "ctx", [(i, i ^ 1) for i in range(count)])

    def array(shape, dtype):
        return jax.ShapeDtypeStruct(shape, dtype)

    info = jnp.stack([mine, core, z, hist_len[0]]).astype(jnp.int32)
    part = rows // 2
    part_own = lax.dynamic_slice(table, (core * part, 0), (part, width))
    parts = [over_table(part_own, m) for m in range(1, tables)]
    parts_other = [swap(p) for p in parts]

    ids = item_owner[:, :, 0] * rows + item_local
    ids_row = jnp.concatenate([ids, swap(ids)], 0)
    ids_col = ids_row[:, :, None]
    d_own = d_out[0]
    d_oth = swap(d_own)
    gain_row = gain[None, :]
    rate_row = lax.dynamic_slice(jnp.repeat(rate, size), (core * half,), (half,))[None, :]

    column_half = pl.BlockSpec((width, half), lambda i, s: (0, s[1]))
    row_half = pl.BlockSpec((half, width), lambda i, s: (s[1], 0))

    g, dest, meta = call(
        functools.partial(prepare, length, tables, rows, cap),
        info,
        (d_own, d_oth, w_out, ids_col, ids_row),
        (None, None, row_half, None, None),
        [
            array((2, length, half), BF16),
            array((2, length), jnp.int32),
            array((tables, 2, 16, cap), BF16),
        ],
        4 * length * width * half,
        "prepare",
    )
    bits = max(chips - 1, 1).bit_length() if chips > 1 else 0
    emb, q_raw, k_raw, v, *sends = call(
        functools.partial(project, length, tables, rows, size, chips),
        info,
        (ids_col, gain_row, w_query, w_key, w_value, g, rate_row, table, *parts, *parts_other),
        (None, None, column_half, column_half, column_half) + (None,) * (3 + 2 * (tables - 1)),
        [array((2, length, width), BF16)]
        + [array((2, length, half), BF16)] * 3
        + [array((size, half), BF16)] * bits,
        4 * length * tables * rows * width,
        "project",
    )
    came = [over_z(sends[m.bit_length() - 1], m) for m in range(1, chips)]
    att, gq, gk, gv = call(
        functools.partial(attend, length, size),
        info,
        (rate_row, q_raw, k_raw, v, g),
        (None,) * 5,
        [array((2, length, half), BF16)] * 4,
        32 * length * length * half,
        "attend",
    )
    att_own, att_oth, row_keep, row_send = call(
        functools.partial(finish, length, size, chips),
        info,
        (rate_row, q_raw, k_raw, v, g, att, gq, gk, gv, emb, gain_row, w_query, w_key, w_value,
         d_own, d_oth, *came),
        (None,) * 11 + (column_half,) * 3 + (None,) * (2 + chips - 1),
        [array((length, half), BF16)] * 2
        + [array((2, length, half), F32), array((2, length, half), BF16)],
        12 * length * width * half,
        "finish",
    )
    row_came = swap(row_send)
    att_came = swap(att_oth)
    outgoing = call(
        functools.partial(compact, length, tables, cap),
        info,
        (row_keep, row_came, dest, meta),
        (None,) * 4,
        [array((2 * cap + 32, half), BF16)] * tables,
        4 * length * 2 * length * half,
        "compact",
    )
    arrived = [outgoing[0]] + [over_table(outgoing[m], m) for m in range(1, tables)]
    (output,) = call(
        result,
        info,
        (emb, att_own, att_came, w_out),
        (pl.BlockSpec((1, length, width), lambda i, s: (0, 0, 0)), None, None, None),
        [array((length, width), BF16)],
        2 * length * width * width,
        "result",
    )
    share = rows // chips
    everything = pl.pallas_call(
        functools.partial(owner_sum, tables, rows, cap, chips),
        grid_spec=pltpu.PrefetchScalarGridSpec(
            num_scalar_prefetch=1,
            grid=(1,),
            in_specs=[pl.BlockSpec(x.shape, lambda i, s: (0, 0)) for x in arrived],
            out_specs=[pl.BlockSpec((share, half), lambda i, s: (0, 0))] * chips,
            scratch_shapes=[pltpu.VMEM((rows, half), F32)],
        ),
        out_shape=[array((share, half), BF16)] * chips,
        compiler_params=pltpu.CompilerParams(vmem_limit_bytes=56 * MIB),
        cost_estimate=pl.CostEstimate(
            flops=4 * rows * length * tables * half, bytes_accessed=MIB, transcendentals=0
        ),
        name="owner_sum",
    )(info, *arrived)
    pieces = [everything[0]] + [over_z(everything[m], m) for m in range(1, chips)]
    (summed,) = call(
        functools.partial(add_up, chips),
        info,
        pieces,
        (None,) * chips,
        [array((share, half), BF16)],
        chips * share * half,
        "add_up",
    )
    own = [summed] + [over_z(summed, m) for m in range(1, chips)]
    other = [swap(x) for x in own]
    table_grad = pl.pallas_call(
        functools.partial(assemble, chips, share, half),
        grid_spec=pltpu.PrefetchScalarGridSpec(
            num_scalar_prefetch=1,
            grid=(1,),
            in_specs=[pl.BlockSpec(memory_space=pl.ANY)] * (2 * chips),
            out_specs=pl.BlockSpec(memory_space=pl.ANY),
            scratch_shapes=[pltpu.SemaphoreType.DMA((2 * chips,))],
        ),
        out_shape=array((rows, width), BF16),
        name="assemble",
    )(info, *own, *other)
    return (output[None], table_grad)


def solution(mesh):
    return jax.shard_map(
        local,
        mesh=mesh,
        in_specs=(
            P("table", "ctx"),
            P("table", "ctx", None),
            P("table"),
            P("table", None),
            P(),
            P(),
            P(),
            P(),
            P(),
            P(),
            P("table", "ctx", None),
        ),
        out_specs=(P("table", "ctx", None), P("table", None)),
        check_vma=False,
    )
```

time: 265 us -> 115 us (0.43)
  local copies, waits for them, and re-layouts: 83.8 us -> 8.84 us
  blocking collectives: 58 us -> 0 us
  Pallas kernels: 0 us -> 50.6 us
  matrix products: 32.2 us -> 0 us
  waiting for transfers between devices: 45.9 us -> 29.6 us
  between operations: 15.3 us -> 1.55 us
  other arithmetic: 13.6 us -> 1.19 us
  starting transfers between devices: 13.3 us -> 22.4 us
    scatter x2 -> x0, local copies, waits for them, and re-layouts: 72.2 us -> none  [the longest x1 38.3 us: local(): jnp.full((tables, capacity), -1, jnp.int32).at[owners, slots]]
    psum x1 -> x0, blocking collectives: 58 us -> none  [local(): table_grad = lax.psum(owner_rows, 'ctx').astype(jnp.bfloat16)]
    pallas_call x0 -> x9, Pallas kernels: none -> 50.6 us  [the longest x7 29.6 us: call(): pl.pallas_call(body, grid_spec=pltpu.PrefetchScalarGridSpec(num_scalar_pr...]
    dot_general x22 -> x0, matrix products: 32.2 us -> none  [the longest x12 24.3 us: precise(): return jnp.einsum(form, left, right, precision=HIGHEST)]
    ppermute x0 -> x26, waiting for transfers between devices: none -> 29.6 us  [the longest x6 18.5 us: over_table(): return lax.ppermute(x, 'table', [(i, i ^ m) for i in range(tables)])]
    all_gather x2 -> x0, waiting for transfers between devices: 27.4 us -> none  [the longest x1 15.9 us: local(): lax.all_gather(adjoint.reshape((1,) + flat_shape), 'ctx', axis=0, tiled=T...]
    ppermute x0 -> x26, starting transfers between devices: none -> 22.4 us  [the longest x9 13.2 us: over_z(): return lax.ppermute(x, 'ctx', [(i, i ^ 2 * m) for i in range(count)])]
    all_to_all x3 -> x0, waiting for transfers between devices: 18.4 us -> none  [the longest x1 8.78 us: local(): lax.all_to_all(outgoing, 'table', split_axis=0, concat_axis=0, tiled=True)]
  transfers between devices with their start and end apart: 5 -> 26, of which waited for: 5 -> 11; matrix products, arithmetic and copies ran while one was open for 8% -> 2% of each run, Pallas kernels for 0% -> 13%
where the time goes in v1:
time: 115 us; the launch traced here: 114 us
  Pallas kernels  50.6 us (44%)
  waiting for transfers between devices  29.6 us (26%)
  starting transfers between devices  22.4 us (19%)
  local copies, waits for them, and re-layouts  8.84 us (8%)
  between operations  1.55 us (1%)
  other arithmetic  1.19 us (1%)
    pallas_call x7, Pallas kernels, call(): pl.pallas_call(body, grid_spec=pltpu.PrefetchScalarGridSpec(num_scalar_pr...  29.6 us
    ppermute x6, waiting for transfers between devices, over_table(): return lax.ppermute(x, 'table', [(i, i ^ m) for i in range(tables)])  18.5 us
    pallas_call x1, Pallas kernels, local(): pl.pallas_call(functools.partial(assemble, chips, share, half), grid_spec...  17.7 us
    ppermute x9, starting transfers between devices, over_z(): return lax.ppermute(x, 'ctx', [(i, i ^ 2 * m) for i in range(count)])  13.2 us
    ppermute x9, waiting for transfers between devices, over_z(): return lax.ppermute(x, 'ctx', [(i, i ^ 2 * m) for i in range(count)])  9.29 us
    ppermute x6, starting transfers between devices, over_table(): return lax.ppermute(x, 'table', [(i, i ^ m) for i in range(tables)])  8.09 us
    unnamed x60, local copies, waits for them, and re-layouts  6.21 us
    pallas_call x1, Pallas kernels, local(): pl.pallas_call(functools.partial(owner_sum, tables, rows, cap, chips), gr...  3.34 us
  transfers between devices with their start and end apart: 26, of which 11 were waited for; matrix products, arithmetic and copies ran while one was open for 2% of the time, Pallas kernels for 13%

profile of v1, /device:TPU:0, one launch (start us, length us, event | category | flops | bytes accessed | tf_op | source)
XLA Modules:
  0.0 114.1 jit_solution(16783530000084909849)
XLA Ops:
  1.7 4.0 %collective-permute-start.4 = (bf16[256,512]{1,0:T(8,128)(2,1)S(1)}, bf16[256,512]{1,0:T(8,128)(2,1)S(1)}, u32[]{:S(2)}, u32[]{:S(2)}) collective-permute-start(bf16[256,512]{1,0:T(8,128)(2,1)S(1)} %constant_dynamic-slice_fusion), channel_id=1, source_target_pairs={{0,24},{8,16},{16,8},{24,0},{1,25},{9,17},{17,9},{25,1},{2,26},{10... | collective-permute-start | bytes 786440 | tf_op jit(solution)/shard_map/ppermute | solution.py:370
  6.3 6.5 %collective-permute-done.4.refs_2_ = bf16[256,512]{1,0:T(8,128)(2,1)S(1)} collective-permute-done((bf16[256,512]{1,0:T(8,128)(2,1)S(1)}, bf16[256,512]{1,0:T(8,128)(2,1)S(1)}, u32[]{:S(2)}, u32[]{:S(2)}) %collective-permute-start.4) | collective-permute-done | bytes 262176 | tf_op jit(solution)/shard_map/ppermute | solution.py:370
  12.8 4.7 %collective-permute-done.3.refs_1_ = bf16[256,512]{1,0:T(8,128)(2,1)S(1)} collective-permute-done((bf16[256,512]{1,0:T(8,128)(2,1)S(1)}, bf16[256,512]{1,0:T(8,128)(2,1)S(1)}, u32[]{:S(2)}, u32[]{:S(2)}) %collective-permute-start.3) | collective-permute-done | bytes 262176 | tf_op jit(solution)/shard_map/ppermute | solution.py:370
  22.7 3.1 %prepare.1 = (bf16[2,256,256]{2,1,0:T(8,128)(2,1)}, s32[2,256]{1,0:T(2,128)}, bf16[4,2,16,128]{3,2,1,0:T(8,128)(2,1)}) custom-call(s32[4]{0:T(128)} %pad_add_fusion.1.info, bf16[256,512]{1,0:T(8,128)(2,1)} %bitcast.11, bf16[256,512]{1,0:T(8,128)(2,1)} %copy-done.1, bf16[512,512]{1,0:T(8,128)(2,1)} %w_out.3, s32[2,256,1]{2,1,0:T(8,128)} %copy.14.ids_col, ...), custom_call_target="tpu_custom_call" | custom-call | flops 134217728 | bytes 1349632 | tf_op jit(solution)/shard_map/prepare/pallas_call | solution.py:39
  26.7 5.9 %project.1 = (bf16[2,256,512]{2,1,0:T(8,128)(2,1)}, bf16[2,256,256]{2,1,0:T(8,128)(2,1)}, bf16[2,256,256]{2,1,0:T(8,128)(2,1)}, bf16[2,256,256]{2,1,0:T(8,128)(2...) custom-call(s32[4]{0:T(128)} %pad_add_fusion.1.info, s32[2,256,1]{2,1,0:T(8,128)} %copy.14.ids_col, ...), custom_call_target="tpu_custom_call" | custom-call | flops 1073741824 | bytes 5313536 | tf_op jit(solution)/shard_map/project/pallas_call | solution.py:39
  32.6 3.6 %collective-permute-start.10 = (bf16[64,256]{1,0:T(8,128)(2,1)}, bf16[64,256]{1,0:T(8,128)(2,1)S(1)}, u32[]{:S(2)}, u32[]{:S(2)}) collective-permute-start(bf16[64,256]{1,0:T(8,128)(2,1)} %get-tuple-element.37), channel_id=1, source_target_pairs={{0,6},{1,7},{2,4},{3,5},{4,2},{5,3},{6,0},{7,1},{8,14},{9,15},{10,... | collective-permute-start | bytes 98312 | tf_op jit(solution)/shard_map/ppermute | solution.py:373
  37.0 6.8 %attend.1 = (bf16[2,256,256]{2,1,0:T(8,128)(2,1)}, bf16[2,256,256]{2,1,0:T(8,128)(2,1)}, bf16[2,256,256]{2,1,0:T(8,128)(2,1)}, bf16[2,256,256]{2,1,0:T(8,128)(2,1)}) custom-call(s32[4]{0:T(128)} %pad_add_fusion.1.info, f32[1,256]{1,0:T(1,128)} %bitcast.16, bf16[2,256,256]{2,1,0:T(8,128)(2,1)} %get-tuple-element.29.q_raw, ...), custom_call_target="tpu_custom_call" | custom-call | flops 536870912 | bytes 2098176 | tf_op jit(solution)/shard_map/attend/pallas_call | solution.py:39
  44.5 5.6 %finish.1 = (bf16[256,256]{1,0:T(8,128)(2,1)}, bf16[256,256]{1,0:T(8,128)(2,1)}, f32[2,256,256]{2,1,0:T(8,128)}, bf16[2,256,256]{2,1,0:T(8,128)(2,1)}) custom-call(s32[4]{0:T(128)} %pad_add_fusion.1.info, f32[1,256]{1,0:T(1,128)} %bitcast.17, bf16[2,256,256]{2,1,0:T(8,128)(2,1)} %get-tuple-element.29.q_raw, bf16[2,256,256]{2,1,0:T(8,128)(2,1)} %get-tuple-element.30.k_raw, ...), custom_call_target="tpu_custom_call" | custom-call | flops 402653184 | bytes 5868544 | tf_op jit(solution)/shard_map/finish/pallas_call | solution.py:39
  50.1 1.7 %collective-permute-done.12.row_came = bf16[2,256,256]{2,1,0:T(8,128)(2,1)S(1)} collective-permute-done((bf16[2,256,256]{2,1,0:T(8,128)(2,1)}, bf16[2,256,256]{2,1,0:T(8,128)(2,1)S(1)}, u32[]{:S(2)}, u32[]{:S(2)}) %collective-permute-start.12) | collective-permute-done | bytes 262176 | tf_op jit(solution)/shard_map/ppermute | solution.py:376
  52.6 2.9 %compact.1 = (bf16[288,256]{1,0:T(8,128)(2,1)}, bf16[288,256]{1,0:T(8,128)(2,1)}, bf16[288,256]{1,0:T(8,128)(2,1)}, bf16[288,256]{1,0:T(8,128)(2,1)}) custom-call(s32[4]{0:T(128)} %pad_add_fusion.1.info, f32[2,256,256]{2,1,0:T(8,128)} %get-tuple-element.40.row_keep, bf16[2,256,256]{2,1,0:T(8,128)(2,1)} %copy-done.8, s32[2,256]{1,0:T(2,128)} %get-tuple-element.42.dest, ...), custom_call_target="tpu_custom_call" | custom-call | flops 134217728 | bytes 1411072 | tf_op jit(solution)/shard_map/compact/pallas_call | solution.py:39
  55.5 1.5 %collective-permute-start.13 = (bf16[288,256]{1,0:T(8,128)(2,1)}, bf16[288,256]{1,0:T(8,128)(2,1)S(1)}, u32[]{:S(2)}, u32[]{:S(2)}) collective-permute-start(bf16[288,256]{1,0:T(8,128)(2,1)} %get-tuple-element.45), channel_id=1, source_target_pairs={{0,8},{8,0},{16,24},{24,16},{1,9},{9,1},{17,25},{25,17},{2,10},{10... | collective-permute-start | bytes 442376 | tf_op jit(solution)/shard_map/ppermute | solution.py:370
  57.6 1.3 %collective-permute-start.15 = (bf16[288,256]{1,0:T(8,128)(2,1)}, bf16[288,256]{1,0:T(8,128)(2,1)S(1)}, u32[]{:S(2)}, u32[]{:S(2)}) collective-permute-start(bf16[288,256]{1,0:T(8,128)(2,1)} %get-tuple-element.47), channel_id=1, source_target_pairs={{0,24},{8,16},{16,8},{24,0},{1,25},{9,17},{17,9},{25,1},{2,26},{10... | collective-permute-start | bytes 442376 | tf_op jit(solution)/shard_map/ppermute | solution.py:370
  59.0 3.3 %collective-permute-done.13.refs_1_ = bf16[288,256]{1,0:T(8,128)(2,1)S(1)} collective-permute-done((bf16[288,256]{1,0:T(8,128)(2,1)}, bf16[288,256]{1,0:T(8,128)(2,1)S(1)}, u32[]{:S(2)}, u32[]{:S(2)}) %collective-permute-start.13) | collective-permute-done | bytes 147488 | tf_op jit(solution)/shard_map/ppermute | solution.py:370
  62.3 3.7 %collective-permute-done.14.refs_2_ = bf16[288,256]{1,0:T(8,128)(2,1)S(1)} collective-permute-done((bf16[288,256]{1,0:T(8,128)(2,1)}, bf16[288,256]{1,0:T(8,128)(2,1)S(1)}, u32[]{:S(2)}, u32[]{:S(2)}) %collective-permute-start.14) | collective-permute-done | bytes 147488 | tf_op jit(solution)/shard_map/ppermute | solution.py:370
  66.7 3.3 %owner_sum.1 = (bf16[128,256]{1,0:T(8,128)(2,1)}, bf16[128,256]{1,0:T(8,128)(2,1)}, bf16[128,256]{1,0:T(8,128)(2,1)}, bf16[128,256]{1,0:T(8,128)(2,1)}) custom-call(s32[4]{0:T(128)} %pad_add_fusion.1.info, bf16[288,256]{1,0:T(8,128)(2,1)} %get-tuple-element.44.refs_0_, bf16[288,256]{1,0:T(8,128)(2,1)} %copy-done.26, bf16[288,256]{1,0:T(8,128)(2,1)} %copy-done.27, ...), custom_call_target="tpu_custom_call" | custom-call | flops 536870912 | bytes 1048576 | tf_op jit(solution)/shard_map/owner_sum/pallas_call | solution.py:466
  71.2 2.9 %collective-permute-start.17 = (bf16[128,256]{1,0:T(8,128)(2,1)}, bf16[128,256]{1,0:T(8,128)(2,1)S(1)}, u32[]{:S(2)}, u32[]{:S(2)}) collective-permute-start(bf16[128,256]{1,0:T(8,128)(2,1)} %get-tuple-element.50), channel_id=1, source_target_pairs={{0,4},{1,5},{2,6},{3,7},{4,0},{5,1},{6,2},{7,3},{8,12},{9,13},{10,... | collective-permute-start | bytes 196616 | tf_op jit(solution)/shard_map/ppermute | solution.py:373
  75.0 3.2 %collective-permute-done.17.refs_2_ = bf16[128,256]{1,0:T(8,128)(2,1)S(1)} collective-permute-done((bf16[128,256]{1,0:T(8,128)(2,1)}, bf16[128,256]{1,0:T(8,128)(2,1)S(1)}, u32[]{:S(2)}, u32[]{:S(2)}) %collective-permute-start.17) | collective-permute-done | bytes 65568 | tf_op jit(solution)/shard_map/ppermute | solution.py:373
  78.2 2.3 %collective-permute-done.18.refs_3_ = bf16[128,256]{1,0:T(8,128)(2,1)S(1)} collective-permute-done((bf16[128,256]{1,0:T(8,128)(2,1)}, bf16[128,256]{1,0:T(8,128)(2,1)S(1)}, u32[]{:S(2)}, u32[]{:S(2)}) %collective-permute-start.18) | collective-permute-done | bytes 65568 | tf_op jit(solution)/shard_map/ppermute | solution.py:373
  81.1 2.3 %add_up.1.refs_0_ = bf16[128,256]{1,0:T(8,128)(2,1)} custom-call(s32[4]{0:T(128)} %pad_add_fusion.1.info, bf16[128,256]{1,0:T(8,128)(2,1)} %get-tuple-element.48.refs_0_, bf16[128,256]{1,0:T(8,128)(2,1)} %copy-done.10, bf16[128,256]{1,0:T(8,128)(2,1)} %copy-done.11, bf16[128,256]{1,0:T(8,128)(2,1)} %copy-done.12), custom_call_target="tpu_custom_call" | custom-call | flops 131072 | bytes 327680 | tf_op jit(solution)/shard_map/add_up/pallas_call | solution.py:39
  84.2 3.5 %collective-permute-start.19 = (bf16[128,256]{1,0:T(8,128)(2,1)}, bf16[128,256]{1,0:T(8,128)(2,1)S(1)}, u32[]{:S(2)}, u32[]{:S(2)}) collective-permute-start(bf16[128,256]{1,0:T(8,128)(2,1)} %add_up.1.refs_0_), channel_id=1, source_target_pairs={{0,2},{1,3},{2,0},{3,1},{4,6},{5,7},{6,4},{7,5},{8,10},{9,11},{10,... | collective-permute-start | bytes 196616 | tf_op jit(solution)/shard_map/ppermute | solution.py:373
  87.7 2.0 %collective-permute-done.21.refs_3_ = bf16[128,256]{1,0:T(8,128)(2,1)S(1)} collective-permute-done((bf16[128,256]{1,0:T(8,128)(2,1)}, bf16[128,256]{1,0:T(8,128)(2,1)S(1)}, u32[]{:S(2)}, u32[]{:S(2)}) %collective-permute-start.21) | collective-permute-done | bytes 65568 | tf_op jit(solution)/shard_map/ppermute | solution.py:373
  89.7 1.2 %collective-permute-done.20.refs_2_ = bf16[128,256]{1,0:T(8,128)(2,1)S(1)} collective-permute-done((bf16[128,256]{1,0:T(8,128)(2,1)}, bf16[128,256]{1,0:T(8,128)(2,1)S(1)}, u32[]{:S(2)}, u32[]{:S(2)}) %collective-permute-start.20) | collective-permute-done | bytes 65568 | tf_op jit(solution)/shard_map/ppermute | solution.py:373
  92.1 2.9 %result.1 = bf16[256,512]{1,0:T(8,128)(2,1)} custom-call(s32[4]{0:T(128)} %pad_add_fusion.1.info, bf16[2,256,512]{2,1,0:T(8,128)(2,1)} %get-tuple-element.28.emb, bf16[256,256]{1,0:T(8,128)(2,1)} %get-tuple-element.38.att_own, bf16[256,256]{1,0:T(8,128)(2,1)} %copy-done.9, bf16[512,512]{1,0:T(8,128)(2,1)} %w_out.3), custom_call_target="tpu_custom_call" | custom-call | flops 134217728 | bytes 1572864 | tf_op jit(solution)/shard_map/result/pallas_call | solution.py:39
  96.4 17.7 %assemble.1 = bf16[512,512]{1,0:T(8,128)(2,1)} custom-call(s32[4]{0:T(128)} %pad_add_fusion.1.info, bf16[128,256]{1,0:T(8,128)(2,1)} %add_up.1.refs_0_, bf16[128,256]{1,0:T(8,128)(2,1)} %copy-done.15, bf16[128,256]{1,0:T(8,128)(2,1)} %copy-done.14, bf16[128,256]{1,0:T(8,128)(2,1)} %copy-done.13, bf16[128,256]{1,0:T(8,128)(2,1)} %copy-done.16, ...), custom_call_target="tpu_custom_call" | custom-call | tf_op jit(solution)/shard_map/assemble/pallas_call | solution.py:494
  (105 shorter events, 16.5 us)
Async XLA Ops:
  1.7 11.1 %collective-permute-start.4 = (bf16[256,512]{1,0:T(8,128)(2,1)S(1)}, bf16[256,512]{1,0:T(8,128)(2,1)S(1)}, u32[]{:S(2)}, u32[]{:S(2)}) collective-permute-start(bf16[256,512]{1,0:T(8,128)(2,1)S(1)} %constant_dynamic-slice_fusion), channel_id=1, source_target_pairs={{0,24},{8,16},{16,8},{24,0},{1,25},{9,17},{17,9},{25,1},{2,26},{10... | collective-permute-start | bytes 786440 | tf_op jit(solution)/shard_map/ppermute | solution.py:370
  5.7 11.9 %collective-permute-start.3 = (bf16[256,512]{1,0:T(8,128)(2,1)S(1)}, bf16[256,512]{1,0:T(8,128)(2,1)S(1)}, u32[]{:S(2)}, u32[]{:S(2)}) collective-permute-start(bf16[256,512]{1,0:T(8,128)(2,1)S(1)} %constant_dynamic-slice_fusion), channel_id=1, source_target_pairs={{0,16},{8,24},{16,0},{24,8},{1,17},{9,25},{17,1},{25,9},{2,18},{10... | collective-permute-start | bytes 786440 | tf_op jit(solution)/shard_map/ppermute | solution.py:370
  6.2 11.7 %collective-permute-start.2 = (bf16[256,512]{1,0:T(8,128)(2,1)S(1)}, bf16[256,512]{1,0:T(8,128)(2,1)S(1)}, u32[]{:S(2)}, u32[]{:S(2)}) collective-permute-start(bf16[256,512]{1,0:T(8,128)(2,1)S(1)} %constant_dynamic-slice_fusion), channel_id=1, source_target_pairs={{0,8},{8,0},{16,24},{24,16},{1,9},{9,1},{17,25},{25,17},{2,10},{10... | collective-permute-start | bytes 786440 | tf_op jit(solution)/shard_map/ppermute | solution.py:370
  6.3 15.7 %collective-permute-start.1 = (bf16[256,512]{1,0:T(8,128)(2,1)S(1)}, bf16[256,512]{1,0:T(8,128)(2,1)S(1)}, u32[]{:S(2)}, u32[]{:S(2)}) collective-permute-start(bf16[256,512]{1,0:T(8,128)(2,1)S(1)} %bitcast.13), channel_id=1, source_target_pairs={{0,1},{1,0},{2,3},{3,2},{4,5},{5,4},{6,7},{7,6},{8,9},{9,8},{10,11... | collective-permute-start | bytes 786440 | tf_op jit(solution)/shard_map/ppermute | solution.py:376
  12.8 13.0 %collective-permute-start.7 = (bf16[256,512]{1,0:T(8,128)(2,1)S(1)}, bf16[256,512]{1,0:T(8,128)(2,1)S(1)}, u32[]{:S(2)}, u32[]{:S(2)}) collective-permute-start(bf16[256,512]{1,0:T(8,128)(2,1)S(1)} %collective-permute-done.4.refs_2_), channel_id=1, source_target_pairs={{0,1},{1,0},{2,3},{3,2},{4,5},{5,4},{6,7},{7,6},{8,9},{9,8},{10,11... | collective-permute-start | bytes 786440 | tf_op jit(solution)/shard_map/ppermute | solution.py:376
  17.6 8.2 %collective-permute-start.6 = (bf16[256,512]{1,0:T(8,128)(2,1)S(1)}, bf16[256,512]{1,0:T(8,128)(2,1)S(1)}, u32[]{:S(2)}, u32[]{:S(2)}) collective-permute-start(bf16[256,512]{1,0:T(8,128)(2,1)S(1)} %collective-permute-done.3.refs_1_), channel_id=1, source_target_pairs={{0,1},{1,0},{2,3},{3,2},{4,5},{5,4},{6,7},{7,6},{8,9},{9,8},{10,11... | collective-permute-start | bytes 786440 | tf_op jit(solution)/shard_map/ppermute | solution.py:376
  17.9 8.0 %collective-permute-start.5 = (bf16[256,512]{1,0:T(8,128)(2,1)S(1)}, bf16[256,512]{1,0:T(8,128)(2,1)S(1)}, u32[]{:S(2)}, u32[]{:S(2)}) collective-permute-start(bf16[256,512]{1,0:T(8,128)(2,1)S(1)} %collective-permute-done.2.refs_0_), channel_id=1, source_target_pairs={{0,1},{1,0},{2,3},{3,2},{4,5},{5,4},{6,7},{7,6},{8,9},{9,8},{10,11... | collective-permute-start | bytes 786440 | tf_op jit(solution)/shard_map/ppermute | solution.py:376
  32.6 11.2 %collective-permute-start.10 = (bf16[64,256]{1,0:T(8,128)(2,1)}, bf16[64,256]{1,0:T(8,128)(2,1)S(1)}, u32[]{:S(2)}, u32[]{:S(2)}) collective-permute-start(bf16[64,256]{1,0:T(8,128)(2,1)} %get-tuple-element.37), channel_id=1, source_target_pairs={{0,6},{1,7},{2,4},{3,5},{4,2},{5,3},{6,0},{7,1},{8,14},{9,15},{10,... | collective-permute-start | bytes 98312 | tf_op jit(solution)/shard_map/ppermute | solution.py:373
  36.2 7.6 %collective-permute-start.9 = (bf16[64,256]{1,0:T(8,128)(2,1)}, bf16[64,256]{1,0:T(8,128)(2,1)S(1)}, u32[]{:S(2)}, u32[]{:S(2)}) collective-permute-start(bf16[64,256]{1,0:T(8,128)(2,1)} %get-tuple-element.37), channel_id=1, source_target_pairs={{0,4},{1,5},{2,6},{3,7},{4,0},{5,1},{6,2},{7,3},{8,12},{9,13},{10,... | collective-permute-start | bytes 98312 | tf_op jit(solution)/shard_map/ppermute | solution.py:373
  36.2 7.6 %collective-permute-start.8 = (bf16[64,256]{1,0:T(8,128)(2,1)}, bf16[64,256]{1,0:T(8,128)(2,1)S(1)}, u32[]{:S(2)}, u32[]{:S(2)}) collective-permute-start(bf16[64,256]{1,0:T(8,128)(2,1)} %get-tuple-element.36), channel_id=1, source_target_pairs={{0,2},{1,3},{2,0},{3,1},{4,6},{5,7},{6,4},{7,5},{8,10},{9,11},{10,... | collective-permute-start | bytes 98312 | tf_op jit(solution)/shard_map/ppermute | solution.py:373
  55.5 6.8 %collective-permute-start.13 = (bf16[288,256]{1,0:T(8,128)(2,1)}, bf16[288,256]{1,0:T(8,128)(2,1)S(1)}, u32[]{:S(2)}, u32[]{:S(2)}) collective-permute-start(bf16[288,256]{1,0:T(8,128)(2,1)} %get-tuple-element.45), channel_id=1, source_target_pairs={{0,8},{8,0},{16,24},{24,16},{1,9},{9,1},{17,25},{25,17},{2,10},{10... | collective-permute-start | bytes 442376 | tf_op jit(solution)/shard_map/ppermute | solution.py:370
  57.0 9.0 %collective-permute-start.14 = (bf16[288,256]{1,0:T(8,128)(2,1)}, bf16[288,256]{1,0:T(8,128)(2,1)S(1)}, u32[]{:S(2)}, u32[]{:S(2)}) collective-permute-start(bf16[288,256]{1,0:T(8,128)(2,1)} %get-tuple-element.46), channel_id=1, source_target_pairs={{0,16},{8,24},{16,0},{24,8},{1,17},{9,25},{17,1},{25,9},{2,18},{10... | collective-permute-start | bytes 442376 | tf_op jit(solution)/shard_map/ppermute | solution.py:370
  57.6 8.3 %collective-permute-start.15 = (bf16[288,256]{1,0:T(8,128)(2,1)}, bf16[288,256]{1,0:T(8,128)(2,1)S(1)}, u32[]{:S(2)}, u32[]{:S(2)}) collective-permute-start(bf16[288,256]{1,0:T(8,128)(2,1)} %get-tuple-element.47), channel_id=1, source_target_pairs={{0,24},{8,16},{16,8},{24,0},{1,25},{9,17},{17,9},{25,1},{2,26},{10... | collective-permute-start | bytes 442376 | tf_op jit(solution)/shard_map/ppermute | solution.py:370
  70.0 5.0 %collective-permute-start.16 = (bf16[128,256]{1,0:T(8,128)(2,1)}, bf16[128,256]{1,0:T(8,128)(2,1)S(1)}, u32[]{:S(2)}, u32[]{:S(2)}) collective-permute-start(bf16[128,256]{1,0:T(8,128)(2,1)} %get-tuple-element.49), channel_id=1, source_target_pairs={{0,2},{1,3},{2,0},{3,1},{4,6},{5,7},{6,4},{7,5},{8,10},{9,11},{10,... | collective-permute-start | bytes 196616 | tf_op jit(solution)/shard_map/ppermute | solution.py:373
  71.2 6.9 %collective-permute-start.17 = (bf16[128,256]{1,0:T(8,128)(2,1)}, bf16[128,256]{1,0:T(8,128)(2,1)S(1)}, u32[]{:S(2)}, u32[]{:S(2)}) collective-permute-start(bf16[128,256]{1,0:T(8,128)(2,1)} %get-tuple-element.50), channel_id=1, source_target_pairs={{0,4},{1,5},{2,6},{3,7},{4,0},{5,1},{6,2},{7,3},{8,12},{9,13},{10,... | collective-permute-start | bytes 196616 | tf_op jit(solution)/shard_map/ppermute | solution.py:373
  74.2 6.3 %collective-permute-start.18 = (bf16[128,256]{1,0:T(8,128)(2,1)}, bf16[128,256]{1,0:T(8,128)(2,1)S(1)}, u32[]{:S(2)}, u32[]{:S(2)}) collective-permute-start(bf16[128,256]{1,0:T(8,128)(2,1)} %get-tuple-element.51), channel_id=1, source_target_pairs={{0,6},{1,7},{2,4},{3,5},{4,2},{5,3},{6,0},{7,1},{8,14},{9,15},{10,... | collective-permute-start | bytes 196616 | tf_op jit(solution)/shard_map/ppermute | solution.py:373
  74.4 17.1 %collective-permute-start.11 = (bf16[256,256]{1,0:T(8,128)(2,1)S(1)}, bf16[256,256]{1,0:T(8,128)(2,1)S(1)}, u32[]{:S(2)}, u32[]{:S(2)}) collective-permute-start(bf16[256,256]{1,0:T(8,128)(2,1)S(1)} %copy-done.29), channel_id=1, source_target_pairs={{0,1},{1,0},{2,3},{3,2},{4,5},{5,4},{6,7},{7,6},{8,9},{9,8},{10,11... | collective-permute-start | bytes 393224 | tf_op jit(solution)/shard_map/ppermute | solution.py:376
  83.3 6.4 %collective-permute-start.21 = (bf16[128,256]{1,0:T(8,128)(2,1)}, bf16[128,256]{1,0:T(8,128)(2,1)S(1)}, u32[]{:S(2)}, u32[]{:S(2)}) collective-permute-start(bf16[128,256]{1,0:T(8,128)(2,1)} %add_up.1.refs_0_), channel_id=1, source_target_pairs={{0,6},{1,7},{2,4},{3,5},{4,2},{5,3},{6,0},{7,1},{8,14},{9,15},{10,... | collective-permute-start | bytes 196616 | tf_op jit(solution)/shard_map/ppermute | solution.py:373
  84.2 6.8 %collective-permute-start.20 = (bf16[128,256]{1,0:T(8,128)(2,1)}, bf16[128,256]{1,0:T(8,128)(2,1)S(1)}, u32[]{:S(2)}, u32[]{:S(2)}) collective-permute-start(bf16[128,256]{1,0:T(8,128)(2,1)} %add_up.1.refs_0_), channel_id=1, source_target_pairs={{0,4},{1,5},{2,6},{3,7},{4,0},{5,1},{6,2},{7,3},{8,12},{9,13},{10,... | collective-permute-start | bytes 196616 | tf_op jit(solution)/shard_map/ppermute | solution.py:373
  84.2 6.8 %collective-permute-start.19 = (bf16[128,256]{1,0:T(8,128)(2,1)}, bf16[128,256]{1,0:T(8,128)(2,1)S(1)}, u32[]{:S(2)}, u32[]{:S(2)}) collective-permute-start(bf16[128,256]{1,0:T(8,128)(2,1)} %add_up.1.refs_0_), channel_id=1, source_target_pairs={{0,2},{1,3},{2,0},{3,1},{4,6},{5,7},{6,4},{7,5},{8,10},{9,11},{10,... | collective-permute-start | bytes 196616 | tf_op jit(solution)/shard_map/ppermute | solution.py:373
  87.7 7.4 %collective-permute-start.22 = (bf16[128,256]{1,0:T(8,128)(2,1)}, bf16[128,256]{1,0:T(8,128)(2,1)S(1)}, u32[]{:S(2)}, u32[]{:S(2)}) collective-permute-start(bf16[128,256]{1,0:T(8,128)(2,1)} %add_up.1.refs_0_), channel_id=1, source_target_pairs={{0,1},{1,0},{2,3},{3,2},{4,5},{5,4},{6,7},{7,6},{8,9},{9,8},{10,11... | collective-permute-start | bytes 196616 | tf_op jit(solution)/shard_map/ppermute | solution.py:376
  89.7 5.4 %collective-permute-start.25 = (bf16[128,256]{1,0:T(8,128)(2,1)S(1)}, bf16[128,256]{1,0:T(8,128)(2,1)S(1)}, u32[]{:S(2)}, u32[]{:S(2)}) collective-permute-start(bf16[128,256]{1,0:T(8,128)(2,1)S(1)} %collective-permute-done.21.refs_3_), channel_id=1, source_target_pairs={{0,1},{1,0},{2,3},{3,2},{4,5},{5,4},{6,7},{7,6},{8,9},{9,8},{10,11... | collective-permute-start | bytes 196616 | tf_op jit(solution)/shard_map/ppermute | solution.py:376
  91.0 4.1 %collective-permute-start.24 = (bf16[128,256]{1,0:T(8,128)(2,1)S(1)}, bf16[128,256]{1,0:T(8,128)(2,1)S(1)}, u32[]{:S(2)}, u32[]{:S(2)}) collective-permute-start(bf16[128,256]{1,0:T(8,128)(2,1)S(1)} %collective-permute-done.20.refs_2_), channel_id=1, source_target_pairs={{0,1},{1,0},{2,3},{3,2},{4,5},{5,4},{6,7},{7,6},{8,9},{9,8},{10,11... | collective-permute-start | bytes 196616 | tf_op jit(solution)/shard_map/ppermute | solution.py:376
  91.0 4.2 %collective-permute-start.23 = (bf16[128,256]{1,0:T(8,128)(2,1)S(1)}, bf16[128,256]{1,0:T(8,128)(2,1)S(1)}, u32[]{:S(2)}, u32[]{:S(2)}) collective-permute-start(bf16[128,256]{1,0:T(8,128)(2,1)S(1)} %collective-permute-done.19.refs_1_), channel_id=1, source_target_pairs={{0,1},{1,0},{2,3},{3,2},{4,5},{5,4},{6,7},{7,6},{8,9},{9,8},{10,11... | collective-permute-start | bytes 196616 | tf_op jit(solution)/shard_map/ppermute | solution.py:376
  (32 other events, 116.9 us)

commit v2 on v1

--- a/solution.py
+++ b/solution.py
@@ -28,27 +28,17 @@
     return dot(left, right, (0, 0))
 
 
-def call(body, info, operands, specs, outs, flops, name):
-    whole = [
-        pl.BlockSpec(x.shape, functools.partial(lambda n, i, s: (0,) * n, x.ndim))
-        if spec is None
-        else spec
-        for x, spec in zip(operands, specs)
-    ]
+def call(body, info, operands, outs, flops, name, final=False, scratch=()):
     moved = sum(math.prod(x.shape) * x.dtype.itemsize for x in (*operands, *outs))
+    here = pl.BlockSpec(memory_space=pltpu.VMEM)
+    operands = [pltpu.with_memory_space_constraint(x, pltpu.VMEM) for x in operands]
     return pl.pallas_call(
         body,
-        grid_spec=pltpu.PrefetchScalarGridSpec(
-            num_scalar_prefetch=1,
-            grid=(1,),
-            in_specs=whole,
-            out_specs=[
-                pl.BlockSpec(o.shape, functools.partial(lambda n, i, s: (0,) * n, len(o.shape)))
-                for o in outs
-            ],
-        ),
-        out_shape=outs,
-        compiler_params=pltpu.CompilerParams(vmem_limit_bytes=56 * MIB),
+        in_specs=[pl.BlockSpec(memory_space=pltpu.SMEM)] + [here] * len(operands),
+        out_specs=[here] * len(outs),
+        out_shape=outs if final else [pltpu.VMEM(o.shape, o.dtype) for o in outs],
+        scratch_shapes=scratch,
+        compiler_params=pltpu.CompilerParams(vmem_limit_bytes=32 * MIB),
         cost_estimate=pl.CostEstimate(flops=flops, bytes_accessed=moved, transcendentals=0),
         name=name,
     )(info, *operands)
@@ -78,7 +68,8 @@
     for j, d_ref in enumerate((d_own, d_oth)):
         side = core if j == 0 else 1 - core
         valid = valid_col(info, (2 * z + side) * length, length)
-        g[j] = (dot_nt(d_ref[...], w_out[...]) * valid).astype(BF16)
+        own_rows = pl.ds(pl.multiple_of(core * g.shape[2], g.shape[2]), g.shape[2])
+        g[j] = (dot_nt(d_ref[...], w_out[own_rows, :]) * valid).astype(BF16)
         column = ids_col[j]
         row = ids_row[j : j + 1, :]
         owner_row = row // rows
@@ -107,8 +98,9 @@
     emb, q_raw, k_raw, v_out = outs[:4]
     sends = outs[4:]
     mine, core, z = info[0], info[1], info[2]
-    half = w_q.shape[1]
+    half = w_q.shape[1] // 2
     part = rows // 2
+    mine_at = pl.ds(pl.multiple_of(core * half, half), half)
     blocks = [(table, mine * rows)]
     for m in range(1, tables):
         blocks.append((parts[m - 1], (mine ^ m) * rows + core * part))
@@ -130,9 +122,9 @@
         rstd = lax.rsqrt(jnp.mean(x * x, axis=1, keepdims=True) + EPS)
         normed = (x * rstd * gain[...]).astype(BF16)
         valid = valid_col(info, (2 * z + side) * length, length)
-        qr = dot(normed, w_q[...])
-        kr = dot(normed, w_k[...])
-        v = (dot(normed, w_v[...]) * valid).astype(BF16)
+        qr = dot(normed, w_q[:, mine_at])
+        kr = dot(normed, w_k[:, mine_at])
+        v = (dot(normed, w_v[:, mine_at]) * valid).astype(BF16)
         q_raw[j] = qr.astype(BF16)
         k_raw[j] = kr.astype(BF16)
         v_out[j] = v
@@ -250,6 +242,7 @@
 
     state, back = spread(state), spread(back)
     keep_at = pl.multiple_of(core * half, half)
+    mine_at = pl.ds(keep_at, half)
     send_at = pl.multiple_of((1 - core) * half, half)
     for j, d_ref in enumerate((d_own, d_oth)):
         qn, kn, q_rms, k_rms, _, _, qa, kb, ga, vb, valid = scaled_inputs(
@@ -271,7 +264,11 @@
         total = jnp.zeros((length, 1), F32)
         for at in (keep_at, send_at):
             rows = pl.ds(at, half)
-            d_normed = dot_nt(d_q, w_q[rows, :]) + dot_nt(d_k, w_k[rows, :]) + dot_nt(d_v, w_v[rows, :])
+            d_normed = (
+                dot_nt(d_q, w_q[rows, mine_at])
+                + dot_nt(d_k, w_k[rows, mine_at])
+                + dot_nt(d_v, w_v[rows, mine_at])
+            )
             d_normed = d_normed * gain[:, rows]
             part = emb[j, :, rows].astype(F32)
             scaled.append((d_normed, part))
@@ -333,20 +330,12 @@
 
 
 def assemble(chips, share, half, info, *refs):
-    own, other, out, sem = refs[:chips], refs[chips : 2 * chips], refs[2 * chips], refs[2 * chips + 1]
+    own, other, out = refs[:chips], refs[chips : 2 * chips], refs[2 * chips]
     core, z = info[1], info[2]
-    copies = []
     for m in range(chips):
         rows = pl.ds(pl.multiple_of((z ^ m) * share, share), share)
-        for n, (ref, side) in enumerate(((own[m], core), (other[m], 1 - core))):
-            columns = pl.ds(pl.multiple_of(side * half, half), half)
-            copies.append(
-                pltpu.make_async_copy(ref, out.at[rows, columns], sem.at[2 * m + n])
-            )
-    for copy in copies:
-        copy.start()
-    for copy in copies:
-        copy.wait()
+        for ref, side in ((own[m], core), (other[m], 1 - core)):
+            out[rows, pl.ds(pl.multiple_of(side * half, half), half)] = ref[...]
 
 
 def local(
@@ -382,7 +371,6 @@
     part = rows // 2
     part_own = lax.dynamic_slice(table, (core * part, 0), (part, width))
     parts = [over_table(part_own, m) for m in range(1, tables)]
-    parts_other = [swap(p) for p in parts]
 
     ids = item_owner[:, :, 0] * rows + item_local
     ids_row = jnp.concatenate([ids, swap(ids)], 0)
@@ -392,14 +380,10 @@
     gain_row = gain[None, :]
     rate_row = lax.dynamic_slice(jnp.repeat(rate, size), (core * half,), (half,))[None, :]
 
-    column_half = pl.BlockSpec((width, half), lambda i, s: (0, s[1]))
-    row_half = pl.BlockSpec((half, width), lambda i, s: (s[1], 0))
-
     g, dest, meta = call(
         functools.partial(prepare, length, tables, rows, cap),
         info,
         (d_own, d_oth, w_out, ids_col, ids_row),
-        (None, None, row_half, None, None),
         [
             array((2, length, half), BF16),
             array((2, length), jnp.int32),
@@ -408,12 +392,12 @@
         4 * length * width * half,
         "prepare",
     )
+    parts_other = [swap(lax.optimization_barrier((p, dest))[0]) for p in parts]
     bits = max(chips - 1, 1).bit_length() if chips > 1 else 0
     emb, q_raw, k_raw, v, *sends = call(
         functools.partial(project, length, tables, rows, size, chips),
         info,
         (ids_col, gain_row, w_query, w_key, w_value, g, rate_row, table, *parts, *parts_other),
-        (None, None, column_half, column_half, column_half) + (None,) * (3 + 2 * (tables - 1)),
         [array((2, length, width), BF16)]
         + [array((2, length, half), BF16)] * 3
         + [array((size, half), BF16)] * bits,
@@ -425,7 +409,6 @@
         functools.partial(attend, length, size),
         info,
         (rate_row, q_raw, k_raw, v, g),
-        (None,) * 5,
         [array((2, length, half), BF16)] * 4,
         32 * length * length * half,
         "attend",
@@ -435,7 +418,6 @@
         info,
         (rate_row, q_raw, k_raw, v, g, att, gq, gk, gv, emb, gain_row, w_query, w_key, w_value,
          d_own, d_oth, *came),
-        (None,) * 11 + (column_half,) * 3 + (None,) * (2 + chips - 1),
         [array((length, half), BF16)] * 2
         + [array((2, length, half), F32), array((2, length, half), BF16)],
         12 * length * width * half,
@@ -447,7 +429,6 @@
         functools.partial(compact, length, tables, cap),
         info,
         (row_keep, row_came, dest, meta),
-        (None,) * 4,
         [array((2 * cap + 32, half), BF16)] * tables,
         4 * length * 2 * length * half,
         "compact",
@@ -457,52 +438,42 @@
         result,
         info,
         (emb, att_own, att_came, w_out),
-        (pl.BlockSpec((1, length, width), lambda i, s: (0, 0, 0)), None, None, None),
         [array((length, width), BF16)],
         2 * length * width * width,
         "result",
+        True,
     )
     share = rows // chips
-    everything = pl.pallas_call(
+    everything = call(
         functools.partial(owner_sum, tables, rows, cap, chips),
-        grid_spec=pltpu.PrefetchScalarGridSpec(
-            num_scalar_prefetch=1,
-            grid=(1,),
-            in_specs=[pl.BlockSpec(x.shape, lambda i, s: (0, 0)) for x in arrived],
-            out_specs=[pl.BlockSpec((share, half), lambda i, s: (0, 0))] * chips,
-            scratch_shapes=[pltpu.VMEM((rows, half), F32)],
-        ),
-        out_shape=[array((share, half), BF16)] * chips,
-        compiler_params=pltpu.CompilerParams(vmem_limit_bytes=56 * MIB),
-        cost_estimate=pl.CostEstimate(
-            flops=4 * rows * length * tables * half, bytes_accessed=MIB, transcendentals=0
-        ),
-        name="owner_sum",
-    )(info, *arrived)
+        info,
+        arrived,
+        [array((share, half), BF16)] * chips,
+        4 * rows * length * tables * half,
+        "owner_sum",
+        False,
+        [pltpu.VMEM((rows, half), F32)],
+    )
     pieces = [everything[0]] + [over_z(everything[m], m) for m in range(1, chips)]
     (summed,) = call(
         functools.partial(add_up, chips),
         info,
         pieces,
-        (None,) * chips,
         [array((share, half), BF16)],
         chips * share * half,
         "add_up",
     )
     own = [summed] + [over_z(summed, m) for m in range(1, chips)]
     other = [swap(x) for x in own]
-    table_grad = pl.pallas_call(
+    (table_grad,) = call(
         functools.partial(assemble, chips, share, half),
-        grid_spec=pltpu.PrefetchScalarGridSpec(
-            num_scalar_prefetch=1,
-            grid=(1,),
-            in_specs=[pl.BlockSpec(memory_space=pl.ANY)] * (2 * chips),
-            out_specs=pl.BlockSpec(memory_space=pl.ANY),
-            scratch_shapes=[pltpu.SemaphoreType.DMA((2 * chips,))],
-        ),
-        out_shape=array((rows, width), BF16),
-        name="assemble",
-    )(info, *own, *other)
+        info,
+        [*own, *other],
+        [array((rows, width), BF16)],
+        rows * width,
+        "assemble",
+        True,
+    )
     return (output[None], table_grad)
 
 

time: 115 us -> 74.8 us (0.65)
  Pallas kernels: 50.6 us -> 17.9 us
  local copies, waits for them, and re-layouts: 8.84 us -> 4.79 us
  waiting for transfers between devices: 29.6 us -> 27.2 us
    pallas_call x9, Pallas kernels: 50.6 us -> 17.9 us  [call(): pl.pallas_call(body, in_specs=[pl.BlockSpec(memory_space=pltpu.SMEM)] + [...]
    ppermute x6, waiting for transfers between devices: 18.5 us -> 14.9 us  [over_table(): return lax.ppermute(x, 'table', [(i, i ^ m) for i in range(tables)])]
    unnamed x60 -> x22, local copies, waits for them, and re-layouts: 6.21 us -> 2.69 us
    ppermute x11, waiting for transfers between devices: 1.76 us -> 3.47 us  [swap(): return lax.ppermute(x, 'ctx', [(i, i ^ 1) for i in range(count)])]
  transfers between devices with their start and end apart: 26 -> 26, of which waited for: 11 -> 15; matrix products, arithmetic and copies ran while one was open for 2% -> 1% of each run, Pallas kernels for 13% -> 11%
where the time goes in v2:
time: 74.8 us; the launch traced here: 74.5 us
  waiting for transfers between devices  27.2 us (36%)
  starting transfers between devices  23 us (31%)
  Pallas kernels  17.9 us (24%)
  local copies, waits for them, and re-layouts  4.79 us (6%)
  between operations  1.48 us (2%)
    pallas_call x9, Pallas kernels, call(): pl.pallas_call(body, in_specs=[pl.BlockSpec(memory_space=pltpu.SMEM)] + [...  17.9 us
    ppermute x6, waiting for transfers between devices, over_table(): return lax.ppermute(x, 'table', [(i, i ^ m) for i in range(tables)])  14.9 us
    ppermute x9, starting transfers between devices, over_z(): return lax.ppermute(x, 'ctx', [(i, i ^ 2 * m) for i in range(count)])  13.4 us
    ppermute x9, waiting for transfers between devices, over_z(): return lax.ppermute(x, 'ctx', [(i, i ^ 2 * m) for i in range(count)])  8.79 us
    ppermute x6, starting transfers between devices, over_table(): return lax.ppermute(x, 'table', [(i, i ^ m) for i in range(tables)])  8.01 us
    ppermute x11, waiting for transfers between devices, swap(): return lax.ppermute(x, 'ctx', [(i, i ^ 1) for i in range(count)])  3.47 us
    unnamed x22, local copies, waits for them, and re-layouts  2.69 us
    dynamic_slice x1, local copies, waits for them, and re-layouts, local(): part_own = lax.dynamic_slice(table, (core * part, 0), (part, width))  1.73 us
  transfers between devices with their start and end apart: 26, of which 15 were waited for; matrix products, arithmetic and copies ran while one was open for 1% of the time, Pallas kernels for 11%

profile of v2, /device:TPU:0, one launch (start us, length us, event | category | flops | bytes accessed | tf_op | source)
XLA Modules:
  0.0 74.5 jit_solution(11649355408696341403)
XLA Ops:
  0.7 1.7 %constant_dynamic-slice_fusion = bf16[256,512]{1,0:T(8,128)(2,1)} fusion(bf16[512,512]{1,0:T(8,128)(2,1)} %table.1, s32[]{:T(128)S(6)} %select_n.17), kind=kLoop, calls=%fused_computation.3 | loop fusion | bytes 524292 | tf_op jit(solution)/shard_map/dynamic_slice | solution.py:372
  2.4 3.9 %collective-permute-start.4 = (bf16[256,512]{1,0:T(8,128)(2,1)}, bf16[256,512]{1,0:T(8,128)(2,1)S(1)}, u32[]{:S(2)}, u32[]{:S(2)}) collective-permute-start(bf16[256,512]{1,0:T(8,128)(2,1)} %constant_dynamic-slice_fusion), channel_id=1, source_target_pairs={{0,24},{8,16},{16,8},{24,0},{1,25},{9,17},{17,9},{25,1},{2,26},{10... | collective-permute-start | bytes 786440 | tf_op jit(solution)/shard_map/ppermute | solution.py:359
  9.6 1.1 %prepare.1 = (bf16[2,256,256]{2,1,0:T(8,128)(2,1)S(1)}, s32[2,256]{1,0:T(2,128)S(1)}, bf16[4,2,16,128]{3,2,1,0:T(8,128)(2,1)S(1)}) custom-call(s32[4]{0:T(128)S(1)} %pad_add_fusion.1.info, bf16[256,512]{1,0:T(8,128)(2,1)S(1)} %bitcast.12, bf16[256,512]{1,0:T(8,128)(2,1)S(1)} %collective-permute-done.1.d_oth, bf16[512,512]{1,0:T(8,128)(2,1)S(1)} %copy-done.3, ...), custom_call_target="tpu_custom_call" | custom-call | flops 134217728 | bytes 1349632 | tf_op jit(solution)/shard_map/prepare/pallas_call | solution.py:35
  10.7 3.0 %collective-permute-done.4.refs_2_ = bf16[256,512]{1,0:T(8,128)(2,1)S(1)} collective-permute-done((bf16[256,512]{1,0:T(8,128)(2,1)}, bf16[256,512]{1,0:T(8,128)(2,1)S(1)}, u32[]{:S(2)}, u32[]{:S(2)}) %collective-permute-start.4) | collective-permute-done | bytes 262176 | tf_op jit(solution)/shard_map/ppermute | solution.py:359
  13.7 4.7 %collective-permute-done.3.refs_1_ = bf16[256,512]{1,0:T(8,128)(2,1)S(1)} collective-permute-done((bf16[256,512]{1,0:T(8,128)(2,1)}, bf16[256,512]{1,0:T(8,128)(2,1)S(1)}, u32[]{:S(2)}, u32[]{:S(2)}) %collective-permute-start.3) | collective-permute-done | bytes 262176 | tf_op jit(solution)/shard_map/ppermute | solution.py:359
  19.6 1.5 %collective-permute-done.5.refs_3_ = bf16[256,512]{1,0:T(8,128)(2,1)} collective-permute-done((bf16[256,512]{1,0:T(8,128)(2,1)}, bf16[256,512]{1,0:T(8,128)(2,1)}, u32[]{:S(2)}, u32[]{:S(2)}) %collective-permute-start.5) | collective-permute-done | bytes 262176 | tf_op jit(solution)/shard_map/ppermute | solution.py:365
  23.0 3.9 %project.1 = (bf16[2,256,512]{2,1,0:T(8,128)(2,1)S(1)}, bf16[2,256,256]{2,1,0:T(8,128)(2,1)S(1)}, bf16[2,256,256]{2,1,0:T(8,128)(2,1)S(1)}, bf16[2,256,256]{2,1,...) custom-call(s32[4]{0:T(128)S(1)} %pad_add_fusion.1.info, s32[2,256,1]{2,1,0:T(8,128)S(1)} %copy.14.ids_col, ...), custom_call_target="tpu_custom_call" | custom-call | flops 1073741824 | bytes 5313536 | tf_op jit(solution)/shard_map/project/pallas_call | solution.py:35
  26.9 3.7 %collective-permute-start.10 = (bf16[64,256]{1,0:T(8,128)(2,1)S(1)}, bf16[64,256]{1,0:T(8,128)(2,1)S(1)}, u32[]{:S(2)}, u32[]{:S(2)}) collective-permute-start(bf16[64,256]{1,0:T(8,128)(2,1)S(1)} %get-tuple-element.44), channel_id=1, source_target_pairs={{0,6},{1,7},{2,4},{3,5},{4,2},{5,3},{6,0},{7,1},{8,14},{9,15},{10,... | collective-permute-start | bytes 98312 | tf_op jit(solution)/shard_map/ppermute | solution.py:362
  31.4 4.7 %attend.1 = (bf16[2,256,256]{2,1,0:T(8,128)(2,1)S(1)}, bf16[2,256,256]{2,1,0:T(8,128)(2,1)S(1)}, bf16[2,256,256]{2,1,0:T(8,128)(2,1)S(1)}, bf16[2,256,256]{2,1,0:T(8,128)(2,1)S(1)}) custom-call(s32[4]{0:T(128)S(1)} %pad_add_fusion.1.info, f32[1,256]{1,0:T(1,128)S(1)} %bitcast.15, bf16[2,256,256]{2,1,0:T(8,128)(2,1)S(1)} %get-tuple-element.36.q_raw, ...), custom_call_target="tpu_custom_call" | custom-call | flops 536870912 | bytes 2098176 | tf_op jit(solution)/shard_map/attend/pallas_call | solution.py:35
  36.1 2.6 %finish.1 = (bf16[256,256]{1,0:T(8,128)(2,1)S(1)}, bf16[256,256]{1,0:T(8,128)(2,1)S(1)}, f32[2,256,256]{2,1,0:T(8,128)S(1)}, bf16[2,256,256]{2,1,0:T(8,128)(2,1)S(1)}) custom-call(s32[4]{0:T(128)S(1)} %pad_add_fusion.1.info, f32[1,256]{1,0:T(1,128)S(1)} %bitcast.16, bf16[2,256,256]{2,1,0:T(8,128)(2,1)S(1)} %get-tuple-element.36.q_raw, ...), custom_call_target="tpu_custom_call" | custom-call | flops 402653184 | bytes 5868544 | tf_op jit(solution)/shard_map/finish/pallas_call | solution.py:35
  38.7 1.5 %collective-permute-done.12.row_came = bf16[2,256,256]{2,1,0:T(8,128)(2,1)S(1)} collective-permute-done((bf16[2,256,256]{2,1,0:T(8,128)(2,1)S(1)}, bf16[2,256,256]{2,1,0:T(8,128)(2,1)S(1)}, u32[]{:S(2)}, u32[]{:S(2)}) %collective-permute-start.12) | collective-permute-done | bytes 262176 | tf_op jit(solution)/shard_map/ppermute | solution.py:365
  41.1 1.6 %collective-permute-start.13 = (bf16[288,256]{1,0:T(8,128)(2,1)S(1)}, bf16[288,256]{1,0:T(8,128)(2,1)S(1)}, u32[]{:S(2)}, u32[]{:S(2)}) collective-permute-start(bf16[288,256]{1,0:T(8,128)(2,1)S(1)} %get-tuple-element.51), channel_id=1, source_target_pairs={{0,8},{8,0},{16,24},{24,16},{1,9},{9,1},{17,25},{25,17},{2,10},{10... | collective-permute-start | bytes 442376 | tf_op jit(solution)/shard_map/ppermute | solution.py:359
  43.2 1.5 %collective-permute-start.15 = (bf16[288,256]{1,0:T(8,128)(2,1)S(1)}, bf16[288,256]{1,0:T(8,128)(2,1)S(1)}, u32[]{:S(2)}, u32[]{:S(2)}) collective-permute-start(bf16[288,256]{1,0:T(8,128)(2,1)S(1)} %get-tuple-element.53), channel_id=1, source_target_pairs={{0,24},{8,16},{16,8},{24,0},{1,25},{9,17},{17,9},{25,1},{2,26},{10... | collective-permute-start | bytes 442376 | tf_op jit(solution)/shard_map/ppermute | solution.py:359
  44.7 3.1 %collective-permute-done.13.refs_1_ = bf16[288,256]{1,0:T(8,128)(2,1)S(1)} collective-permute-done((bf16[288,256]{1,0:T(8,128)(2,1)S(1)}, bf16[288,256]{1,0:T(8,128)(2,1)S(1)}, u32[]{:S(2)}, u32[]{:S(2)}) %collective-permute-start.13) | collective-permute-done | bytes 147488 | tf_op jit(solution)/shard_map/ppermute | solution.py:359
  47.7 3.8 %collective-permute-done.14.refs_2_ = bf16[288,256]{1,0:T(8,128)(2,1)S(1)} collective-permute-done((bf16[288,256]{1,0:T(8,128)(2,1)S(1)}, bf16[288,256]{1,0:T(8,128)(2,1)S(1)}, u32[]{:S(2)}, u32[]{:S(2)}) %collective-permute-start.14) | collective-permute-done | bytes 147488 | tf_op jit(solution)/shard_map/ppermute | solution.py:359
  51.5 1.3 %owner_sum.1 = (bf16[128,256]{1,0:T(8,128)(2,1)S(1)}, bf16[128,256]{1,0:T(8,128)(2,1)S(1)}, bf16[128,256]{1,0:T(8,128)(2,1)S(1)}, bf16[128,256]{1,0:T(8,128)(2,1)S(1)}) custom-call(s32[4]{0:T(128)S(1)} %pad_add_fusion.1.info, bf16[288,256]{1,0:T(8,128)(2,1)S(1)} %get-tuple-element.50.refs_0_, bf16[288,256]{1,0:T(8,128)(2,1)S(1)} %collective-permute-done.13.refs_1_, ...), custom_call_target="tpu_custom_call" | custom-call | flops 536870912 | bytes 851968 | tf_op jit(solution)/shard_map/owner_sum/pallas_call | solution.py:35
  52.8 1.3 %collective-permute-start.16 = (bf16[128,256]{1,0:T(8,128)(2,1)S(1)}, bf16[128,256]{1,0:T(8,128)(2,1)S(1)}, u32[]{:S(2)}, u32[]{:S(2)}) collective-permute-start(bf16[128,256]{1,0:T(8,128)(2,1)S(1)} %get-tuple-element.55), channel_id=1, source_target_pairs={{0,2},{1,3},{2,0},{3,1},{4,6},{5,7},{6,4},{7,5},{8,10},{9,11},{10,... | collective-permute-start | bytes 196616 | tf_op jit(solution)/shard_map/ppermute | solution.py:362
  54.0 2.9 %collective-permute-start.17 = (bf16[128,256]{1,0:T(8,128)(2,1)S(1)}, bf16[128,256]{1,0:T(8,128)(2,1)S(1)}, u32[]{:S(2)}, u32[]{:S(2)}) collective-permute-start(bf16[128,256]{1,0:T(8,128)(2,1)S(1)} %get-tuple-element.56), channel_id=1, source_target_pairs={{0,4},{1,5},{2,6},{3,7},{4,0},{5,1},{6,2},{7,3},{8,12},{9,13},{10,... | collective-permute-start | bytes 196616 | tf_op jit(solution)/shard_map/ppermute | solution.py:362
  57.6 3.0 %collective-permute-done.17.refs_2_ = bf16[128,256]{1,0:T(8,128)(2,1)S(1)} collective-permute-done((bf16[128,256]{1,0:T(8,128)(2,1)S(1)}, bf16[128,256]{1,0:T(8,128)(2,1)S(1)}, u32[]{:S(2)}, u32[]{:S(2)}) %collective-permute-start.17) | collective-permute-done | bytes 65568 | tf_op jit(solution)/shard_map/ppermute | solution.py:362
  60.6 2.5 %collective-permute-done.18.refs_3_ = bf16[128,256]{1,0:T(8,128)(2,1)S(1)} collective-permute-done((bf16[128,256]{1,0:T(8,128)(2,1)S(1)}, bf16[128,256]{1,0:T(8,128)(2,1)S(1)}, u32[]{:S(2)}, u32[]{:S(2)}) %collective-permute-start.18) | collective-permute-done | bytes 65568 | tf_op jit(solution)/shard_map/ppermute | solution.py:362
  64.5 3.7 %collective-permute-start.19 = (bf16[128,256]{1,0:T(8,128)(2,1)S(1)}, bf16[128,256]{1,0:T(8,128)(2,1)S(1)}, u32[]{:S(2)}, u32[]{:S(2)}) collective-permute-start(bf16[128,256]{1,0:T(8,128)(2,1)S(1)} %add_up.1.refs_0_), channel_id=1, source_target_pairs={{0,2},{1,3},{2,0},{3,1},{4,6},{5,7},{6,4},{7,5},{8,10},{9,11},{10,... | collective-permute-start | bytes 196616 | tf_op jit(solution)/shard_map/ppermute | solution.py:362
  68.2 1.8 %collective-permute-done.21.refs_3_ = bf16[128,256]{1,0:T(8,128)(2,1)S(1)} collective-permute-done((bf16[128,256]{1,0:T(8,128)(2,1)S(1)}, bf16[128,256]{1,0:T(8,128)(2,1)S(1)}, u32[]{:S(2)}, u32[]{:S(2)}) %collective-permute-start.21) | collective-permute-done | bytes 65568 | tf_op jit(solution)/shard_map/ppermute | solution.py:362
  71.6 1.6 %result.1 = bf16[256,512]{1,0:T(8,128)(2,1)} custom-call(s32[4]{0:T(128)S(1)} %pad_add_fusion.1.info, bf16[2,256,512]{2,1,0:T(8,128)(2,1)S(1)} %get-tuple-element.35.emb, bf16[256,256]{1,0:T(8,128)(2,1)S(1)} %get-tuple-element.45.att_own, bf16[256,256]{1,0:T(8,128)(2,1)S(1)} %collective-permute-done.11.att_came, bf16[512,512]{1,0:T(8,128)(2,1)S(1)} %copy-done.3), custom_call_target="tpu_custom_call" | custom-call | flops 134217728 | bytes 1572864 | tf_op jit(solution)/shard_map/result/pallas_call | solution.py:35
  73.1 1.4 %assemble.1 = bf16[512,512]{1,0:T(8,128)(2,1)} custom-call(s32[4]{0:T(128)S(1)} %pad_add_fusion.1.info, bf16[128,256]{1,0:T(8,128)(2,1)S(1)} %add_up.1.refs_0_, bf16[128,256]{1,0:T(8,128)(2,1)S(1)} %collective-permute-done.19.refs_1_, bf16[128,256]{1,0:T(8,128)(2,1)S(1)} %collective-permute-done.20.refs_2_, ...), custom_call_target="tpu_custom_call" | custom-call | flops 262144 | bytes 1048576 | tf_op jit(solution)/shard_map/assemble/pallas_call | solution.py:35
  (67 shorter events, 11.4 us)
Async XLA Ops:
  2.4 11.3 %collective-permute-start.4 = (bf16[256,512]{1,0:T(8,128)(2,1)}, bf16[256,512]{1,0:T(8,128)(2,1)S(1)}, u32[]{:S(2)}, u32[]{:S(2)}) collective-permute-start(bf16[256,512]{1,0:T(8,128)(2,1)} %constant_dynamic-slice_fusion), channel_id=1, source_target_pairs={{0,24},{8,16},{16,8},{24,0},{1,25},{9,17},{17,9},{25,1},{2,26},{10... | collective-permute-start | bytes 786440 | tf_op jit(solution)/shard_map/ppermute | solution.py:359
  6.3 12.1 %collective-permute-start.3 = (bf16[256,512]{1,0:T(8,128)(2,1)}, bf16[256,512]{1,0:T(8,128)(2,1)S(1)}, u32[]{:S(2)}, u32[]{:S(2)}) collective-permute-start(bf16[256,512]{1,0:T(8,128)(2,1)} %constant_dynamic-slice_fusion), channel_id=1, source_target_pairs={{0,16},{8,24},{16,0},{24,8},{1,17},{9,25},{17,1},{25,9},{2,18},{10... | collective-permute-start | bytes 786440 | tf_op jit(solution)/shard_map/ppermute | solution.py:359
  6.8 12.0 %collective-permute-start.2 = (bf16[256,512]{1,0:T(8,128)(2,1)}, bf16[256,512]{1,0:T(8,128)(2,1)}, u32[]{:S(2)}, u32[]{:S(2)}) collective-permute-start(bf16[256,512]{1,0:T(8,128)(2,1)} %constant_dynamic-slice_fusion), channel_id=1, source_target_pairs={{0,8},{8,0},{16,24},{24,16},{1,9},{9,1},{17,25},{25,17},{2,10},{10... | collective-permute-start | bytes 786440 | tf_op jit(solution)/shard_map/ppermute | solution.py:359
  6.9 1.7 %collective-permute-start.1 = (bf16[256,512]{1,0:T(8,128)(2,1)}, bf16[256,512]{1,0:T(8,128)(2,1)S(1)}, u32[]{:S(2)}, u32[]{:S(2)}) collective-permute-start(bf16[256,512]{1,0:T(8,128)(2,1)} %bitcast.11), channel_id=1, source_target_pairs={{0,1},{1,0},{2,3},{3,2},{4,5},{5,4},{6,7},{7,6},{8,9},{9,8},{10,11... | collective-permute-start | bytes 786440 | tf_op jit(solution)/shard_map/ppermute | solution.py:365
  18.8 2.2 %collective-permute-start.5 = (bf16[256,512]{1,0:T(8,128)(2,1)}, bf16[256,512]{1,0:T(8,128)(2,1)}, u32[]{:S(2)}, u32[]{:S(2)}) collective-permute-start(bf16[256,512]{1,0:T(8,128)(2,1)} %collective-permute-done.2.refs_0_), channel_id=1, source_target_pairs={{0,1},{1,0},{2,3},{3,2},{4,5},{5,4},{6,7},{7,6},{8,9},{9,8},{10,11... | collective-permute-start | bytes 786440 | tf_op jit(solution)/shard_map/ppermute | solution.py:365
  18.8 2.2 %collective-permute-start.6 = (bf16[256,512]{1,0:T(8,128)(2,1)S(1)}, bf16[256,512]{1,0:T(8,128)(2,1)}, u32[]{:S(2)}, u32[]{:S(2)}) collective-permute-start(bf16[256,512]{1,0:T(8,128)(2,1)S(1)} %collective-permute-done.3.refs_1_), channel_id=1, source_target_pairs={{0,1},{1,0},{2,3},{3,2},{4,5},{5,4},{6,7},{7,6},{8,9},{9,8},{10,11... | collective-permute-start | bytes 786440 | tf_op jit(solution)/shard_map/ppermute | solution.py:365
  19.3 1.9 %collective-permute-start.7 = (bf16[256,512]{1,0:T(8,128)(2,1)S(1)}, bf16[256,512]{1,0:T(8,128)(2,1)}, u32[]{:S(2)}, u32[]{:S(2)}) collective-permute-start(bf16[256,512]{1,0:T(8,128)(2,1)S(1)} %collective-permute-done.4.refs_2_), channel_id=1, source_target_pairs={{0,1},{1,0},{2,3},{3,2},{4,5},{5,4},{6,7},{7,6},{8,9},{9,8},{10,11... | collective-permute-start | bytes 786440 | tf_op jit(solution)/shard_map/ppermute | solution.py:365
  26.9 9.1 %collective-permute-start.10 = (bf16[64,256]{1,0:T(8,128)(2,1)S(1)}, bf16[64,256]{1,0:T(8,128)(2,1)S(1)}, u32[]{:S(2)}, u32[]{:S(2)}) collective-permute-start(bf16[64,256]{1,0:T(8,128)(2,1)S(1)} %get-tuple-element.44), channel_id=1, source_target_pairs={{0,6},{1,7},{2,4},{3,5},{4,2},{5,3},{6,0},{7,1},{8,14},{9,15},{10,... | collective-permute-start | bytes 98312 | tf_op jit(solution)/shard_map/ppermute | solution.py:362
  30.6 5.5 %collective-permute-start.9 = (bf16[64,256]{1,0:T(8,128)(2,1)S(1)}, bf16[64,256]{1,0:T(8,128)(2,1)S(1)}, u32[]{:S(2)}, u32[]{:S(2)}) collective-permute-start(bf16[64,256]{1,0:T(8,128)(2,1)S(1)} %get-tuple-element.44), channel_id=1, source_target_pairs={{0,4},{1,5},{2,6},{3,7},{4,0},{5,1},{6,2},{7,3},{8,12},{9,13},{10,... | collective-permute-start | bytes 98312 | tf_op jit(solution)/shard_map/ppermute | solution.py:362
  30.6 5.5 %collective-permute-start.8 = (bf16[64,256]{1,0:T(8,128)(2,1)S(1)}, bf16[64,256]{1,0:T(8,128)(2,1)S(1)}, u32[]{:S(2)}, u32[]{:S(2)}) collective-permute-start(bf16[64,256]{1,0:T(8,128)(2,1)S(1)} %get-tuple-element.43), channel_id=1, source_target_pairs={{0,2},{1,3},{2,0},{3,1},{4,6},{5,7},{6,4},{7,5},{8,10},{9,11},{10,... | collective-permute-start | bytes 98312 | tf_op jit(solution)/shard_map/ppermute | solution.py:362
  41.1 6.6 %collective-permute-start.13 = (bf16[288,256]{1,0:T(8,128)(2,1)S(1)}, bf16[288,256]{1,0:T(8,128)(2,1)S(1)}, u32[]{:S(2)}, u32[]{:S(2)}) collective-permute-start(bf16[288,256]{1,0:T(8,128)(2,1)S(1)} %get-tuple-element.51), channel_id=1, source_target_pairs={{0,8},{8,0},{16,24},{24,16},{1,9},{9,1},{17,25},{25,17},{2,10},{10... | collective-permute-start | bytes 442376 | tf_op jit(solution)/shard_map/ppermute | solution.py:359
  42.7 8.8 %collective-permute-start.14 = (bf16[288,256]{1,0:T(8,128)(2,1)S(1)}, bf16[288,256]{1,0:T(8,128)(2,1)S(1)}, u32[]{:S(2)}, u32[]{:S(2)}) collective-permute-start(bf16[288,256]{1,0:T(8,128)(2,1)S(1)} %get-tuple-element.52), channel_id=1, source_target_pairs={{0,16},{8,24},{16,0},{24,8},{1,17},{9,25},{17,1},{25,9},{2,18},{10... | collective-permute-start | bytes 442376 | tf_op jit(solution)/shard_map/ppermute | solution.py:359
  43.2 8.3 %collective-permute-start.15 = (bf16[288,256]{1,0:T(8,128)(2,1)S(1)}, bf16[288,256]{1,0:T(8,128)(2,1)S(1)}, u32[]{:S(2)}, u32[]{:S(2)}) collective-permute-start(bf16[288,256]{1,0:T(8,128)(2,1)S(1)} %get-tuple-element.53), channel_id=1, source_target_pairs={{0,24},{8,16},{16,8},{24,0},{1,25},{9,17},{17,9},{25,1},{2,26},{10... | collective-permute-start | bytes 442376 | tf_op jit(solution)/shard_map/ppermute | solution.py:359
  52.8 4.9 %collective-permute-start.16 = (bf16[128,256]{1,0:T(8,128)(2,1)S(1)}, bf16[128,256]{1,0:T(8,128)(2,1)S(1)}, u32[]{:S(2)}, u32[]{:S(2)}) collective-permute-start(bf16[128,256]{1,0:T(8,128)(2,1)S(1)} %get-tuple-element.55), channel_id=1, source_target_pairs={{0,2},{1,3},{2,0},{3,1},{4,6},{5,7},{6,4},{7,5},{8,10},{9,11},{10,... | collective-permute-start | bytes 196616 | tf_op jit(solution)/shard_map/ppermute | solution.py:362
  54.0 6.6 %collective-permute-start.17 = (bf16[128,256]{1,0:T(8,128)(2,1)S(1)}, bf16[128,256]{1,0:T(8,128)(2,1)S(1)}, u32[]{:S(2)}, u32[]{:S(2)}) collective-permute-start(bf16[128,256]{1,0:T(8,128)(2,1)S(1)} %get-tuple-element.56), channel_id=1, source_target_pairs={{0,4},{1,5},{2,6},{3,7},{4,0},{5,1},{6,2},{7,3},{8,12},{9,13},{10,... | collective-permute-start | bytes 196616 | tf_op jit(solution)/shard_map/ppermute | solution.py:362
  57.0 6.2 %collective-permute-start.18 = (bf16[128,256]{1,0:T(8,128)(2,1)S(1)}, bf16[128,256]{1,0:T(8,128)(2,1)S(1)}, u32[]{:S(2)}, u32[]{:S(2)}) collective-permute-start(bf16[128,256]{1,0:T(8,128)(2,1)S(1)} %get-tuple-element.57), channel_id=1, source_target_pairs={{0,6},{1,7},{2,4},{3,5},{4,2},{5,3},{6,0},{7,1},{8,14},{9,15},{10,... | collective-permute-start | bytes 196616 | tf_op jit(solution)/shard_map/ppermute | solution.py:362
  57.2 14.4 %collective-permute-start.11 = (bf16[256,256]{1,0:T(8,128)(2,1)S(1)}, bf16[256,256]{1,0:T(8,128)(2,1)S(1)}, u32[]{:S(2)}, u32[]{:S(2)}) collective-permute-start(bf16[256,256]{1,0:T(8,128)(2,1)S(1)} %get-tuple-element.46), channel_id=1, source_target_pairs={{0,1},{1,0},{2,3},{3,2},{4,5},{5,4},{6,7},{7,6},{8,9},{9,8},{10,11... | collective-permute-start | bytes 393224 | tf_op jit(solution)/shard_map/ppermute | solution.py:365
  63.7 6.2 %collective-permute-start.21 = (bf16[128,256]{1,0:T(8,128)(2,1)S(1)}, bf16[128,256]{1,0:T(8,128)(2,1)S(1)}, u32[]{:S(2)}, u32[]{:S(2)}) collective-permute-start(bf16[128,256]{1,0:T(8,128)(2,1)S(1)} %add_up.1.refs_0_), channel_id=1, source_target_pairs={{0,6},{1,7},{2,4},{3,5},{4,2},{5,3},{6,0},{7,1},{8,14},{9,15},{10,... | collective-permute-start | bytes 196616 | tf_op jit(solution)/shard_map/ppermute | solution.py:362
  64.5 6.6 %collective-permute-start.20 = (bf16[128,256]{1,0:T(8,128)(2,1)S(1)}, bf16[128,256]{1,0:T(8,128)(2,1)S(1)}, u32[]{:S(2)}, u32[]{:S(2)}) collective-permute-start(bf16[128,256]{1,0:T(8,128)(2,1)S(1)} %add_up.1.refs_0_), channel_id=1, source_target_pairs={{0,4},{1,5},{2,6},{3,7},{4,0},{5,1},{6,2},{7,3},{8,12},{9,13},{10,... | collective-permute-start | bytes 196616 | tf_op jit(solution)/shard_map/ppermute | solution.py:362
  64.5 6.6 %collective-permute-start.19 = (bf16[128,256]{1,0:T(8,128)(2,1)S(1)}, bf16[128,256]{1,0:T(8,128)(2,1)S(1)}, u32[]{:S(2)}, u32[]{:S(2)}) collective-permute-start(bf16[128,256]{1,0:T(8,128)(2,1)S(1)} %add_up.1.refs_0_), channel_id=1, source_target_pairs={{0,2},{1,3},{2,0},{3,1},{4,6},{5,7},{6,4},{7,5},{8,10},{9,11},{10,... | collective-permute-start | bytes 196616 | tf_op jit(solution)/shard_map/ppermute | solution.py:362
  68.2 5.0 %collective-permute-start.22 = (bf16[128,256]{1,0:T(8,128)(2,1)S(1)}, bf16[128,256]{1,0:T(8,128)(2,1)S(1)}, u32[]{:S(2)}, u32[]{:S(2)}) collective-permute-start(bf16[128,256]{1,0:T(8,128)(2,1)S(1)} %add_up.1.refs_0_), channel_id=1, source_target_pairs={{0,1},{1,0},{2,3},{3,2},{4,5},{5,4},{6,7},{7,6},{8,9},{9,8},{10,11... | collective-permute-start | bytes 196616 | tf_op jit(solution)/shard_map/ppermute | solution.py:365
  70.0 3.2 %collective-permute-start.25 = (bf16[128,256]{1,0:T(8,128)(2,1)S(1)}, bf16[128,256]{1,0:T(8,128)(2,1)S(1)}, u32[]{:S(2)}, u32[]{:S(2)}) collective-permute-start(bf16[128,256]{1,0:T(8,128)(2,1)S(1)} %collective-permute-done.21.refs_3_), channel_id=1, source_target_pairs={{0,1},{1,0},{2,3},{3,2},{4,5},{5,4},{6,7},{7,6},{8,9},{9,8},{10,11... | collective-permute-start | bytes 196616 | tf_op jit(solution)/shard_map/ppermute | solution.py:365
  71.0 2.1 %collective-permute-start.24 = (bf16[128,256]{1,0:T(8,128)(2,1)S(1)}, bf16[128,256]{1,0:T(8,128)(2,1)S(1)}, u32[]{:S(2)}, u32[]{:S(2)}) collective-permute-start(bf16[128,256]{1,0:T(8,128)(2,1)S(1)} %collective-permute-done.20.refs_2_), channel_id=1, source_target_pairs={{0,1},{1,0},{2,3},{3,2},{4,5},{5,4},{6,7},{7,6},{8,9},{9,8},{10,11... | collective-permute-start | bytes 196616 | tf_op jit(solution)/shard_map/ppermute | solution.py:365
  71.0 2.1 %collective-permute-start.23 = (bf16[128,256]{1,0:T(8,128)(2,1)S(1)}, bf16[128,256]{1,0:T(8,128)(2,1)S(1)}, u32[]{:S(2)}, u32[]{:S(2)}) collective-permute-start(bf16[128,256]{1,0:T(8,128)(2,1)S(1)} %collective-permute-done.19.refs_1_), channel_id=1, source_target_pairs={{0,1},{1,0},{2,3},{3,2},{4,5},{5,4},{6,7},{7,6},{8,9},{9,8},{10,11... | collective-permute-start | bytes 196616 | tf_op jit(solution)/shard_map/ppermute | solution.py:365
  (13 other events, 74.0 us)

commit v3 on v2

--- a/solution.py
+++ b/solution.py
@@ -29,19 +29,20 @@
 
 
 def call(body, info, operands, outs, flops, name, final=False, scratch=()):
+    scalars = info if isinstance(info, tuple) else (info,)
     moved = sum(math.prod(x.shape) * x.dtype.itemsize for x in (*operands, *outs))
     here = pl.BlockSpec(memory_space=pltpu.VMEM)
     operands = [pltpu.with_memory_space_constraint(x, pltpu.VMEM) for x in operands]
     return pl.pallas_call(
         body,
-        in_specs=[pl.BlockSpec(memory_space=pltpu.SMEM)] + [here] * len(operands),
+        in_specs=[pl.BlockSpec(memory_space=pltpu.SMEM)] * len(scalars) + [here] * len(operands),
         out_specs=[here] * len(outs),
         out_shape=outs if final else [pltpu.VMEM(o.shape, o.dtype) for o in outs],
         scratch_shapes=scratch,
         compiler_params=pltpu.CompilerParams(vmem_limit_bytes=32 * MIB),
         cost_estimate=pl.CostEstimate(flops=flops, bytes_accessed=moved, transcendentals=0),
         name=name,
-    )(info, *operands)
+    )(*scalars, *operands)
 
 
 def iota(shape, dim):
@@ -63,8 +64,24 @@
     return jnp.exp(-rate * moment), jnp.exp(rate * moment)
 
 
-def prepare(length, tables, rows, cap, info, d_own, d_oth, w_out, ids_col, ids_row, g, dest, meta):
+def pick(part, table, out):
+    at = pl.multiple_of((lax.axis_index("ctx") & 1) * part, part)
+    pltpu.sync_copy(table.at[pl.ds(at, part), :], out)
+
+
+def prepare(
+    length, tables, rows, cap, size, info, rate, d_own, d_oth, w_out, ids_col, ids_row, table, gain,
+    g, dest, meta, emb, rate_row, gain_row,
+):
     mine, core, z = info[0], info[1], info[2]
+    half = g.shape[2]
+    gain_row[...] = gain[...]
+    head = head_of((1, half), 1, size) + core * (half // size)
+    rates = jnp.zeros((1, half), F32)
+    for h in range(rate.shape[0]):
+        rates = jnp.where(head == h, rate[h], rates)
+    rate_row[...] = rates
+    numbers = []
     for j, d_ref in enumerate((d_own, d_oth)):
         side = core if j == 0 else 1 - core
         valid = valid_col(info, (2 * z + side) * length, length)
@@ -79,20 +96,22 @@
         slot = jnp.sum(same, axis=0, keepdims=True).astype(jnp.int32)
         where_to = (owner_row ^ mine) * cap + slot
         dest[j : j + 1, :] = where_to
+        hit = jnp.where(column - mine * rows == iota((length, rows), 1), 1.0, 0.0).astype(BF16)
+        emb[j] = dot(hit, table[...]).astype(BF16)
         high = local_row // 32
-        pick = iota((16, length), 0)
-        coded = jnp.where(
-            pick == 0, high + 1, jnp.where(pick == 1, local_row - high * 32, 0)
-        )
-        coded = coded.astype(F32).astype(BF16)
-        for m in range(tables):
+        line = iota((16, length), 0) - 2 * j
+        coded = jnp.where(line == 0, high + 1, jnp.where(line == 1, local_row - high * 32, 0))
+        numbers.append((coded.astype(F32).astype(BF16), where_to))
+    for m in range(tables):
+        total = jnp.zeros((16, cap), F32)
+        for coded, where_to in numbers:
             hit = iota((cap, length), 0) + m * cap == where_to
-            hit = jnp.where(hit, 1.0, 0.0).astype(BF16)
-            meta[m, j] = dot_nt(coded, hit).astype(BF16)
+            total = total + dot_nt(coded, jnp.where(hit, 1.0, 0.0).astype(BF16))
+        meta[m] = total.astype(BF16)
 
 
 def project(
-    length, tables, rows, size, chips, info, ids_col, gain, w_q, w_k, w_v, g, rate, table, *refs
+    length, tables, rows, size, chips, info, ids_col, gain, w_q, w_k, w_v, g, rate, emb_own, *refs
 ):
     parts, outs = refs[: 2 * (tables - 1)], refs[2 * (tables - 1) :]
     emb, q_raw, k_raw, v_out = outs[:4]
@@ -101,7 +120,7 @@
     half = w_q.shape[1] // 2
     part = rows // 2
     mine_at = pl.ds(pl.multiple_of(core * half, half), half)
-    blocks = [(table, mine * rows)]
+    blocks = []
     for m in range(1, tables):
         blocks.append((parts[m - 1], (mine ^ m) * rows + core * part))
         blocks.append((parts[tables - 1 + m - 1], (mine ^ m) * rows + (1 - core) * part))
@@ -113,7 +132,7 @@
     for j in range(2):
         side = core if j == 0 else 1 - core
         column = ids_col[j]
-        x = jnp.zeros((length, table.shape[1]), F32)
+        x = emb_own[j].astype(F32)
         for ref, base in blocks:
             count = ref.shape[0]
             hit = column - base == iota((length, count), 1)
@@ -288,10 +307,8 @@
             hit = jnp.where(hit, 1.0, 0.0).astype(BF16)
             outs[m][j * cap : (j + 1) * cap, :] = dot(hit, grads).astype(BF16)
     for m in range(tables):
-        for j in range(2):
-            base = 2 * cap + 16 * j
-            outs[m][base : base + 16, :] = jnp.zeros((16, outs[m].shape[1]), BF16)
-            outs[m][base : base + 16, 0:cap] = meta[m, j]
+        outs[m][2 * cap : 2 * cap + 16, :] = jnp.zeros((16, outs[m].shape[1]), BF16)
+        outs[m][2 * cap : 2 * cap + 16, 0:cap] = meta[m]
 
 
 def result(info, emb, att_own, att_came, w_out, out):
@@ -308,10 +325,10 @@
     z = info[2]
     total = None
     for m in range(tables):
+        coded = came[m][2 * cap : 2 * cap + 16, 0:cap].astype(F32)
         for j in range(2):
-            base = 2 * cap + 16 * j
-            coded = came[m][base : base + 16, 0:cap].astype(F32)
-            number = ((coded[0:1, :] - 1.0) * 32.0 + coded[1:2, :]).astype(jnp.int32)
+            high, low = coded[2 * j : 2 * j + 1, :], coded[2 * j + 1 : 2 * j + 2, :]
+            number = ((high - 1.0) * 32.0 + low).astype(jnp.int32)
             hit = jnp.where(iota((rows, cap), 0) == number, 1.0, 0.0).astype(BF16)
             part = dot(hit, came[m][j * cap : (j + 1) * cap, :])
             total = part if total is None else total + part
@@ -369,7 +386,13 @@
 
     info = jnp.stack([mine, core, z, hist_len[0]]).astype(jnp.int32)
     part = rows // 2
-    part_own = lax.dynamic_slice(table, (core * part, 0), (part, width))
+    part_own = pl.pallas_call(
+        functools.partial(pick, part),
+        in_specs=[pl.BlockSpec(memory_space=pl.ANY)],
+        out_specs=pl.BlockSpec(memory_space=pltpu.VMEM),
+        out_shape=pltpu.VMEM((part, width), BF16),
+        name="pick",
+    )(table)
     parts = [over_table(part_own, m) for m in range(1, tables)]
 
     ids = item_owner[:, :, 0] * rows + item_local
@@ -377,27 +400,27 @@
     ids_col = ids_row[:, :, None]
     d_own = d_out[0]
     d_oth = swap(d_own)
-    gain_row = gain[None, :]
-    rate_row = lax.dynamic_slice(jnp.repeat(rate, size), (core * half,), (half,))[None, :]
-
-    g, dest, meta = call(
-        functools.partial(prepare, length, tables, rows, cap),
-        info,
-        (d_own, d_oth, w_out, ids_col, ids_row),
+    g, dest, meta, emb_own, rate_row, gain_row = call(
+        functools.partial(prepare, length, tables, rows, cap, size),
+        (info, rate),
+        (d_own, d_oth, w_out, ids_col, ids_row, table, gain[None, :]),
         [
             array((2, length, half), BF16),
             array((2, length), jnp.int32),
-            array((tables, 2, 16, cap), BF16),
+            array((tables, 16, cap), BF16),
+            array((2, length, width), BF16),
+            array((1, half), F32),
+            array((1, width), F32),
         ],
         4 * length * width * half,
         "prepare",
     )
-    parts_other = [swap(lax.optimization_barrier((p, dest))[0]) for p in parts]
+    parts_other = [swap(p) for p in parts[:-1]] + [swap(lax.optimization_barrier((parts[-1], dest))[0])]
     bits = max(chips - 1, 1).bit_length() if chips > 1 else 0
     emb, q_raw, k_raw, v, *sends = call(
         functools.partial(project, length, tables, rows, size, chips),
         info,
-        (ids_col, gain_row, w_query, w_key, w_value, g, rate_row, table, *parts, *parts_other),
+        (ids_col, gain_row, w_query, w_key, w_value, g, rate_row, emb_own, *parts, *parts_other),
         [array((2, length, width), BF16)]
         + [array((2, length, half), BF16)] * 3
         + [array((size, half), BF16)] * bits,
@@ -429,10 +452,11 @@
         functools.partial(compact, length, tables, cap),
         info,
         (row_keep, row_came, dest, meta),
-        [array((2 * cap + 32, half), BF16)] * tables,
+        [array((2 * cap + 16, half), BF16)] * tables,
         4 * length * 2 * length * half,
         "compact",
     )
+    outgoing, att_came = lax.optimization_barrier((outgoing, att_came))
     arrived = [outgoing[0]] + [over_table(outgoing[m], m) for m in range(1, tables)]
     (output,) = call(
         result,
@@ -443,6 +467,7 @@
         "result",
         True,
     )
+    arrived, output = lax.optimization_barrier((arrived, output))
     share = rows // chips
     everything = call(
         functools.partial(owner_sum, tables, rows, cap, chips),

time: 74.8 us -> 70.1 us (0.937)
  waiting for transfers between devices: 27.2 us -> 23.9 us
  local copies, waits for them, and re-layouts: 4.79 us -> 1.76 us
    ppermute x6, waiting for transfers between devices: 14.9 us -> 11.4 us  [over_table(): return lax.ppermute(x, 'table', [(i, i ^ m) for i in range(tables)])]
    dynamic_slice x2 -> x0, local copies, waits for them, and re-layouts: 1.8 us -> none  [the longest x1 1.73 us: local(): part_own = lax.dynamic_slice(table, (core * part, 0), (part, width))]
    unnamed x22 -> x18, local copies, waits for them, and re-layouts: 2.69 us -> 1.62 us
    pallas_call x9 -> x10, Pallas kernels: 17.9 us -> 18.4 us  [the longest x9 17.3 us: call(): pl.pallas_call(body, in_specs=[pl.BlockSpec(memory_space=pltpu.SMEM)] * l...]
  transfers between devices with their start and end apart: 26 -> 26, of which waited for: 15 -> 17; matrix products, arithmetic and copies ran while one was open for 1% -> 1% of each run, Pallas kernels for 11% -> 12%
where the time goes in v3:
time: 70.1 us; the launch traced here: 69.8 us
  waiting for transfers between devices  23.9 us (34%)
  starting transfers between devices  23.5 us (34%)
  Pallas kernels  18.4 us (26%)
  local copies, waits for them, and re-layouts  1.76 us (3%)
  between operations  1.48 us (2%)
  other arithmetic  0.79 us (1%)
    pallas_call x9, Pallas kernels, call(): pl.pallas_call(body, in_specs=[pl.BlockSpec(memory_space=pltpu.SMEM)] * l...  17.3 us
    ppermute x9, starting transfers between devices, over_z(): return lax.ppermute(x, 'ctx', [(i, i ^ 2 * m) for i in range(count)])  13.4 us
    ppermute x6, waiting for transfers between devices, over_table(): return lax.ppermute(x, 'table', [(i, i ^ m) for i in range(tables)])  11.4 us
    ppermute x9, waiting for transfers between devices, over_z(): return lax.ppermute(x, 'ctx', [(i, i ^ 2 * m) for i in range(count)])  8.97 us
    ppermute x6, starting transfers between devices, over_table(): return lax.ppermute(x, 'table', [(i, i ^ m) for i in range(tables)])  8.01 us
    ppermute x11, waiting for transfers between devices, swap(): return lax.ppermute(x, 'ctx', [(i, i ^ 1) for i in range(count)])  3.49 us
    ppermute x11, starting transfers between devices, swap(): return lax.ppermute(x, 'ctx', [(i, i ^ 1) for i in range(count)])  2.12 us
    unnamed x18, local copies, waits for them, and re-layouts  1.62 us
  transfers between devices with their start and end apart: 26, of which 17 were waited for; matrix products, arithmetic and copies ran while one was open for 1% of the time, Pallas kernels for 12%

profile of v3, /device:TPU:0, one launch (start us, length us, event | category | flops | bytes accessed | tf_op | source)
XLA Modules:
  0.0 69.8 jit_solution(7653821769926171603)
XLA Ops:
  0.6 1.0 %pick.1 = bf16[256,512]{1,0:T(8,128)(2,1)S(1)} custom-call(bf16[512,512]{1,0:T(8,128)(2,1)} %table.3), custom_call_target="tpu_custom_call" | custom-call | tf_op jit(solution)/shard_map/pick/pallas_call | solution.py:389
  1.7 3.9 %collective-permute-start.4 = (bf16[256,512]{1,0:T(8,128)(2,1)S(1)}, bf16[256,512]{1,0:T(8,128)(2,1)S(1)}, u32[]{:S(2)}, u32[]{:S(2)}) collective-permute-start(bf16[256,512]{1,0:T(8,128)(2,1)S(1)} %pick.1), channel_id=1, source_target_pairs={{0,24},{8,16},{16,8},{24,0},{1,25},{9,17},{17,9},{25,1},{2,26},{10... | collective-permute-start | bytes 786440 | tf_op jit(solution)/shard_map/ppermute | solution.py:376
  10.0 1.4 %prepare.1 = (bf16[2,256,256]{2,1,0:T(8,128)(2,1)S(1)}, s32[2,256]{1,0:T(2,128)S(1)}, bf16[4,16,128]{2,1,0:T(8,128)(2,1)S(1)}, bf16[2,256,512]{2,1,0:T(8,128)(2,...) custom-call(s32[4]{0:T(128)S(1)} %pad_add_fusion.1.info, f32[8]{0:T(128)S(1)} %copy-done.8, ...), custom_call_target="tpu_custom_call" | custom-call | flops 134217728 | bytes 2386944 | tf_op jit(solution)/shard_map/prepare/pallas_call | solution.py:36
  11.4 1.4 %collective-permute-done.4.refs_2_ = bf16[256,512]{1,0:T(8,128)(2,1)S(1)} collective-permute-done((bf16[256,512]{1,0:T(8,128)(2,1)S(1)}, bf16[256,512]{1,0:T(8,128)(2,1)S(1)}, u32[]{:S(2)}, u32[]{:S(2)}) %collective-permute-start.4) | collective-permute-done | bytes 262176 | tf_op jit(solution)/shard_map/ppermute | solution.py:376
  12.8 4.7 %collective-permute-done.3.refs_1_ = bf16[256,512]{1,0:T(8,128)(2,1)S(1)} collective-permute-done((bf16[256,512]{1,0:T(8,128)(2,1)S(1)}, bf16[256,512]{1,0:T(8,128)(2,1)S(1)}, u32[]{:S(2)}, u32[]{:S(2)}) %collective-permute-start.3) | collective-permute-done | bytes 262176 | tf_op jit(solution)/shard_map/ppermute | solution.py:376
  19.8 3.1 %project.1 = (bf16[2,256,512]{2,1,0:T(8,128)(2,1)S(1)}, bf16[2,256,256]{2,1,0:T(8,128)(2,1)S(1)}, bf16[2,256,256]{2,1,0:T(8,128)(2,1)S(1)}, bf16[2,256,256]{2,1,...) custom-call(s32[4]{0:T(128)S(1)} %pad_add_fusion.1.info, s32[2,256,1]{2,1,0:T(8,128)S(1)} %copy.13.ids_col, ...), custom_call_target="tpu_custom_call" | custom-call | flops 1073741824 | bytes 5313536 | tf_op jit(solution)/shard_map/project/pallas_call | solution.py:36
  22.9 3.9 %collective-permute-start.10 = (bf16[64,256]{1,0:T(8,128)(2,1)S(1)}, bf16[64,256]{1,0:T(8,128)(2,1)S(1)}, u32[]{:S(2)}, u32[]{:S(2)}) collective-permute-start(bf16[64,256]{1,0:T(8,128)(2,1)S(1)} %get-tuple-element.56), channel_id=1, source_target_pairs={{0,6},{1,7},{2,4},{3,5},{4,2},{5,3},{6,0},{7,1},{8,14},{9,15},{10,... | collective-permute-start | bytes 98312 | tf_op jit(solution)/shard_map/ppermute | solution.py:379
  27.4 4.7 %attend.1 = (bf16[2,256,256]{2,1,0:T(8,128)(2,1)S(1)}, bf16[2,256,256]{2,1,0:T(8,128)(2,1)S(1)}, bf16[2,256,256]{2,1,0:T(8,128)(2,1)S(1)}, bf16[2,256,256]{2,1,0:T(8,128)(2,1)S(1)}) custom-call(s32[4]{0:T(128)S(1)} %pad_add_fusion.1.info, f32[1,256]{1,0:T(1,128)S(1)} %get-tuple-element.41.rate, bf16[2,256,256]{2,1,0:T(8,128)(2,1)S(1)} %get-tuple-element.47.q_raw, ...), custom_call_target="tpu_custom_call" | custom-call | flops 536870912 | bytes 2098176 | tf_op jit(solution)/shard_map/attend/pallas_call | solution.py:36
  32.1 2.6 %finish.1 = (bf16[256,256]{1,0:T(8,128)(2,1)S(1)}, bf16[256,256]{1,0:T(8,128)(2,1)S(1)}, f32[2,256,256]{2,1,0:T(8,128)S(1)}, bf16[2,256,256]{2,1,0:T(8,128)(2,1)S(1)}) custom-call(s32[4]{0:T(128)S(1)} %pad_add_fusion.1.info, f32[1,256]{1,0:T(1,128)S(1)} %get-tuple-element.41.rate, bf16[2,256,256]{2,1,0:T(8,128)(2,1)S(1)} %get-tuple-element.47.q_raw, ...), custom_call_target="tpu_custom_call" | custom-call | flops 402653184 | bytes 5868544 | tf_op jit(solution)/shard_map/finish/pallas_call | solution.py:36
  35.3 1.0 %collective-permute-done.11.row_came = bf16[2,256,256]{2,1,0:T(8,128)(2,1)S(1)} collective-permute-done((bf16[2,256,256]{2,1,0:T(8,128)(2,1)S(1)}, bf16[2,256,256]{2,1,0:T(8,128)(2,1)S(1)}, u32[]{:S(2)}, u32[]{:S(2)}) %collective-permute-start.11) | collective-permute-done | bytes 262176 | tf_op jit(solution)/shard_map/ppermute | solution.py:382
  37.2 1.7 %collective-permute-start.13 = (bf16[272,256]{1,0:T(8,128)(2,1)S(1)}, bf16[272,256]{1,0:T(8,128)(2,1)S(1)}, u32[]{:S(2)}, u32[]{:S(2)}) collective-permute-start(bf16[272,256]{1,0:T(8,128)(2,1)S(1)} %get-tuple-element.66), channel_id=1, source_target_pairs={{0,8},{8,0},{16,24},{24,16},{1,9},{9,1},{17,25},{25,17},{2,10},{10... | collective-permute-start | bytes 417800 | tf_op jit(solution)/shard_map/ppermute | solution.py:376
  39.6 1.2 %collective-permute-start.15 = (bf16[272,256]{1,0:T(8,128)(2,1)S(1)}, bf16[272,256]{1,0:T(8,128)(2,1)S(1)}, u32[]{:S(2)}, u32[]{:S(2)}) collective-permute-start(bf16[272,256]{1,0:T(8,128)(2,1)S(1)} %get-tuple-element.68), channel_id=1, source_target_pairs={{0,24},{8,16},{16,8},{24,0},{1,25},{9,17},{17,9},{25,1},{2,26},{10... | collective-permute-start | bytes 417800 | tf_op jit(solution)/shard_map/ppermute | solution.py:376
  40.8 1.6 %result.1 = bf16[256,512]{1,0:T(8,128)(2,1)} custom-call(s32[4]{0:T(128)S(1)} %pad_add_fusion.1.info, bf16[2,256,512]{2,1,0:T(8,128)(2,1)S(1)} %get-tuple-element.54.emb, bf16[256,256]{1,0:T(8,128)(2,1)S(1)} %get-tuple-element.69.att_own, bf16[256,256]{1,0:T(8,128)(2,1)S(1)} %collective-permute-done.12.att_came, bf16[512,512]{1,0:T(8,128)(2,1)S(1)} %copy-done.4), custom_call_target="tpu_custom_call" | custom-call | flops 134217728 | bytes 1572864 | tf_op jit(solution)/shard_map/result/pallas_call | solution.py:36
  42.3 1.1 %collective-permute-done.13.refs_1_ = bf16[272,256]{1,0:T(8,128)(2,1)S(1)} collective-permute-done((bf16[272,256]{1,0:T(8,128)(2,1)S(1)}, bf16[272,256]{1,0:T(8,128)(2,1)S(1)}, u32[]{:S(2)}, u32[]{:S(2)}) %collective-permute-start.13) | collective-permute-done | bytes 139296 | tf_op jit(solution)/shard_map/ppermute | solution.py:376
  43.4 4.0 %collective-permute-done.14.refs_2_ = bf16[272,256]{1,0:T(8,128)(2,1)S(1)} collective-permute-done((bf16[272,256]{1,0:T(8,128)(2,1)S(1)}, bf16[272,256]{1,0:T(8,128)(2,1)S(1)}, u32[]{:S(2)}, u32[]{:S(2)}) %collective-permute-start.14) | collective-permute-done | bytes 139296 | tf_op jit(solution)/shard_map/ppermute | solution.py:376
  47.3 1.3 %owner_sum.1 = (bf16[128,256]{1,0:T(8,128)(2,1)S(1)}, bf16[128,256]{1,0:T(8,128)(2,1)S(1)}, bf16[128,256]{1,0:T(8,128)(2,1)S(1)}, bf16[128,256]{1,0:T(8,128)(2,1)S(1)}) custom-call(s32[4]{0:T(128)S(1)} %pad_add_fusion.1.info, bf16[272,256]{1,0:T(8,128)(2,1)S(1)} %get-tuple-element.72.refs_0_, bf16[272,256]{1,0:T(8,128)(2,1)S(1)} %collective-permute-done.13.refs_1_, ...), custom_call_target="tpu_custom_call" | custom-call | flops 536870912 | bytes 819200 | tf_op jit(solution)/shard_map/owner_sum/pallas_call | solution.py:36
  48.6 1.3 %collective-permute-start.16 = (bf16[128,256]{1,0:T(8,128)(2,1)S(1)}, bf16[128,256]{1,0:T(8,128)(2,1)S(1)}, u32[]{:S(2)}, u32[]{:S(2)}) collective-permute-start(bf16[128,256]{1,0:T(8,128)(2,1)S(1)} %get-tuple-element.77), channel_id=1, source_target_pairs={{0,2},{1,3},{2,0},{3,1},{4,6},{5,7},{6,4},{7,5},{8,10},{9,11},{10,... | collective-permute-start | bytes 196616 | tf_op jit(solution)/shard_map/ppermute | solution.py:379
  49.9 2.9 %collective-permute-start.17 = (bf16[128,256]{1,0:T(8,128)(2,1)S(1)}, bf16[128,256]{1,0:T(8,128)(2,1)S(1)}, u32[]{:S(2)}, u32[]{:S(2)}) collective-permute-start(bf16[128,256]{1,0:T(8,128)(2,1)S(1)} %get-tuple-element.78), channel_id=1, source_target_pairs={{0,4},{1,5},{2,6},{3,7},{4,0},{5,1},{6,2},{7,3},{8,12},{9,13},{10,... | collective-permute-start | bytes 196616 | tf_op jit(solution)/shard_map/ppermute | solution.py:379
  53.4 3.3 %collective-permute-done.17.refs_2_ = bf16[128,256]{1,0:T(8,128)(2,1)S(1)} collective-permute-done((bf16[128,256]{1,0:T(8,128)(2,1)S(1)}, bf16[128,256]{1,0:T(8,128)(2,1)S(1)}, u32[]{:S(2)}, u32[]{:S(2)}) %collective-permute-start.17) | collective-permute-done | bytes 65568 | tf_op jit(solution)/shard_map/ppermute | solution.py:379
  56.7 2.2 %collective-permute-done.18.refs_3_ = bf16[128,256]{1,0:T(8,128)(2,1)S(1)} collective-permute-done((bf16[128,256]{1,0:T(8,128)(2,1)S(1)}, bf16[128,256]{1,0:T(8,128)(2,1)S(1)}, u32[]{:S(2)}, u32[]{:S(2)}) %collective-permute-start.18) | collective-permute-done | bytes 65568 | tf_op jit(solution)/shard_map/ppermute | solution.py:379
  60.5 3.5 %collective-permute-start.19 = (bf16[128,256]{1,0:T(8,128)(2,1)S(1)}, bf16[128,256]{1,0:T(8,128)(2,1)S(1)}, u32[]{:S(2)}, u32[]{:S(2)}) collective-permute-start(bf16[128,256]{1,0:T(8,128)(2,1)S(1)} %add_up.1.refs_0_), channel_id=1, source_target_pairs={{0,2},{1,3},{2,0},{3,1},{4,6},{5,7},{6,4},{7,5},{8,10},{9,11},{10,... | collective-permute-start | bytes 196616 | tf_op jit(solution)/shard_map/ppermute | solution.py:379
  64.0 1.8 %collective-permute-done.21.refs_3_ = bf16[128,256]{1,0:T(8,128)(2,1)S(1)} collective-permute-done((bf16[128,256]{1,0:T(8,128)(2,1)S(1)}, bf16[128,256]{1,0:T(8,128)(2,1)S(1)}, u32[]{:S(2)}, u32[]{:S(2)}) %collective-permute-start.21) | collective-permute-done | bytes 65568 | tf_op jit(solution)/shard_map/ppermute | solution.py:379
  65.7 1.3 %collective-permute-done.20.refs_2_ = bf16[128,256]{1,0:T(8,128)(2,1)S(1)} collective-permute-done((bf16[128,256]{1,0:T(8,128)(2,1)S(1)}, bf16[128,256]{1,0:T(8,128)(2,1)S(1)}, u32[]{:S(2)}, u32[]{:S(2)}) %collective-permute-start.20) | collective-permute-done | bytes 65568 | tf_op jit(solution)/shard_map/ppermute | solution.py:379
  68.5 1.4 %assemble.1 = bf16[512,512]{1,0:T(8,128)(2,1)} custom-call(s32[4]{0:T(128)S(1)} %pad_add_fusion.1.info, bf16[128,256]{1,0:T(8,128)(2,1)S(1)} %add_up.1.refs_0_, bf16[128,256]{1,0:T(8,128)(2,1)S(1)} %collective-permute-done.19.refs_1_, bf16[128,256]{1,0:T(8,128)(2,1)S(1)} %collective-permute-done.20.refs_2_, ...), custom_call_target="tpu_custom_call" | custom-call | flops 262144 | bytes 1048576 | tf_op jit(solution)/shard_map/assemble/pallas_call | solution.py:36
  (60 shorter events, 12.3 us)
Async XLA Ops:
  1.7 11.1 %collective-permute-start.4 = (bf16[256,512]{1,0:T(8,128)(2,1)S(1)}, bf16[256,512]{1,0:T(8,128)(2,1)S(1)}, u32[]{:S(2)}, u32[]{:S(2)}) collective-permute-start(bf16[256,512]{1,0:T(8,128)(2,1)S(1)} %pick.1), channel_id=1, source_target_pairs={{0,24},{8,16},{16,8},{24,0},{1,25},{9,17},{17,9},{25,1},{2,26},{10... | collective-permute-start | bytes 786440 | tf_op jit(solution)/shard_map/ppermute | solution.py:376
  5.6 11.9 %collective-permute-start.3 = (bf16[256,512]{1,0:T(8,128)(2,1)S(1)}, bf16[256,512]{1,0:T(8,128)(2,1)S(1)}, u32[]{:S(2)}, u32[]{:S(2)}) collective-permute-start(bf16[256,512]{1,0:T(8,128)(2,1)S(1)} %pick.1), channel_id=1, source_target_pairs={{0,16},{8,24},{16,0},{24,8},{1,17},{9,25},{17,1},{25,9},{2,18},{10... | collective-permute-start | bytes 786440 | tf_op jit(solution)/shard_map/ppermute | solution.py:376
  6.1 11.7 %collective-permute-start.2 = (bf16[256,512]{1,0:T(8,128)(2,1)S(1)}, bf16[256,512]{1,0:T(8,128)(2,1)S(1)}, u32[]{:S(2)}, u32[]{:S(2)}) collective-permute-start(bf16[256,512]{1,0:T(8,128)(2,1)S(1)} %pick.1), channel_id=1, source_target_pairs={{0,8},{8,0},{16,24},{24,16},{1,9},{9,1},{17,25},{25,17},{2,10},{10... | collective-permute-start | bytes 786440 | tf_op jit(solution)/shard_map/ppermute | solution.py:376
  6.2 2.2 %collective-permute-start = (bf16[256,512]{1,0:T(8,128)(2,1)}, bf16[256,512]{1,0:T(8,128)(2,1)S(1)}, u32[]{:S(2)}, u32[]{:S(2)}) collective-permute-start(bf16[256,512]{1,0:T(8,128)(2,1)} %bitcast.10), channel_id=1, source_target_pairs={{0,1},{1,0},{2,3},{3,2},{4,5},{5,4},{6,7},{7,6},{8,9},{9,8},{10,11... | collective-permute-start | bytes 786440 | tf_op jit(solution)/shard_map/ppermute | solution.py:382
  17.5 1.5 %collective-permute-start.6 = (bf16[256,512]{1,0:T(8,128)(2,1)S(1)}, bf16[256,512]{1,0:T(8,128)(2,1)S(1)}, u32[]{:S(2)}, u32[]{:S(2)}) collective-permute-start(bf16[256,512]{1,0:T(8,128)(2,1)S(1)} %collective-permute-done.3.refs_1_), channel_id=1, source_target_pairs={{0,1},{1,0},{2,3},{3,2},{4,5},{5,4},{6,7},{7,6},{8,9},{9,8},{10,11... | collective-permute-start | bytes 786440 | tf_op jit(solution)/shard_map/ppermute | solution.py:382
  17.8 1.6 %collective-permute-start.5 = (bf16[256,512]{1,0:T(8,128)(2,1)S(1)}, bf16[256,512]{1,0:T(8,128)(2,1)S(1)}, u32[]{:S(2)}, u32[]{:S(2)}) collective-permute-start(bf16[256,512]{1,0:T(8,128)(2,1)S(1)} %collective-permute-done.2.refs_0_), channel_id=1, source_target_pairs={{0,1},{1,0},{2,3},{3,2},{4,5},{5,4},{6,7},{7,6},{8,9},{9,8},{10,11... | collective-permute-start | bytes 786440 | tf_op jit(solution)/shard_map/ppermute | solution.py:382
  18.0 1.8 %collective-permute-start.7 = (bf16[256,512]{1,0:T(8,128)(2,1)S(1)}, bf16[256,512]{1,0:T(8,128)(2,1)S(1)}, u32[]{:S(2)}, u32[]{:S(2)}) collective-permute-start(bf16[256,512]{1,0:T(8,128)(2,1)S(1)} %collective-permute-done.4.refs_2_), channel_id=1, source_target_pairs={{0,1},{1,0},{2,3},{3,2},{4,5},{5,4},{6,7},{7,6},{8,9},{9,8},{10,11... | collective-permute-start | bytes 786440 | tf_op jit(solution)/shard_map/ppermute | solution.py:382
  22.9 9.2 %collective-permute-start.10 = (bf16[64,256]{1,0:T(8,128)(2,1)S(1)}, bf16[64,256]{1,0:T(8,128)(2,1)S(1)}, u32[]{:S(2)}, u32[]{:S(2)}) collective-permute-start(bf16[64,256]{1,0:T(8,128)(2,1)S(1)} %get-tuple-element.56), channel_id=1, source_target_pairs={{0,6},{1,7},{2,4},{3,5},{4,2},{5,3},{6,0},{7,1},{8,14},{9,15},{10,... | collective-permute-start | bytes 98312 | tf_op jit(solution)/shard_map/ppermute | solution.py:379
  26.7 5.4 %collective-permute-start.9 = (bf16[64,256]{1,0:T(8,128)(2,1)S(1)}, bf16[64,256]{1,0:T(8,128)(2,1)S(1)}, u32[]{:S(2)}, u32[]{:S(2)}) collective-permute-start(bf16[64,256]{1,0:T(8,128)(2,1)S(1)} %get-tuple-element.56), channel_id=1, source_target_pairs={{0,4},{1,5},{2,6},{3,7},{4,0},{5,1},{6,2},{7,3},{8,12},{9,13},{10,... | collective-permute-start | bytes 98312 | tf_op jit(solution)/shard_map/ppermute | solution.py:379
  26.7 5.3 %collective-permute-start.8 = (bf16[64,256]{1,0:T(8,128)(2,1)S(1)}, bf16[64,256]{1,0:T(8,128)(2,1)S(1)}, u32[]{:S(2)}, u32[]{:S(2)}) collective-permute-start(bf16[64,256]{1,0:T(8,128)(2,1)S(1)} %get-tuple-element.55), channel_id=1, source_target_pairs={{0,2},{1,3},{2,0},{3,1},{4,6},{5,7},{6,4},{7,5},{8,10},{9,11},{10,... | collective-permute-start | bytes 98312 | tf_op jit(solution)/shard_map/ppermute | solution.py:379
  34.7 1.6 %collective-permute-start.11 = (bf16[2,256,256]{2,1,0:T(8,128)(2,1)S(1)}, bf16[2,256,256]{2,1,0:T(8,128)(2,1)S(1)}, u32[]{:S(2)}, u32[]{:S(2)}) collective-permute-start(bf16[2,256,256]{2,1,0:T(8,128)(2,1)S(1)} %get-tuple-element.58), channel_id=1, source_target_pairs={{0,1},{1,0},{2,3},{3,2},{4,5},{5,4},{6,7},{7,6},{8,9},{9,8},{10,11... | collective-permute-start | bytes 786440 | tf_op jit(solution)/shard_map/ppermute | solution.py:382
  34.8 2.4 %collective-permute-start.12 = (bf16[256,256]{1,0:T(8,128)(2,1)S(1)}, bf16[256,256]{1,0:T(8,128)(2,1)S(1)}, u32[]{:S(2)}, u32[]{:S(2)}) collective-permute-start(bf16[256,256]{1,0:T(8,128)(2,1)S(1)} %get-tuple-element.64), channel_id=1, source_target_pairs={{0,1},{1,0},{2,3},{3,2},{4,5},{5,4},{6,7},{7,6},{8,9},{9,8},{10,11... | collective-permute-start | bytes 393224 | tf_op jit(solution)/shard_map/ppermute | solution.py:382
  37.2 6.2 %collective-permute-start.13 = (bf16[272,256]{1,0:T(8,128)(2,1)S(1)}, bf16[272,256]{1,0:T(8,128)(2,1)S(1)}, u32[]{:S(2)}, u32[]{:S(2)}) collective-permute-start(bf16[272,256]{1,0:T(8,128)(2,1)S(1)} %get-tuple-element.66), channel_id=1, source_target_pairs={{0,8},{8,0},{16,24},{24,16},{1,9},{9,1},{17,25},{25,17},{2,10},{10... | collective-permute-start | bytes 417800 | tf_op jit(solution)/shard_map/ppermute | solution.py:376
  38.9 8.4 %collective-permute-start.14 = (bf16[272,256]{1,0:T(8,128)(2,1)S(1)}, bf16[272,256]{1,0:T(8,128)(2,1)S(1)}, u32[]{:S(2)}, u32[]{:S(2)}) collective-permute-start(bf16[272,256]{1,0:T(8,128)(2,1)S(1)} %get-tuple-element.67), channel_id=1, source_target_pairs={{0,16},{8,24},{16,0},{24,8},{1,17},{9,25},{17,1},{25,9},{2,18},{10... | collective-permute-start | bytes 417800 | tf_op jit(solution)/shard_map/ppermute | solution.py:376
  39.6 7.7 %collective-permute-start.15 = (bf16[272,256]{1,0:T(8,128)(2,1)S(1)}, bf16[272,256]{1,0:T(8,128)(2,1)S(1)}, u32[]{:S(2)}, u32[]{:S(2)}) collective-permute-start(bf16[272,256]{1,0:T(8,128)(2,1)S(1)} %get-tuple-element.68), channel_id=1, source_target_pairs={{0,24},{8,16},{16,8},{24,0},{1,25},{9,17},{17,9},{25,1},{2,26},{10... | collective-permute-start | bytes 417800 | tf_op jit(solution)/shard_map/ppermute | solution.py:376
  48.6 4.9 %collective-permute-start.16 = (bf16[128,256]{1,0:T(8,128)(2,1)S(1)}, bf16[128,256]{1,0:T(8,128)(2,1)S(1)}, u32[]{:S(2)}, u32[]{:S(2)}) collective-permute-start(bf16[128,256]{1,0:T(8,128)(2,1)S(1)} %get-tuple-element.77), channel_id=1, source_target_pairs={{0,2},{1,3},{2,0},{3,1},{4,6},{5,7},{6,4},{7,5},{8,10},{9,11},{10,... | collective-permute-start | bytes 196616 | tf_op jit(solution)/shard_map/ppermute | solution.py:379
  49.9 6.8 %collective-permute-start.17 = (bf16[128,256]{1,0:T(8,128)(2,1)S(1)}, bf16[128,256]{1,0:T(8,128)(2,1)S(1)}, u32[]{:S(2)}, u32[]{:S(2)}) collective-permute-start(bf16[128,256]{1,0:T(8,128)(2,1)S(1)} %get-tuple-element.78), channel_id=1, source_target_pairs={{0,4},{1,5},{2,6},{3,7},{4,0},{5,1},{6,2},{7,3},{8,12},{9,13},{10,... | collective-permute-start | bytes 196616 | tf_op jit(solution)/shard_map/ppermute | solution.py:379
  52.8 6.1 %collective-permute-start.18 = (bf16[128,256]{1,0:T(8,128)(2,1)S(1)}, bf16[128,256]{1,0:T(8,128)(2,1)S(1)}, u32[]{:S(2)}, u32[]{:S(2)}) collective-permute-start(bf16[128,256]{1,0:T(8,128)(2,1)S(1)} %get-tuple-element.79), channel_id=1, source_target_pairs={{0,6},{1,7},{2,4},{3,5},{4,2},{5,3},{6,0},{7,1},{8,14},{9,15},{10,... | collective-permute-start | bytes 196616 | tf_op jit(solution)/shard_map/ppermute | solution.py:379
  59.5 6.2 %collective-permute-start.21 = (bf16[128,256]{1,0:T(8,128)(2,1)S(1)}, bf16[128,256]{1,0:T(8,128)(2,1)S(1)}, u32[]{:S(2)}, u32[]{:S(2)}) collective-permute-start(bf16[128,256]{1,0:T(8,128)(2,1)S(1)} %add_up.1.refs_0_), channel_id=1, source_target_pairs={{0,6},{1,7},{2,4},{3,5},{4,2},{5,3},{6,0},{7,1},{8,14},{9,15},{10,... | collective-permute-start | bytes 196616 | tf_op jit(solution)/shard_map/ppermute | solution.py:379
  60.5 6.6 %collective-permute-start.20 = (bf16[128,256]{1,0:T(8,128)(2,1)S(1)}, bf16[128,256]{1,0:T(8,128)(2,1)S(1)}, u32[]{:S(2)}, u32[]{:S(2)}) collective-permute-start(bf16[128,256]{1,0:T(8,128)(2,1)S(1)} %add_up.1.refs_0_), channel_id=1, source_target_pairs={{0,4},{1,5},{2,6},{3,7},{4,0},{5,1},{6,2},{7,3},{8,12},{9,13},{10,... | collective-permute-start | bytes 196616 | tf_op jit(solution)/shard_map/ppermute | solution.py:379
  60.5 6.6 %collective-permute-start.19 = (bf16[128,256]{1,0:T(8,128)(2,1)S(1)}, bf16[128,256]{1,0:T(8,128)(2,1)S(1)}, u32[]{:S(2)}, u32[]{:S(2)}) collective-permute-start(bf16[128,256]{1,0:T(8,128)(2,1)S(1)} %add_up.1.refs_0_), channel_id=1, source_target_pairs={{0,2},{1,3},{2,0},{3,1},{4,6},{5,7},{6,4},{7,5},{8,10},{9,11},{10,... | collective-permute-start | bytes 196616 | tf_op jit(solution)/shard_map/ppermute | solution.py:379
  64.0 3.6 %collective-permute-start.22 = (bf16[128,256]{1,0:T(8,128)(2,1)S(1)}, bf16[128,256]{1,0:T(8,128)(2,1)S(1)}, u32[]{:S(2)}, u32[]{:S(2)}) collective-permute-start(bf16[128,256]{1,0:T(8,128)(2,1)S(1)} %add_up.1.refs_0_), channel_id=1, source_target_pairs={{0,1},{1,0},{2,3},{3,2},{4,5},{5,4},{6,7},{7,6},{8,9},{9,8},{10,11... | collective-permute-start | bytes 196616 | tf_op jit(solution)/shard_map/ppermute | solution.py:382
  65.7 1.8 %collective-permute-start.25 = (bf16[128,256]{1,0:T(8,128)(2,1)S(1)}, bf16[128,256]{1,0:T(8,128)(2,1)S(1)}, u32[]{:S(2)}, u32[]{:S(2)}) collective-permute-start(bf16[128,256]{1,0:T(8,128)(2,1)S(1)} %collective-permute-done.21.refs_3_), channel_id=1, source_target_pairs={{0,1},{1,0},{2,3},{3,2},{4,5},{5,4},{6,7},{7,6},{8,9},{9,8},{10,11... | collective-permute-start | bytes 196616 | tf_op jit(solution)/shard_map/ppermute | solution.py:382
  67.0 1.4 %collective-permute-start.23 = (bf16[128,256]{1,0:T(8,128)(2,1)S(1)}, bf16[128,256]{1,0:T(8,128)(2,1)S(1)}, u32[]{:S(2)}, u32[]{:S(2)}) collective-permute-start(bf16[128,256]{1,0:T(8,128)(2,1)S(1)} %collective-permute-done.19.refs_1_), channel_id=1, source_target_pairs={{0,1},{1,0},{2,3},{3,2},{4,5},{5,4},{6,7},{7,6},{8,9},{9,8},{10,11... | collective-permute-start | bytes 196616 | tf_op jit(solution)/shard_map/ppermute | solution.py:382
  (11 other events, 54.5 us)

commit v4 on v3

v4 whole, which is shorter than its diff:
```python
import functools
import math

import jax
import jax.numpy as jnp
from jax import lax
from jax.experimental import pallas as pl
from jax.experimental.pallas import tpu as pltpu
from jax.sharding import PartitionSpec as P

EPS = 1e-06
F32 = jnp.float32
BF16 = jnp.bfloat16
MIB = 1 << 20


def dot(left, right, ways=(1, 0)):
    return lax.dot_general(
        left, right, (((ways[0],), (ways[1],)), ((), ())), preferred_element_type=F32
    )


def dot_nt(left, right):
    return dot(left, right, (1, 1))


def dot_tn(left, right):
    return dot(left, right, (0, 0))


def call(body, info, operands, outs, flops, name, final=None, scratch=(), away=()):
    moved = sum(math.prod(x.shape) * x.dtype.itemsize for x in (*operands, *outs))
    here = pl.BlockSpec(memory_space=pltpu.VMEM)
    operands = [pltpu.with_memory_space_constraint(x, pltpu.VMEM) for x in operands]
    return pl.pallas_call(
        body,
        in_specs=[pl.BlockSpec(memory_space=pltpu.SMEM)]
        + [here] * len(operands)
        + [pl.BlockSpec(memory_space=pl.ANY)] * len(away),
        out_specs=[pl.BlockSpec(memory_space=final) if final else here] * len(outs),
        out_shape=outs if final else [pltpu.VMEM(o.shape, o.dtype) for o in outs],
        scratch_shapes=scratch,
        compiler_params=pltpu.CompilerParams(vmem_limit_bytes=32 * MIB),
        cost_estimate=pl.CostEstimate(flops=flops, bytes_accessed=moved, transcendentals=0),
        name=name,
    )(info, *operands, *away)


def iota(shape, dim):
    return lax.broadcasted_iota(jnp.int32, shape, dim)


def head_of(shape, dim, size):
    return iota(shape, dim) // size


def valid_col(info, offset, length):
    position = offset + iota((length, 1), 0)
    return (position < info[3]).astype(F32)


def decay(rate, offset, length, chip):
    centre = (chip - 1) / 2.0
    moment = (offset + iota((length, rate.shape[1]), 0)).astype(F32) - centre
    return jnp.exp(-rate * moment), jnp.exp(rate * moment)


def pick(part, table, first, second, sems):
    core = lax.axis_index("ctx") & 1
    copies = []
    for n, (side, out) in enumerate(((core, first), (1 - core, second))):
        at = pl.multiple_of(side * part, part)
        copies.append(pltpu.make_async_copy(table.at[pl.ds(at, part), :], out, sems.at[n]))
    for copy in copies:
        copy.start()
    for copy in copies:
        copy.wait()


def held_rows(where_from, refs, info, rows):
    mine, core = info[0], info[1]
    for ref, (masks, sides) in zip(refs, where_from):
        owner = mine ^ jnp.where(core == 0, masks[0], masks[1])
        yield ref, owner * rows + jnp.where(core == 0, sides[0], sides[1]) * (rows // 2)


def chosen_rows(x, column, blocks):
    for ref, base in blocks:
        hit = column - base == iota((column.shape[0], ref.shape[0]), 1)
        x = x + dot(jnp.where(hit, 1.0, 0.0).astype(BF16), ref[...])
    return x


def prepare(
    length, tables, rows, cap, size, where_from, info, d_oth, ids_col, ids_row, *refs
):
    parts = refs[: len(where_from)]
    (rate, w_out, d_own, gain,
    g, ga, dest, meta, emb, falling, rising, rate_row, gain_row, w_here, d_here, rates, sems) = refs[len(where_from) :]
    pairs = ((rate, rates), (d_own, d_here), (w_out, w_here), (gain, gain_row))
    copies = [pltpu.make_async_copy(a, b, sems.at[n]) for n, (a, b) in enumerate(pairs)]
    for copy in copies:
        copy.start()
    mine, core, z = info[0], info[1], info[2]
    half = g.shape[2]
    blocks = list(held_rows(where_from, parts, info, rows))
    numbers = []
    for j in range(2):
        column = ids_col[j]
        row = ids_row[j : j + 1, :]
        owner_row = row // rows
        local_row = row - owner_row * rows
        order = iota((length, length), 0) < iota((length, length), 1)
        same = jnp.where((column // rows == owner_row) & order, 1.0, 0.0)
        slot = jnp.sum(same, axis=0, keepdims=True).astype(jnp.int32)
        where_to = (owner_row ^ mine) * cap + slot
        dest[j : j + 1, :] = where_to
        x = chosen_rows(jnp.zeros((length, emb.shape[2]), F32), column, blocks)
        emb[j] = x.astype(BF16)
        high = local_row // 32
        line = iota((16, length), 0) - 2 * j
        coded = jnp.where(line == 0, high + 1, jnp.where(line == 1, local_row - high * 32, 0))
        numbers.append((coded.astype(F32).astype(BF16), where_to))
    for m in range(tables):
        total = jnp.zeros((16, cap), F32)
        for coded, where_to in numbers:
            hit = iota((cap, length), 0) + m * cap == where_to
            total = total + dot_nt(coded, jnp.where(hit, 1.0, 0.0).astype(BF16))
        meta[m] = total.astype(BF16)
    for copy in copies:
        copy.wait()
    head = head_of((1, half), 1, size) + core * (half // size)
    chosen = jnp.zeros((1, half), F32)
    for h in range(rates.shape[1]):
        chosen = jnp.where(head == h, rates[0:1, h : h + 1], chosen)
    rate_row[...] = chosen
    own_rows = pl.ds(pl.multiple_of(core * half, half), half)
    for j, d_ref in enumerate((d_here, d_oth)):
        side = core if j == 0 else 1 - core
        valid = valid_col(info, (2 * z + side) * length, length)
        down, up = decay(chosen, side * length, length, 2 * length)
        falling[j], rising[j] = down, up
        grads = (dot_nt(d_ref[...], w_here[own_rows, :]) * valid).astype(BF16)
        g[j] = grads
        ga[j] = (grads.astype(F32) * down).astype(BF16)


def same_heads(half, size):
    return head_of((half, half), 0, size) == head_of((half, half), 1, size)


def project(
    length, where_from, rows, size, chips, info, ids_col, gain, w_q, w_k, w_v, g, falling, rising, emb_own, *refs
):
    parts, outs = refs[: len(where_from)], refs[len(where_from) :]
    emb, v_out, qa_out, kb_out, vb_out, qn_out, kn_out, qs_out, ks_out, rstd_out, states = outs[:11]
    sends = outs[11:]
    mine, core, z = info[0], info[1], info[2]
    half = w_q.shape[1] // 2
    mine_at = pl.ds(pl.multiple_of(core * half, half), half)
    blocks = list(held_rows(where_from, parts, info, rows))
    same_head = same_heads(half, size)
    mean_of = jnp.where(same_head, 1.0 / size, 0.0).astype(BF16)
    totals = [0.0, 0.0]
    for j in range(2):
        side = core if j == 0 else 1 - core
        column = ids_col[j]
        x = chosen_rows(emb_own[j].astype(F32), column, blocks)
        emb[j] = x.astype(BF16)
        rstd = lax.rsqrt(jnp.mean(x * x, axis=1, keepdims=True) + EPS)
        rstd_out[j] = rstd
        normed = (x * rstd * gain[...]).astype(BF16)
        valid = valid_col(info, (2 * z + side) * length, length)
        qr = dot(normed, w_q[:, mine_at])
        kr = dot(normed, w_k[:, mine_at])
        v = dot(normed, w_v[:, mine_at]) * valid
        q_rms = lax.rsqrt(dot((qr * qr).astype(BF16), mean_of) + EPS)
        k_rms = lax.rsqrt(dot((kr * kr).astype(BF16), mean_of) + EPS)
        qn = qr * q_rms
        kn = kr * k_rms * valid
        qa = (qn * falling[j] / size).astype(BF16)
        kb = (kn * rising[j] / math.sqrt(size)).astype(BF16)
        vb_out[j] = (v * rising[j]).astype(BF16)
        v = v.astype(BF16)
        v_out[j] = v
        qa_out[j] = qa
        kb_out[j] = kb
        qn_out[j] = qn.astype(BF16)
        kn_out[j] = kn.astype(BF16)
        qs_out[j] = q_rms / size
        ks_out[j] = k_rms * (valid / math.sqrt(size))
        for n, full in enumerate((dot_tn(kb, v), dot_tn(qa, g[j]))):
            full = jnp.where(same_head, full, 0.0)
            states[n, j] = full.astype(BF16)
            totals[n] = totals[n] + full

    def packed(full):
        return sum(full[h * size : (h + 1) * size, :] for h in range(half // size))

    carried, adjoint = packed(totals[0]), packed(totals[1])
    for bit, ref in enumerate(sends):
        low = ((z >> bit) & 1) == 0
        ref[...] = jnp.where(low, carried, adjoint).astype(BF16)


class Pairs:
    def __init__(self, length, half, size):
        self.length, self.count = length, half // size
        self.lane_head = head_of((length, half), 1, size)
        self.lanes = [
            jnp.where(self.lane_head == h, 1.0, 0.0).astype(BF16) for h in range(self.count)
        ]
        ahead = iota((length, length), 0) - iota((length, length), 1)
        self.causal = jnp.where(ahead >= 0, 1.0, 0.0).astype(BF16)
        self.anti = jnp.where(ahead <= 0, 1.0, 0.0).astype(BF16)

    def __call__(self, left, right, mask, value):
        length = self.length
        every = jnp.concatenate([left * only for only in self.lanes], 0)
        scores = dot_nt(every, right).astype(BF16)
        scores = [scores[h * length : (h + 1) * length] * mask for h in range(self.count)]
        whole = dot(jnp.concatenate(scores, 0), value)
        total = whole[:length]
        for h in range(1, self.count):
            total = jnp.where(self.lane_head == h, whole[h * length : (h + 1) * length], total)
        return total


def attend(length, size, info, qa_in, kb_in, v_in, vb_in, g_in, ga_in, states, gq, gk, gv):
    core = info[1]
    pairs = Pairs(length, qa_in.shape[2], size)
    for j in range(2):
        qa, kb, v, vb, g, ga = qa_in[j], kb_in[j], v_in[j], vb_in[j], g_in[j], ga_in[j]
        later = (core if j == 0 else 1 - core).astype(F32)
        grad_q = pairs(ga, v, pairs.causal, kb) + later * dot_nt(ga, states[0, 1 - j])
        grad_k = pairs(vb, g, pairs.anti, qa) + (1.0 - later) * dot_nt(vb, states[1, 1 - j])
        grad_v = pairs(kb, qa, pairs.anti, g) + (1.0 - later) * dot(kb, states[1, 1 - j])
        gq[j], gk[j], gv[j] = grad_q.astype(BF16), grad_k.astype(BF16), grad_v.astype(BF16)


def finish(
    length, size, chips, info, rate, kb, vb, ga, qn_in, kn_in, qs, ks, rstd_in, gq, gk, gv,
    emb, gain, w_q, w_k, w_v, d_own, d_oth, *refs
):
    came, (before_out, row_keep, row_send) = refs[: chips - 1], refs[chips - 1 :]
    core, z = info[1], info[2]
    half = kb.shape[2]
    same_head = same_heads(half, size)
    mean_of = jnp.where(same_head, 1.0 / size, 0.0).astype(BF16)
    state = jnp.zeros((size, half), F32)
    back = jnp.zeros((size, half), F32)
    for m in range(1, chips):
        peer = z ^ m
        apart = jnp.abs(peer - z).astype(F32) * (2.0 * length)
        piece = came[m - 1][...].astype(F32) * jnp.exp(-rate[...] * apart)
        before = peer < z
        state = state + jnp.where(before, piece, 0.0)
        back = back + jnp.where(before, 0.0, piece)

    def spread(packed):
        return jnp.where(same_head, jnp.concatenate([packed] * (half // size), 0), 0.0).astype(BF16)

    state, back = spread(state), spread(back)
    before_out[...] = state
    keep_at = pl.multiple_of(core * half, half)
    mine_at = pl.ds(keep_at, half)
    send_at = pl.multiple_of((1 - core) * half, half)
    for j, d_ref in enumerate((d_own, d_oth)):
        side = core if j == 0 else 1 - core
        valid = valid_col(info, (2 * z + side) * length, length)
        grad_q = gq[j].astype(F32) + dot_nt(ga[j], state)
        grad_k = gk[j].astype(F32) + dot_nt(vb[j], back)
        grad_v = gv[j].astype(F32) + dot(kb[j], back)
        qn, kn = qn_in[j].astype(F32), kn_in[j].astype(F32)
        d_q = qs[j] * (grad_q - qn * dot((qn * grad_q).astype(BF16), mean_of))
        d_k = ks[j] * (grad_k - kn * dot((kn * grad_k).astype(BF16), mean_of))
        d_q, d_k, d_v = d_q.astype(BF16), d_k.astype(BF16), (grad_v * valid).astype(BF16)
        rstd = rstd_in[j]
        scaled = []
        total = jnp.zeros((length, 1), F32)
        for at in (keep_at, send_at):
            rows = pl.ds(at, half)
            d_normed = (
                dot_nt(d_q, w_q[rows, mine_at])
                + dot_nt(d_k, w_k[rows, mine_at])
                + dot_nt(d_v, w_v[rows, mine_at])
            )
            d_normed = d_normed * gain[:, rows]
            part = emb[j, :, rows].astype(F32)
            scaled.append((d_normed, part))
            total = total + jnp.sum(d_normed * part, axis=1, keepdims=True)
        pull = total * (rstd * rstd / (2 * half))
        kept = rstd * (scaled[0][0] - scaled[0][1] * pull)
        row_keep[j] = kept + d_ref[:, pl.ds(keep_at, half)].astype(F32) * valid
        row_send[1 - j] = (rstd * (scaled[1][0] - scaled[1][1] * pull)).astype(BF16)


def outward(length, size, info, qa_in, kb_in, v_in, states, before, att_own, att_oth):
    core = info[1]
    pairs = Pairs(length, qa_in.shape[2], size)
    for j, out in enumerate((att_own, att_oth)):
        qa = qa_in[j]
        later = (core if j == 0 else 1 - core).astype(F32)
        whole = pairs(qa, kb_in[j], pairs.causal, v_in[j]) + dot(qa, before[...])
        out[...] = (whole + later * dot(qa, states[0, 1 - j])).astype(BF16)


def compact(length, tables, cap, info, row_keep, row_came, dest, meta, *outs):
    for j in range(2):
        grads = (row_keep[j] + row_came[j].astype(F32)).astype(BF16)
        where_to = dest[j : j + 1, :]
        for m in range(tables):
            hit = iota((cap, length), 0) + m * cap == where_to
            hit = jnp.where(hit, 1.0, 0.0).astype(BF16)
            outs[m][j * cap : (j + 1) * cap, :] = dot(hit, grads).astype(BF16)
    for m in range(tables):
        outs[m][2 * cap : 2 * cap + 16, :] = jnp.zeros((16, outs[m].shape[1]), BF16)
        outs[m][2 * cap : 2 * cap + 16, 0:cap] = meta[m]


def result(info, emb, att_own, att_came, w_out, out):
    core = info[1]
    half = att_own.shape[1]
    own = pl.ds(pl.multiple_of(core * half, half), half)
    other = pl.ds(pl.multiple_of((1 - core) * half, half), half)
    total = dot(att_own[...], w_out[own, :]) + dot(att_came[...], w_out[other, :])
    out[...] = (emb[0].astype(F32) + total).astype(BF16)


def row_sums(rows, cap, refs):
    total = None
    for ref in refs:
        coded = ref[2 * cap : 2 * cap + 16, 0:cap].astype(F32)
        hits = []
        for j in range(2):
            high, low = coded[2 * j : 2 * j + 1, :], coded[2 * j + 1 : 2 * j + 2, :]
            number = ((high - 1.0) * 32.0 + low).astype(jnp.int32)
            hits.append(jnp.where(iota((rows, cap), 0) == number, 1.0, 0.0).astype(BF16))
        if cap % 128 == 0:
            parts = [dot(jnp.concatenate(hits, 1), ref[: 2 * cap, :])]
        else:
            parts = [dot(hit, ref[j * cap : (j + 1) * cap, :]) for j, hit in enumerate(hits)]
        for part in parts:
            total = part if total is None else total + part
    return total


def early_sum(rows, cap, info, *refs):
    refs[-1][...] = row_sums(rows, cap, refs[:-1])


def owner_sum(rows, cap, chips, count, info, early, *refs):
    came, outs, acc = refs[:count], refs[count : count + chips], refs[count + chips]
    z = info[2]
    acc[...] = early[...] + row_sums(rows, cap, came)
    share = rows // chips
    for m in range(chips):
        at = pl.multiple_of((z ^ m) * share, share)
        outs[m][...] = acc[pl.ds(at, share), :].astype(BF16)


def add_up(chips, info, *refs):
    total = refs[0][...].astype(F32)
    for m in range(1, chips):
        total = total + refs[m][...].astype(F32)
    refs[chips][...] = total.astype(BF16)


def assemble(chips, share, half, info, *refs):
    own, other, (out, held, sems) = refs[:chips], refs[chips : 2 * chips], refs[2 * chips :]
    core, z = info[1], info[2]
    copies = []
    for m in range(chips):
        rows = pl.ds(pl.multiple_of((z ^ m) * share, share), share)
        for ref, side in ((own[m], core), (other[m], 1 - core)):
            held[m, :, pl.ds(pl.multiple_of(side * half, half), half)] = ref[...]
        copies.append(pltpu.make_async_copy(held.at[m], out.at[rows, :], sems.at[m]))
        copies[-1].start()
    for copy in copies:
        copy.wait()


def local(
    item_local, item_owner, hist_len, table, gain, w_query, w_key, w_value, w_out, rate, d_out
):
    tables = lax.axis_size("table")
    count = lax.axis_size("ctx")
    length = item_local.shape[1]
    rows, width = table.shape
    heads = rate.shape[0]
    size = width // heads
    half = width // 2
    chips = count // 2
    cap = 2 * length // tables
    mine = lax.axis_index("table")
    block = lax.axis_index("ctx")
    core = block % 2
    z = block // 2

    def over_table(x, m):
        return lax.ppermute(x, "table", [(i, i ^ m) for i in range(tables)])

    def over_z(x, m):
        return lax.ppermute(x, "ctx", [(i, i ^ (2 * m)) for i in range(count)])

    def swap(x):
        return lax.ppermute(x, "ctx", [(i, i ^ 1) for i in range(count)])

    def array(shape, dtype):
        return jax.ShapeDtypeStruct(shape, dtype)

    info = jnp.stack([mine, core, z, hist_len[0]]).astype(jnp.int32)
    part = rows // 2
    first, second = pl.pallas_call(
        functools.partial(pick, part),
        in_specs=[pl.BlockSpec(memory_space=pl.ANY)],
        out_specs=[pl.BlockSpec(memory_space=pltpu.VMEM)] * 2,
        out_shape=[pltpu.VMEM((part, width), BF16)] * 2,
        scratch_shapes=[pltpu.SemaphoreType.DMA((2,))],
        name="pick",
    )(table)

    def from_mask(x, masks):
        return lax.ppermute(
            x,
            ("table", "ctx"),
            [
                (t * count + c, (t ^ masks[c % 2]) * count + c)
                for t in range(tables)
                for c in range(count)
            ],
        )

    ids = item_owner[:, :, 0] * rows + item_local
    ids_row = jnp.concatenate([ids, swap(ids)], 0)
    ids_col = ids_row[:, :, None]
    if tables == 4:
        near = from_mask(first, (1, 2))
        rest = from_mask(second, (1, 2))
        far = from_mask(lax.optimization_barrier((near, ids_row))[0], (2, 1))
        fetched = [(near, (1, 2), (0, 1)), (rest, (1, 2), (1, 0)), (far, (3, 3), (0, 1))]
        early = fetched[:2]
    else:
        fetched = [(over_table(first, m), (m, m), (0, 1)) for m in range(1, tables)]
        early = []
    late = fetched[len(early) :]
    early = [(first, (0, 0), (0, 1)), (second, (0, 0), (1, 0)), *early]

    d_own = d_out[0]
    d_oth = swap(d_own)
    g, ga, dest, meta, emb_own, falling, rising, rate_row, gain_row, w_here, d_here = call(
        functools.partial(prepare, length, tables, rows, cap, size, [x[1:] for x in early]),
        info,
        (d_oth, ids_col, ids_row, *[x[0] for x in early]),
        [
            array((2, length, half), BF16),
            array((2, length, half), BF16),
            array((2, length), jnp.int32),
            array((tables, 16, cap), BF16),
            array((2, length, width), BF16),
            array((2, length, half), F32),
            array((2, length, half), F32),
            array((1, half), F32),
            array((1, width), F32),
            array((width, width), BF16),
            array((length, width), BF16),
        ],
        4 * length * width * half,
        "prepare",
        away=(rate[None, :], w_out, d_own, gain[None, :]),
        scratch=[pltpu.VMEM((1, heads), F32), pltpu.SemaphoreType.DMA((4,))],
    )
    others = [swap(x) for x, _, _ in fetched[:-1]]
    others.append(swap(lax.optimization_barrier((fetched[-1][0], dest))[0]))
    late += [(x, m[::-1], h[::-1]) for x, (_, m, h) in zip(others, fetched)]
    bits = max(chips - 1, 1).bit_length() if chips > 1 else 0
    emb, v, qa, kb, vb, qn, kn, qs, ks, rstd, states, *sends = call(
        functools.partial(project, length, [x[1:] for x in late], rows, size, chips),
        info,
        (ids_col, gain_row, w_query, w_key, w_value, g, falling, rising, emb_own, *[x[0] for x in late]),
        [array((2, length, width), BF16)]
        + [array((2, length, half), BF16)] * 6
        + [array((2, length, half), F32)] * 2
        + [array((2, length, 1), F32), array((2, 2, half, half), BF16)]
        + [array((size, half), BF16)] * bits,
        4 * length * tables * rows * width,
        "project",
    )
    came = [over_z(sends[m.bit_length() - 1], m) for m in range(1, chips)]
    gq, gk, gv = call(
        functools.partial(attend, length, size),
        info,
        (qa, kb, v, vb, g, ga, states),
        [array((2, length, half), BF16)] * 3,
        24 * length * length * half,
        "attend",
    )
    before, row_keep, row_send = call(
        functools.partial(finish, length, size, chips),
        info,
        (rate_row, kb, vb, ga, qn, kn, qs, ks, rstd, gq, gk, gv, emb, gain_row, w_query, w_key, w_value,
         d_here, d_oth, *came),
        [
            array((half, half), BF16),
            array((2, length, half), F32),
            array((2, length, half), BF16),
        ],
        12 * length * width * half,
        "finish",
    )
    row_came = swap(row_send)
    outgoing = call(
        functools.partial(compact, length, tables, cap),
        info,
        (row_keep, row_came, dest, meta),
        [array((2 * cap + 16, half), BF16)] * tables,
        4 * length * 2 * length * half,
        "compact",
    )
    arrived = [over_table(outgoing[m], m) for m in range(1, tables)]
    arrived[0], before = lax.optimization_barrier((arrived[0], before))
    (early,) = call(
        functools.partial(early_sum, rows, cap),
        info,
        (outgoing[0], arrived[0]),
        [array((rows, half), F32)],
        8 * rows * length * half,
        "early_sum",
    )
    att_own, att_oth = call(
        functools.partial(outward, length, size),
        info,
        (qa, kb, v, states, before),
        [array((length, half), BF16)] * 2,
        8 * length * length * half,
        "outward",
    )
    share = rows // chips
    early, att_oth = lax.optimization_barrier((early, att_oth))
    att_came = swap(att_oth)
    everything = call(
        functools.partial(owner_sum, rows, cap, chips, tables - 2),
        info,
        (early, *arrived[1:]),
        [array((share, half), BF16)] * chips,
        8 * rows * length * (tables - 2) * half,
        "owner_sum",
        None,
        [pltpu.VMEM((rows, half), F32)],
    )
    pieces = [over_z(everything[m], m) for m in reversed(range(1, chips))]
    if pieces:
        pieces[0], att_came = lax.optimization_barrier((pieces[0], att_came))
    (output,) = call(
        result,
        info,
        (emb, att_own, att_came, w_here),
        [array((length, width), BF16)],
        2 * length * width * width,
        "result",
        pltpu.VMEM,
    )
    pieces, output = lax.optimization_barrier((pieces, output))
    pieces = [everything[0]] + pieces
    (summed,) = call(
        functools.partial(add_up, chips),
        info,
        pieces,
        [array((share, half), BF16)],
        chips * share * half,
        "add_up",
    )
    own = [summed] + [over_z(summed, m) for m in range(1, chips)]
    other = [swap(x) for x in own]
    (table_grad,) = call(
        functools.partial(assemble, chips, share, half),
        info,
        [*own, *other],
        [array((rows, width), BF16)],
        rows * width,
        "assemble",
        pl.ANY,
        [pltpu.VMEM((chips, share, width), BF16), pltpu.SemaphoreType.DMA((chips,))],
    )
    return (output[None], table_grad)


def solution(mesh):
    return jax.shard_map(
        local,
        mesh=mesh,
        in_specs=(
            P("table", "ctx"),
            P("table", "ctx", None),
            P("table"),
            P("table", None),
            P(),
            P(),
            P(),
            P(),
            P(),
            P(),
            P("table", "ctx", None),
        ),
        out_specs=(P("table", "ctx", None), P("table", None)),
        check_vma=False,
    )
```

time: 70.1 us -> 66.1 us (0.943)
  waiting for transfers between devices: 23.9 us -> 19.4 us
  local copies, waits for them, and re-layouts: 1.76 us -> 0.81 us
  starting transfers between devices: 23.5 us -> 24.4 us
    ppermute x6 -> x3, waiting for transfers between devices: 11.4 us -> 3.85 us  [over_table(): return lax.ppermute(x, 'table', [(i, i ^ m) for i in range(tables)])]
    ppermute x0 -> x3, starting transfers between devices: none -> 5.69 us  [from_mask(): lax.ppermute(x, ('table', 'ctx'), [(t * count + c, (t ^ masks[c % 2]) * c...]
    ppermute x6 -> x3, starting transfers between devices: 8.01 us -> 3.55 us  [over_table(): return lax.ppermute(x, 'table', [(i, i ^ m) for i in range(tables)])]
    ppermute x0 -> x3, waiting for transfers between devices: none -> 3.99 us  [from_mask(): lax.ppermute(x, ('table', 'ctx'), [(t * count + c, (t ^ masks[c % 2]) * c...]
    ppermute x9, waiting for transfers between devices: 8.97 us -> 7.99 us  [over_z(): return lax.ppermute(x, 'ctx', [(i, i ^ 2 * m) for i in range(count)])]
    unnamed x18 -> x14, local copies, waits for them, and re-layouts: 1.62 us -> 0.66 us
    pallas_call x9 -> x11, Pallas kernels: 17.3 us -> 17.9 us  [call(): pl.pallas_call(body, in_specs=[pl.BlockSpec(memory_space=pltpu.SMEM)] + [...]
  transfers between devices with their start and end apart: 26 -> 26, of which waited for: 17 -> 14; matrix products, arithmetic and copies ran while one was open for 1% -> 1% of each run, Pallas kernels for 12% -> 15%
where the time goes in v4:
time: 66.1 us; the launch traced here: 65.9 us
  starting transfers between devices  24.4 us (37%)
  waiting for transfers between devices  19.4 us (29%)
  Pallas kernels  19 us (29%)
  between operations  1.48 us (2%)
  local copies, waits for them, and re-layouts  0.81 us (1%)
  other arithmetic  0.78 us (1%)
    pallas_call x11, Pallas kernels, call(): pl.pallas_call(body, in_specs=[pl.BlockSpec(memory_space=pltpu.SMEM)] + [...  17.9 us
    ppermute x9, starting transfers between devices, over_z(): return lax.ppermute(x, 'ctx', [(i, i ^ 2 * m) for i in range(count)])  13.4 us
    ppermute x9, waiting for transfers between devices, over_z(): return lax.ppermute(x, 'ctx', [(i, i ^ 2 * m) for i in range(count)])  7.99 us
    ppermute x3, starting transfers between devices, from_mask(): lax.ppermute(x, ('table', 'ctx'), [(t * count + c, (t ^ masks[c % 2]) * c...  5.69 us
    ppermute x3, waiting for transfers between devices, from_mask(): lax.ppermute(x, ('table', 'ctx'), [(t * count + c, (t ^ masks[c % 2]) * c...  3.99 us
    ppermute x3, waiting for transfers between devices, over_table(): return lax.ppermute(x, 'table', [(i, i ^ m) for i in range(tables)])  3.85 us
    ppermute x11, waiting for transfers between devices, swap(): return lax.ppermute(x, 'ctx', [(i, i ^ 1) for i in range(count)])  3.59 us
    ppermute x3, starting transfers between devices, over_table(): return lax.ppermute(x, 'table', [(i, i ^ m) for i in range(tables)])  3.55 us
  transfers between devices with their start and end apart: 26, of which 14 were waited for; matrix products, arithmetic and copies ran while one was open for 1% of the time, Pallas kernels for 15%

profile of v4, /device:TPU:0, one launch (start us, length us, event | category | flops | bytes accessed | tf_op | source)
XLA Modules:
  0.0 65.9 jit_solution(8111817967305812584)
XLA Ops:
  1.8 3.0 %collective-permute-start.2 = (bf16[256,512]{1,0:T(8,128)(2,1)S(1)}, bf16[256,512]{1,0:T(8,128)(2,1)S(1)}, u32[]{:S(2)}, u32[]{:S(2)}) collective-permute-start(bf16[256,512]{1,0:T(8,128)(2,1)S(1)} %get-tuple-element.56.refs_0_), channel_id=1, source_target_pairs={{0,8},{1,17},{2,10},{3,19},{4,12},{5,21},{6,14},{7,23},{8,0},{9,25... | collective-permute-start | bytes 786440 | tf_op jit(solution)/shard_map/ppermute | solution.py:424
  6.6 2.5 %collective-permute-done.2.refs_2_ = bf16[256,512]{1,0:T(8,128)(2,1)S(1)} collective-permute-done((bf16[256,512]{1,0:T(8,128)(2,1)S(1)}, bf16[256,512]{1,0:T(8,128)(2,1)S(1)}, u32[]{:S(2)}, u32[]{:S(2)}) %collective-permute-start.2) | collective-permute-done | bytes 262176 | tf_op jit(solution)/shard_map/ppermute | solution.py:424
  9.1 2.0 %collective-permute-start.4 = (bf16[256,512]{1,0:T(8,128)(2,1)S(1)}, bf16[256,512]{1,0:T(8,128)(2,1)S(1)}, u32[]{:S(2)}, u32[]{:S(2)}) collective-permute-start(bf16[256,512]{1,0:T(8,128)(2,1)S(1)} %collective-permute-done.2.refs_2_), channel_id=1, source_target_pairs={{0,16},{1,9},{2,18},{3,11},{4,20},{5,13},{6,22},{7,15},{8,24},{9,1... | collective-permute-start | bytes 786440 | tf_op jit(solution)/shard_map/ppermute | solution.py:424
  12.2 1.5 %collective-permute-done.3.refs_3_ = bf16[256,512]{1,0:T(8,128)(2,1)S(1)} collective-permute-done((bf16[256,512]{1,0:T(8,128)(2,1)S(1)}, bf16[256,512]{1,0:T(8,128)(2,1)S(1)}, u32[]{:S(2)}, u32[]{:S(2)}) %collective-permute-start.3) | collective-permute-done | bytes 262176 | tf_op jit(solution)/shard_map/ppermute | solution.py:424
  14.3 2.0 %prepare.1 = (bf16[2,256,256]{2,1,0:T(8,128)(2,1)S(1)}, bf16[2,256,256]{2,1,0:T(8,128)(2,1)S(1)}, s32[2,256]{1,0:T(2,128)S(1)}, bf16[4,16,128]{2,1,0:T(8,128)(2,...) custom-call(s32[4]{0:T(128)S(1)} %pad_add_fusion.1.info, ...), custom_call_target="tpu_custom_call" | custom-call | flops 134217728 | bytes 4219904 | tf_op jit(solution)/shard_map/prepare/pallas_call | solution.py:35
  16.9 1.2 %collective-permute-done.7.refs_3_ = bf16[256,512]{1,0:T(8,128)(2,1)S(1)} collective-permute-done((bf16[256,512]{1,0:T(8,128)(2,1)S(1)}, bf16[256,512]{1,0:T(8,128)(2,1)S(1)}, u32[]{:S(2)}, u32[]{:S(2)}) %collective-permute-start.7) | collective-permute-done | bytes 262176 | tf_op jit(solution)/shard_map/ppermute | solution.py:407
  18.1 2.9 %project.1 = (bf16[2,256,512]{2,1,0:T(8,128)(2,1)S(1)}, bf16[2,256,256]{2,1,0:T(8,128)(2,1)S(1)}, bf16[2,256,256]{2,1,0:T(8,128)(2,1)S(1)}, bf16[2,256,256]{2,1,...) custom-call(s32[4]{0:T(128)S(1)} %pad_add_fusion.1.info, ...), custom_call_target="tpu_custom_call" | custom-call | flops 1073741824 | bytes 8198144 | tf_op jit(solution)/shard_map/project/pallas_call | solution.py:35
  21.0 3.7 %collective-permute-start.10 = (bf16[64,256]{1,0:T(8,128)(2,1)S(1)}, bf16[64,256]{1,0:T(8,128)(2,1)S(1)}, u32[]{:S(2)}, u32[]{:S(2)}) collective-permute-start(bf16[64,256]{1,0:T(8,128)(2,1)S(1)} %get-tuple-element.84), channel_id=1, source_target_pairs={{0,6},{1,7},{2,4},{3,5},{4,2},{5,3},{6,0},{7,1},{8,14},{9,15},{10,... | collective-permute-start | bytes 98312 | tf_op jit(solution)/shard_map/ppermute | solution.py:404
  25.5 3.1 %attend.1 = (bf16[2,256,256]{2,1,0:T(8,128)(2,1)S(1)}, bf16[2,256,256]{2,1,0:T(8,128)(2,1)S(1)}, bf16[2,256,256]{2,1,0:T(8,128)(2,1)S(1)}) custom-call(s32[4]{0:T(128)S(1)} %pad_add_fusion.1.info, bf16[2,256,256]{2,1,0:T(8,128)(2,1)S(1)} %get-tuple-element.75.qa_in, bf16[2,256,256]{2,1,0:T(8,128)(2,1)S(1)} %get-tuple-element.67.kb_in.kb, ...), custom_call_target="tpu_custom_call" | custom-call | flops 402653184 | bytes 2883584 | tf_op jit(solution)/shard_map/attend/pallas_call | solution.py:35
  29.5 2.1 %finish.1 = (bf16[256,256]{1,0:T(8,128)(2,1)S(1)}, f32[2,256,256]{2,1,0:T(8,128)S(1)}, bf16[2,256,256]{2,1,0:T(8,128)(2,1)S(1)}) custom-call(s32[4]{0:T(128)S(1)} %pad_add_fusion.1.info, f32[1,256]{1,0:T(1,128)S(1)} %get-tuple-element.58.rate, bf16[2,256,256]{2,1,0:T(8,128)(2,1)S(1)} %get-tuple-element.67.kb_in.kb, ...), custom_call_target="tpu_custom_call" | custom-call | flops 402653184 | bytes 6788096 | tf_op jit(solution)/shard_map/finish/pallas_call | solution.py:35
  31.7 1.5 %collective-permute-done.11.row_came = bf16[2,256,256]{2,1,0:T(8,128)(2,1)S(1)} collective-permute-done((bf16[2,256,256]{2,1,0:T(8,128)(2,1)S(1)}, bf16[2,256,256]{2,1,0:T(8,128)(2,1)S(1)}, u32[]{:S(2)}, u32[]{:S(2)}) %collective-permute-start.11) | collective-permute-done | bytes 262176 | tf_op jit(solution)/shard_map/ppermute | solution.py:407
  34.1 1.6 %collective-permute-start.12 = (bf16[272,256]{1,0:T(8,128)(2,1)S(1)}, bf16[272,256]{1,0:T(8,128)(2,1)S(1)}, u32[]{:S(2)}, u32[]{:S(2)}) collective-permute-start(bf16[272,256]{1,0:T(8,128)(2,1)S(1)} %get-tuple-element.89), channel_id=1, source_target_pairs={{0,8},{8,0},{16,24},{24,16},{1,9},{9,1},{17,25},{25,17},{2,10},{10... | collective-permute-start | bytes 417800 | tf_op jit(solution)/shard_map/ppermute | solution.py:401
  35.7 1.5 %collective-permute-start.13 = (bf16[272,256]{1,0:T(8,128)(2,1)S(1)}, bf16[272,256]{1,0:T(8,128)(2,1)S(1)}, u32[]{:S(2)}, u32[]{:S(2)}) collective-permute-start(bf16[272,256]{1,0:T(8,128)(2,1)S(1)} %get-tuple-element.95), channel_id=1, source_target_pairs={{0,16},{8,24},{16,0},{24,8},{1,17},{9,25},{17,1},{25,9},{2,18},{10... | collective-permute-start | bytes 417800 | tf_op jit(solution)/shard_map/ppermute | solution.py:401
  37.7 2.8 %collective-permute-done.12.refs_1_ = bf16[272,256]{1,0:T(8,128)(2,1)S(1)} collective-permute-done((bf16[272,256]{1,0:T(8,128)(2,1)S(1)}, bf16[272,256]{1,0:T(8,128)(2,1)S(1)}, u32[]{:S(2)}, u32[]{:S(2)}) %collective-permute-start.12) | collective-permute-done | bytes 139296 | tf_op jit(solution)/shard_map/ppermute | solution.py:401
  40.4 1.6 %outward.1 = (bf16[256,256]{1,0:T(8,128)(2,1)S(1)}, bf16[256,256]{1,0:T(8,128)(2,1)S(1)}) custom-call(s32[4]{0:T(128)S(1)} %pad_add_fusion.1.info, bf16[2,256,256]{2,1,0:T(8,128)(2,1)S(1)} %get-tuple-element.75.qa_in, bf16[2,256,256]{2,1,0:T(8,128)(2,1)S(1)} %get-tuple-element.67.kb_in.kb, bf16[2,256,256]{2,1,0:T(8,128)(2,1)S(1)} %get-tuple-element.76.v_in, ...), custom_call_target="tpu_custom_call" | custom-call | flops 134217728 | bytes 1703936 | tf_op jit(solution)/shard_map/outward/pallas_call | solution.py:35
  45.0 2.8 %collective-permute-start.15 = (bf16[128,256]{1,0:T(8,128)(2,1)S(1)}, bf16[128,256]{1,0:T(8,128)(2,1)S(1)}, u32[]{:S(2)}, u32[]{:S(2)}) collective-permute-start(bf16[128,256]{1,0:T(8,128)(2,1)S(1)} %get-tuple-element.97), channel_id=1, source_target_pairs={{0,6},{1,7},{2,4},{3,5},{4,2},{5,3},{6,0},{7,1},{8,14},{9,15},{10,... | collective-permute-start | bytes 196616 | tf_op jit(solution)/shard_map/ppermute | solution.py:404
  47.8 1.7 %collective-permute-start.18 = (bf16[128,256]{1,0:T(8,128)(2,1)S(1)}, bf16[128,256]{1,0:T(8,128)(2,1)S(1)}, u32[]{:S(2)}, u32[]{:S(2)}) collective-permute-start(bf16[128,256]{1,0:T(8,128)(2,1)S(1)} %get-tuple-element.101), channel_id=1, source_target_pairs={{0,2},{1,3},{2,0},{3,1},{4,6},{5,7},{6,4},{7,5},{8,10},{9,11},{10,... | collective-permute-start | bytes 196616 | tf_op jit(solution)/shard_map/ppermute | solution.py:404
  49.4 1.7 %collective-permute-done.15.refs_1_ = bf16[128,256]{1,0:T(8,128)(2,1)S(1)} collective-permute-done((bf16[128,256]{1,0:T(8,128)(2,1)S(1)}, bf16[128,256]{1,0:T(8,128)(2,1)S(1)}, u32[]{:S(2)}, u32[]{:S(2)}) %collective-permute-start.15) | collective-permute-done | bytes 65568 | tf_op jit(solution)/shard_map/ppermute | solution.py:404
  51.2 1.6 %result.1 = bf16[256,512]{1,0:T(8,128)(2,1)} custom-call(s32[4]{0:T(128)S(1)} %pad_add_fusion.1.info, bf16[2,256,512]{2,1,0:T(8,128)(2,1)S(1)} %get-tuple-element.81.emb, bf16[256,256]{1,0:T(8,128)(2,1)S(1)} %get-tuple-element.102.att_own, bf16[256,256]{1,0:T(8,128)(2,1)S(1)} %collective-permute-done.16.att_came, bf16[512,512]{1,0:T(8,128)(2,1)S(1)} %get-tuple-element.104.w_out), custom_call_target="tpu_custom_call" | custom-call | flops 134217728 | bytes 1572864 | tf_op jit(solution)/shard_map/result/pallas_call | solution.py:35
  54.1 2.9 %collective-permute-start.21 = (bf16[128,256]{1,0:T(8,128)(2,1)S(1)}, bf16[128,256]{1,0:T(8,128)(2,1)S(1)}, u32[]{:S(2)}, u32[]{:S(2)}) collective-permute-start(bf16[128,256]{1,0:T(8,128)(2,1)S(1)} %add_up.1.refs_0_), channel_id=1, source_target_pairs={{0,6},{1,7},{2,4},{3,5},{4,2},{5,3},{6,0},{7,1},{8,14},{9,15},{10,... | collective-permute-start | bytes 196616 | tf_op jit(solution)/shard_map/ppermute | solution.py:404
  57.1 1.5 %collective-permute-start.19 = (bf16[128,256]{1,0:T(8,128)(2,1)S(1)}, bf16[128,256]{1,0:T(8,128)(2,1)S(1)}, u32[]{:S(2)}, u32[]{:S(2)}) collective-permute-start(bf16[128,256]{1,0:T(8,128)(2,1)S(1)} %add_up.1.refs_0_), channel_id=1, source_target_pairs={{0,2},{1,3},{2,0},{3,1},{4,6},{5,7},{6,4},{7,5},{8,10},{9,11},{10,... | collective-permute-start | bytes 196616 | tf_op jit(solution)/shard_map/ppermute | solution.py:404
  58.6 1.8 %collective-permute-done.21.refs_3_ = bf16[128,256]{1,0:T(8,128)(2,1)S(1)} collective-permute-done((bf16[128,256]{1,0:T(8,128)(2,1)S(1)}, bf16[128,256]{1,0:T(8,128)(2,1)S(1)}, u32[]{:S(2)}, u32[]{:S(2)}) %collective-permute-start.21) | collective-permute-done | bytes 65568 | tf_op jit(solution)/shard_map/ppermute | solution.py:404
  60.4 2.7 %collective-permute-done.20.refs_2_ = bf16[128,256]{1,0:T(8,128)(2,1)S(1)} collective-permute-done((bf16[128,256]{1,0:T(8,128)(2,1)S(1)}, bf16[128,256]{1,0:T(8,128)(2,1)S(1)}, u32[]{:S(2)}, u32[]{:S(2)}) %collective-permute-start.20) | collective-permute-done | bytes 65568 | tf_op jit(solution)/shard_map/ppermute | solution.py:404
  64.5 1.4 %assemble.1 = bf16[512,512]{1,0:T(8,128)(2,1)} custom-call(s32[4]{0:T(128)S(1)} %pad_add_fusion.1.info, bf16[128,256]{1,0:T(8,128)(2,1)S(1)} %add_up.1.refs_0_, bf16[128,256]{1,0:T(8,128)(2,1)S(1)} %collective-permute-done.19.refs_1_, bf16[128,256]{1,0:T(8,128)(2,1)S(1)} %collective-permute-done.20.refs_2_, ...), custom_call_target="tpu_custom_call" | custom-call | flops 262144 | bytes 1048576 | tf_op jit(solution)/shard_map/assemble/pallas_call | solution.py:35
  (58 shorter events, 13.4 us)
Async XLA Ops:
  1.8 7.4 %collective-permute-start.2 = (bf16[256,512]{1,0:T(8,128)(2,1)S(1)}, bf16[256,512]{1,0:T(8,128)(2,1)S(1)}, u32[]{:S(2)}, u32[]{:S(2)}) collective-permute-start(bf16[256,512]{1,0:T(8,128)(2,1)S(1)} %get-tuple-element.56.refs_0_), channel_id=1, source_target_pairs={{0,8},{1,17},{2,10},{3,19},{4,12},{5,21},{6,14},{7,23},{8,0},{9,25... | collective-permute-start | bytes 786440 | tf_op jit(solution)/shard_map/ppermute | solution.py:424
  5.5 8.2 %collective-permute-start = (bf16[256,512]{1,0:T(8,128)(2,1)S(1)}, bf16[256,512]{1,0:T(8,128)(2,1)S(1)}, u32[]{:S(2)}, u32[]{:S(2)}) collective-permute-start(bf16[256,512]{1,0:T(8,128)(2,1)S(1)} %bitcast.11), channel_id=1, source_target_pairs={{0,1},{1,0},{2,3},{3,2},{4,5},{5,4},{6,7},{7,6},{8,9},{9,8},{10,11... | collective-permute-start | bytes 786440 | tf_op jit(solution)/shard_map/ppermute | solution.py:407
  6.0 7.7 %collective-permute-start.3 = (bf16[256,512]{1,0:T(8,128)(2,1)S(1)}, bf16[256,512]{1,0:T(8,128)(2,1)S(1)}, u32[]{:S(2)}, u32[]{:S(2)}) collective-permute-start(bf16[256,512]{1,0:T(8,128)(2,1)S(1)} %get-tuple-element.57.refs_1_), channel_id=1, source_target_pairs={{0,8},{1,17},{2,10},{3,19},{4,12},{5,21},{6,14},{7,23},{8,0},{9,25... | collective-permute-start | bytes 786440 | tf_op jit(solution)/shard_map/ppermute | solution.py:424
  9.1 7.2 %collective-permute-start.4 = (bf16[256,512]{1,0:T(8,128)(2,1)S(1)}, bf16[256,512]{1,0:T(8,128)(2,1)S(1)}, u32[]{:S(2)}, u32[]{:S(2)}) collective-permute-start(bf16[256,512]{1,0:T(8,128)(2,1)S(1)} %collective-permute-done.2.refs_2_), channel_id=1, source_target_pairs={{0,16},{1,9},{2,18},{3,11},{4,20},{5,13},{6,22},{7,15},{8,24},{9,1... | collective-permute-start | bytes 786440 | tf_op jit(solution)/shard_map/ppermute | solution.py:424
  12.1 4.9 %collective-permute-start.5 = (bf16[256,512]{1,0:T(8,128)(2,1)S(1)}, bf16[256,512]{1,0:T(8,128)(2,1)S(1)}, u32[]{:S(2)}, u32[]{:S(2)}) collective-permute-start(bf16[256,512]{1,0:T(8,128)(2,1)S(1)} %collective-permute-done.2.refs_2_), channel_id=1, source_target_pairs={{0,1},{1,0},{2,3},{3,2},{4,5},{5,4},{6,7},{7,6},{8,9},{9,8},{10,11... | collective-permute-start | bytes 786440 | tf_op jit(solution)/shard_map/ppermute | solution.py:407
  13.7 3.3 %collective-permute-start.6 = (bf16[256,512]{1,0:T(8,128)(2,1)S(1)}, bf16[256,512]{1,0:T(8,128)(2,1)S(1)}, u32[]{:S(2)}, u32[]{:S(2)}) collective-permute-start(bf16[256,512]{1,0:T(8,128)(2,1)S(1)} %collective-permute-done.3.refs_3_), channel_id=1, source_target_pairs={{0,1},{1,0},{2,3},{3,2},{4,5},{5,4},{6,7},{7,6},{8,9},{9,8},{10,11... | collective-permute-start | bytes 786440 | tf_op jit(solution)/shard_map/ppermute | solution.py:407
  16.4 1.7 %collective-permute-start.7 = (bf16[256,512]{1,0:T(8,128)(2,1)S(1)}, bf16[256,512]{1,0:T(8,128)(2,1)S(1)}, u32[]{:S(2)}, u32[]{:S(2)}) collective-permute-start(bf16[256,512]{1,0:T(8,128)(2,1)S(1)} %collective-permute-done.4.refs_0_), channel_id=1, source_target_pairs={{0,1},{1,0},{2,3},{3,2},{4,5},{5,4},{6,7},{7,6},{8,9},{9,8},{10,11... | collective-permute-start | bytes 786440 | tf_op jit(solution)/shard_map/ppermute | solution.py:407
  21.0 7.9 %collective-permute-start.10 = (bf16[64,256]{1,0:T(8,128)(2,1)S(1)}, bf16[64,256]{1,0:T(8,128)(2,1)S(1)}, u32[]{:S(2)}, u32[]{:S(2)}) collective-permute-start(bf16[64,256]{1,0:T(8,128)(2,1)S(1)} %get-tuple-element.84), channel_id=1, source_target_pairs={{0,6},{1,7},{2,4},{3,5},{4,2},{5,3},{6,0},{7,1},{8,14},{9,15},{10,... | collective-permute-start | bytes 98312 | tf_op jit(solution)/shard_map/ppermute | solution.py:404
  24.7 4.8 %collective-permute-start.9 = (bf16[64,256]{1,0:T(8,128)(2,1)S(1)}, bf16[64,256]{1,0:T(8,128)(2,1)S(1)}, u32[]{:S(2)}, u32[]{:S(2)}) collective-permute-start(bf16[64,256]{1,0:T(8,128)(2,1)S(1)} %get-tuple-element.84), channel_id=1, source_target_pairs={{0,4},{1,5},{2,6},{3,7},{4,0},{5,1},{6,2},{7,3},{8,12},{9,13},{10,... | collective-permute-start | bytes 98312 | tf_op jit(solution)/shard_map/ppermute | solution.py:404
  24.7 4.3 %collective-permute-start.8 = (bf16[64,256]{1,0:T(8,128)(2,1)S(1)}, bf16[64,256]{1,0:T(8,128)(2,1)S(1)}, u32[]{:S(2)}, u32[]{:S(2)}) collective-permute-start(bf16[64,256]{1,0:T(8,128)(2,1)S(1)} %get-tuple-element.83), channel_id=1, source_target_pairs={{0,2},{1,3},{2,0},{3,1},{4,6},{5,7},{6,4},{7,5},{8,10},{9,11},{10,... | collective-permute-start | bytes 98312 | tf_op jit(solution)/shard_map/ppermute | solution.py:404
  31.7 1.6 %collective-permute-start.11 = (bf16[2,256,256]{2,1,0:T(8,128)(2,1)S(1)}, bf16[2,256,256]{2,1,0:T(8,128)(2,1)S(1)}, u32[]{:S(2)}, u32[]{:S(2)}) collective-permute-start(bf16[2,256,256]{2,1,0:T(8,128)(2,1)S(1)} %get-tuple-element.86), channel_id=1, source_target_pairs={{0,1},{1,0},{2,3},{3,2},{4,5},{5,4},{6,7},{7,6},{8,9},{9,8},{10,11... | collective-permute-start | bytes 786440 | tf_op jit(solution)/shard_map/ppermute | solution.py:407
  34.1 6.3 %collective-permute-start.12 = (bf16[272,256]{1,0:T(8,128)(2,1)S(1)}, bf16[272,256]{1,0:T(8,128)(2,1)S(1)}, u32[]{:S(2)}, u32[]{:S(2)}) collective-permute-start(bf16[272,256]{1,0:T(8,128)(2,1)S(1)} %get-tuple-element.89), channel_id=1, source_target_pairs={{0,8},{8,0},{16,24},{24,16},{1,9},{9,1},{17,25},{25,17},{2,10},{10... | collective-permute-start | bytes 417800 | tf_op jit(solution)/shard_map/ppermute | solution.py:401
  35.7 8.4 %collective-permute-start.13 = (bf16[272,256]{1,0:T(8,128)(2,1)S(1)}, bf16[272,256]{1,0:T(8,128)(2,1)S(1)}, u32[]{:S(2)}, u32[]{:S(2)}) collective-permute-start(bf16[272,256]{1,0:T(8,128)(2,1)S(1)} %get-tuple-element.95), channel_id=1, source_target_pairs={{0,16},{8,24},{16,0},{24,8},{1,17},{9,25},{17,1},{25,9},{2,18},{10... | collective-permute-start | bytes 417800 | tf_op jit(solution)/shard_map/ppermute | solution.py:401
  37.2 6.9 %collective-permute-start.14 = (bf16[272,256]{1,0:T(8,128)(2,1)S(1)}, bf16[272,256]{1,0:T(8,128)(2,1)S(1)}, u32[]{:S(2)}, u32[]{:S(2)}) collective-permute-start(bf16[272,256]{1,0:T(8,128)(2,1)S(1)} %get-tuple-element.96), channel_id=1, source_target_pairs={{0,24},{8,16},{16,8},{24,0},{1,25},{9,17},{17,9},{25,1},{2,26},{10... | collective-permute-start | bytes 417800 | tf_op jit(solution)/shard_map/ppermute | solution.py:401
  42.9 8.2 %collective-permute-start.16 = (bf16[256,256]{1,0:T(8,128)(2,1)S(1)}, bf16[256,256]{1,0:T(8,128)(2,1)S(1)}, u32[]{:S(2)}, u32[]{:S(2)}) collective-permute-start(bf16[256,256]{1,0:T(8,128)(2,1)S(1)} %get-tuple-element.98), channel_id=1, source_target_pairs={{0,1},{1,0},{2,3},{3,2},{4,5},{5,4},{6,7},{7,6},{8,9},{9,8},{10,11... | collective-permute-start | bytes 393224 | tf_op jit(solution)/shard_map/ppermute | solution.py:407
  45.0 6.2 %collective-permute-start.15 = (bf16[128,256]{1,0:T(8,128)(2,1)S(1)}, bf16[128,256]{1,0:T(8,128)(2,1)S(1)}, u32[]{:S(2)}, u32[]{:S(2)}) collective-permute-start(bf16[128,256]{1,0:T(8,128)(2,1)S(1)} %get-tuple-element.97), channel_id=1, source_target_pairs={{0,6},{1,7},{2,4},{3,5},{4,2},{5,3},{6,0},{7,1},{8,14},{9,15},{10,... | collective-permute-start | bytes 196616 | tf_op jit(solution)/shard_map/ppermute | solution.py:404
  47.8 5.8 %collective-permute-start.17 = (bf16[128,256]{1,0:T(8,128)(2,1)S(1)}, bf16[128,256]{1,0:T(8,128)(2,1)S(1)}, u32[]{:S(2)}, u32[]{:S(2)}) collective-permute-start(bf16[128,256]{1,0:T(8,128)(2,1)S(1)} %get-tuple-element.100), channel_id=1, source_target_pairs={{0,4},{1,5},{2,6},{3,7},{4,0},{5,1},{6,2},{7,3},{8,12},{9,13},{10,... | collective-permute-start | bytes 196616 | tf_op jit(solution)/shard_map/ppermute | solution.py:404
  47.8 5.8 %collective-permute-start.18 = (bf16[128,256]{1,0:T(8,128)(2,1)S(1)}, bf16[128,256]{1,0:T(8,128)(2,1)S(1)}, u32[]{:S(2)}, u32[]{:S(2)}) collective-permute-start(bf16[128,256]{1,0:T(8,128)(2,1)S(1)} %get-tuple-element.101), channel_id=1, source_target_pairs={{0,2},{1,3},{2,0},{3,1},{4,6},{5,7},{6,4},{7,5},{8,10},{9,11},{10,... | collective-permute-start | bytes 196616 | tf_op jit(solution)/shard_map/ppermute | solution.py:404
  54.1 6.3 %collective-permute-start.21 = (bf16[128,256]{1,0:T(8,128)(2,1)S(1)}, bf16[128,256]{1,0:T(8,128)(2,1)S(1)}, u32[]{:S(2)}, u32[]{:S(2)}) collective-permute-start(bf16[128,256]{1,0:T(8,128)(2,1)S(1)} %add_up.1.refs_0_), channel_id=1, source_target_pairs={{0,6},{1,7},{2,4},{3,5},{4,2},{5,3},{6,0},{7,1},{8,14},{9,15},{10,... | collective-permute-start | bytes 196616 | tf_op jit(solution)/shard_map/ppermute | solution.py:404
  57.1 6.1 %collective-permute-start.20 = (bf16[128,256]{1,0:T(8,128)(2,1)S(1)}, bf16[128,256]{1,0:T(8,128)(2,1)S(1)}, u32[]{:S(2)}, u32[]{:S(2)}) collective-permute-start(bf16[128,256]{1,0:T(8,128)(2,1)S(1)} %add_up.1.refs_0_), channel_id=1, source_target_pairs={{0,4},{1,5},{2,6},{3,7},{4,0},{5,1},{6,2},{7,3},{8,12},{9,13},{10,... | collective-permute-start | bytes 196616 | tf_op jit(solution)/shard_map/ppermute | solution.py:404
  57.1 6.0 %collective-permute-start.19 = (bf16[128,256]{1,0:T(8,128)(2,1)S(1)}, bf16[128,256]{1,0:T(8,128)(2,1)S(1)}, u32[]{:S(2)}, u32[]{:S(2)}) collective-permute-start(bf16[128,256]{1,0:T(8,128)(2,1)S(1)} %add_up.1.refs_0_), channel_id=1, source_target_pairs={{0,2},{1,3},{2,0},{3,1},{4,6},{5,7},{6,4},{7,5},{8,10},{9,11},{10,... | collective-permute-start | bytes 196616 | tf_op jit(solution)/shard_map/ppermute | solution.py:404
  58.6 5.0 %collective-permute-start.22 = (bf16[128,256]{1,0:T(8,128)(2,1)S(1)}, bf16[128,256]{1,0:T(8,128)(2,1)S(1)}, u32[]{:S(2)}, u32[]{:S(2)}) collective-permute-start(bf16[128,256]{1,0:T(8,128)(2,1)S(1)} %add_up.1.refs_0_), channel_id=1, source_target_pairs={{0,1},{1,0},{2,3},{3,2},{4,5},{5,4},{6,7},{7,6},{8,9},{9,8},{10,11... | collective-permute-start | bytes 196616 | tf_op jit(solution)/shard_map/ppermute | solution.py:407
  60.4 3.2 %collective-permute-start.25 = (bf16[128,256]{1,0:T(8,128)(2,1)S(1)}, bf16[128,256]{1,0:T(8,128)(2,1)S(1)}, u32[]{:S(2)}, u32[]{:S(2)}) collective-permute-start(bf16[128,256]{1,0:T(8,128)(2,1)S(1)} %collective-permute-done.21.refs_3_), channel_id=1, source_target_pairs={{0,1},{1,0},{2,3},{3,2},{4,5},{5,4},{6,7},{7,6},{8,9},{9,8},{10,11... | collective-permute-start | bytes 196616 | tf_op jit(solution)/shard_map/ppermute | solution.py:407
  63.1 1.4 %collective-permute-start.23 = (bf16[128,256]{1,0:T(8,128)(2,1)S(1)}, bf16[128,256]{1,0:T(8,128)(2,1)S(1)}, u32[]{:S(2)}, u32[]{:S(2)}) collective-permute-start(bf16[128,256]{1,0:T(8,128)(2,1)S(1)} %collective-permute-done.19.refs_1_), channel_id=1, source_target_pairs={{0,1},{1,0},{2,3},{3,2},{4,5},{5,4},{6,7},{7,6},{8,9},{9,8},{10,11... | collective-permute-start | bytes 196616 | tf_op jit(solution)/shard_map/ppermute | solution.py:407
  (9 other events, 33.9 us)

commit v5 on v4

--- a/solution.py
+++ b/solution.py
@@ -219,10 +219,8 @@
         every = jnp.concatenate([left * only for only in self.lanes], 0)
         scores = dot_nt(every, right).astype(BF16)
         scores = [scores[h * length : (h + 1) * length] * mask for h in range(self.count)]
-        whole = dot(jnp.concatenate(scores, 0), value)
-        total = whole[:length]
-        for h in range(1, self.count):
-            total = jnp.where(self.lane_head == h, whole[h * length : (h + 1) * length], total)
+        values = jnp.concatenate([value * only for only in self.lanes], 0)
+        total = dot(jnp.concatenate(scores, 1), values)
         return total
 
 
@@ -439,7 +437,7 @@
         rest = from_mask(second, (1, 2))
         far = from_mask(lax.optimization_barrier((near, ids_row))[0], (2, 1))
         fetched = [(near, (1, 2), (0, 1)), (rest, (1, 2), (1, 0)), (far, (3, 3), (0, 1))]
-        early = fetched[:2]
+        early = fetched[:1]
     else:
         fetched = [(over_table(first, m), (m, m), (0, 1)) for m in range(1, tables)]
         early = []
@@ -470,8 +468,8 @@
         away=(rate[None, :], w_out, d_own, gain[None, :]),
         scratch=[pltpu.VMEM((1, heads), F32), pltpu.SemaphoreType.DMA((4,))],
     )
-    others = [swap(x) for x, _, _ in fetched[:-1]]
-    others.append(swap(lax.optimization_barrier((fetched[-1][0], dest))[0]))
+    others = [swap(fetched[0][0])]
+    others += [swap(lax.optimization_barrier((x, meta))[0]) for x, _, _ in fetched[1:]]
     late += [(x, m[::-1], h[::-1]) for x, (_, m, h) in zip(others, fetched)]
     bits = max(chips - 1, 1).bit_length() if chips > 1 else 0
     emb, v, qa, kb, vb, qn, kn, qs, ks, rstd, states, *sends = call(
@@ -548,7 +546,7 @@
         None,
         [pltpu.VMEM((rows, half), F32)],
     )
-    pieces = [over_z(everything[m], m) for m in reversed(range(1, chips))]
+    pieces = [over_z(everything[m], m) for m in (*range(chips - 1, chips), *range(1, chips - 1)) if m]
     if pieces:
         pieces[0], att_came = lax.optimization_barrier((pieces[0], att_came))
     (output,) = call(

time: 66.1 us -> 64.5 us (0.976)
  waiting for transfers between devices: 19.4 us -> 18 us
    ppermute x3, waiting for transfers between devices: 3.99 us -> 2.78 us  [from_mask(): lax.ppermute(x, ('table', 'ctx'), [(t * count + c, (t ^ masks[c % 2]) * c...]
    ppermute x9, waiting for transfers between devices: 7.99 us -> 7.31 us  [over_z(): return lax.ppermute(x, 'ctx', [(i, i ^ 2 * m) for i in range(count)])]
  transfers between devices with their start and end apart: 26 -> 26, of which waited for: 14 -> 15; matrix products, arithmetic and copies ran while one was open for 1% -> 1% of each run, Pallas kernels for 15% -> 14%
where the time goes in v5:
time: 64.5 us; the launch traced here: 64.3 us
  starting transfers between devices  24.7 us (38%)
  Pallas kernels  18.5 us (29%)
  waiting for transfers between devices  18 us (28%)
  between operations  1.49 us (2%)
  local copies, waits for them, and re-layouts  0.82 us (1%)
  other arithmetic  0.78 us (1%)
    pallas_call x11, Pallas kernels, call(): pl.pallas_call(body, in_specs=[pl.BlockSpec(memory_space=pltpu.SMEM)] + [...  17.4 us
    ppermute x9, starting transfers between devices, over_z(): return lax.ppermute(x, 'ctx', [(i, i ^ 2 * m) for i in range(count)])  13.7 us
    ppermute x9, waiting for transfers between devices, over_z(): return lax.ppermute(x, 'ctx', [(i, i ^ 2 * m) for i in range(count)])  7.31 us
    ppermute x3, starting transfers between devices, from_mask(): lax.ppermute(x, ('table', 'ctx'), [(t * count + c, (t ^ masks[c % 2]) * c...  5.69 us
    ppermute x3, waiting for transfers between devices, over_table(): return lax.ppermute(x, 'table', [(i, i ^ m) for i in range(tables)])  3.99 us
    ppermute x11, waiting for transfers between devices, swap(): return lax.ppermute(x, 'ctx', [(i, i ^ 1) for i in range(count)])  3.96 us
    ppermute x3, starting transfers between devices, over_table(): return lax.ppermute(x, 'table', [(i, i ^ m) for i in range(tables)])  3.55 us
    ppermute x3, waiting for transfers between devices, from_mask(): lax.ppermute(x, ('table', 'ctx'), [(t * count + c, (t ^ masks[c % 2]) * c...  2.78 us
  transfers between devices with their start and end apart: 26, of which 15 were waited for; matrix products, arithmetic and copies ran while one was open for 1% of the time, Pallas kernels for 14%

profile of v5, /device:TPU:0, one launch (start us, length us, event | category | flops | bytes accessed | tf_op | source)
XLA Modules:
  0.0 64.3 jit_solution(8103049941878228438)
XLA Ops:
  0.7 1.1 %pick.1 = (bf16[256,512]{1,0:T(8,128)(2,1)S(1)}, bf16[256,512]{1,0:T(8,128)(2,1)S(1)}) custom-call(bf16[512,512]{1,0:T(8,128)(2,1)} %table.1), custom_call_target="tpu_custom_call" | custom-call | tf_op jit(solution)/shard_map/pick/pallas_call | solution.py:412
  1.8 3.0 %collective-permute-start.2 = (bf16[256,512]{1,0:T(8,128)(2,1)S(1)}, bf16[256,512]{1,0:T(8,128)(2,1)S(1)}, u32[]{:S(2)}, u32[]{:S(2)}) collective-permute-start(bf16[256,512]{1,0:T(8,128)(2,1)S(1)} %get-tuple-element.57.refs_0_), channel_id=1, source_target_pairs={{0,8},{1,17},{2,10},{3,19},{4,12},{5,21},{6,14},{7,23},{8,0},{9,25... | collective-permute-start | bytes 786440 | tf_op jit(solution)/shard_map/ppermute | solution.py:422
  6.6 2.5 %collective-permute-done.2.refs_2_ = bf16[256,512]{1,0:T(8,128)(2,1)S(1)} collective-permute-done((bf16[256,512]{1,0:T(8,128)(2,1)S(1)}, bf16[256,512]{1,0:T(8,128)(2,1)S(1)}, u32[]{:S(2)}, u32[]{:S(2)}) %collective-permute-start.2) | collective-permute-done | bytes 262176 | tf_op jit(solution)/shard_map/ppermute | solution.py:422
  9.1 2.0 %collective-permute-start.4 = (bf16[256,512]{1,0:T(8,128)(2,1)S(1)}, bf16[256,512]{1,0:T(8,128)(2,1)S(1)}, u32[]{:S(2)}, u32[]{:S(2)}) collective-permute-start(bf16[256,512]{1,0:T(8,128)(2,1)S(1)} %collective-permute-done.2.refs_2_), channel_id=1, source_target_pairs={{0,16},{1,9},{2,18},{3,11},{4,20},{5,13},{6,22},{7,15},{8,24},{9,1... | collective-permute-start | bytes 786440 | tf_op jit(solution)/shard_map/ppermute | solution.py:422
  12.8 1.9 %prepare.1 = (bf16[2,256,256]{2,1,0:T(8,128)(2,1)S(1)}, bf16[2,256,256]{2,1,0:T(8,128)(2,1)S(1)}, s32[2,256]{1,0:T(2,128)S(1)}, bf16[4,16,128]{2,1,0:T(8,128)(2,...) custom-call(s32[4]{0:T(128)S(1)} %pad_add_fusion.1.info, ...), custom_call_target="tpu_custom_call" | custom-call | flops 134217728 | bytes 3957760 | tf_op jit(solution)/shard_map/prepare/pallas_call | solution.py:35
  17.1 3.1 %project.1 = (bf16[2,256,512]{2,1,0:T(8,128)(2,1)S(1)}, bf16[2,256,256]{2,1,0:T(8,128)(2,1)S(1)}, bf16[2,256,256]{2,1,0:T(8,128)(2,1)S(1)}, bf16[2,256,256]{2,1,...) custom-call(s32[4]{0:T(128)S(1)} %pad_add_fusion.1.info, ...), custom_call_target="tpu_custom_call" | custom-call | flops 1073741824 | bytes 8460288 | tf_op jit(solution)/shard_map/project/pallas_call | solution.py:35
  20.2 4.2 %collective-permute-start.10 = (bf16[64,256]{1,0:T(8,128)(2,1)S(1)}, bf16[64,256]{1,0:T(8,128)(2,1)S(1)}, u32[]{:S(2)}, u32[]{:S(2)}) collective-permute-start(bf16[64,256]{1,0:T(8,128)(2,1)S(1)} %get-tuple-element.86), channel_id=1, source_target_pairs={{0,6},{1,7},{2,4},{3,5},{4,2},{5,3},{6,0},{7,1},{8,14},{9,15},{10,... | collective-permute-start | bytes 98312 | tf_op jit(solution)/shard_map/ppermute | solution.py:402
  25.0 2.7 %attend.1 = (bf16[2,256,256]{2,1,0:T(8,128)(2,1)S(1)}, bf16[2,256,256]{2,1,0:T(8,128)(2,1)S(1)}, bf16[2,256,256]{2,1,0:T(8,128)(2,1)S(1)}) custom-call(s32[4]{0:T(128)S(1)} %pad_add_fusion.1.info, bf16[2,256,256]{2,1,0:T(8,128)(2,1)S(1)} %get-tuple-element.77.qa_in, bf16[2,256,256]{2,1,0:T(8,128)(2,1)S(1)} %get-tuple-element.69.kb_in.kb, ...), custom_call_target="tpu_custom_call" | custom-call | flops 402653184 | bytes 2883584 | tf_op jit(solution)/shard_map/attend/pallas_call | solution.py:35
  29.2 2.1 %finish.1 = (bf16[256,256]{1,0:T(8,128)(2,1)S(1)}, f32[2,256,256]{2,1,0:T(8,128)S(1)}, bf16[2,256,256]{2,1,0:T(8,128)(2,1)S(1)}) custom-call(s32[4]{0:T(128)S(1)} %pad_add_fusion.1.info, f32[1,256]{1,0:T(1,128)S(1)} %get-tuple-element.59.rate, bf16[2,256,256]{2,1,0:T(8,128)(2,1)S(1)} %get-tuple-element.69.kb_in.kb, ...), custom_call_target="tpu_custom_call" | custom-call | flops 402653184 | bytes 6788096 | tf_op jit(solution)/shard_map/finish/pallas_call | solution.py:35
  31.4 1.5 %collective-permute-done.11.row_came = bf16[2,256,256]{2,1,0:T(8,128)(2,1)S(1)} collective-permute-done((bf16[2,256,256]{2,1,0:T(8,128)(2,1)S(1)}, bf16[2,256,256]{2,1,0:T(8,128)(2,1)S(1)}, u32[]{:S(2)}, u32[]{:S(2)}) %collective-permute-start.11) | collective-permute-done | bytes 262176 | tf_op jit(solution)/shard_map/ppermute | solution.py:405
  33.8 1.6 %collective-permute-start.12 = (bf16[272,256]{1,0:T(8,128)(2,1)S(1)}, bf16[272,256]{1,0:T(8,128)(2,1)S(1)}, u32[]{:S(2)}, u32[]{:S(2)}) collective-permute-start(bf16[272,256]{1,0:T(8,128)(2,1)S(1)} %get-tuple-element.91), channel_id=1, source_target_pairs={{0,8},{8,0},{16,24},{24,16},{1,9},{9,1},{17,25},{25,17},{2,10},{10... | collective-permute-start | bytes 417800 | tf_op jit(solution)/shard_map/ppermute | solution.py:399
  35.3 1.5 %collective-permute-start.13 = (bf16[272,256]{1,0:T(8,128)(2,1)S(1)}, bf16[272,256]{1,0:T(8,128)(2,1)S(1)}, u32[]{:S(2)}, u32[]{:S(2)}) collective-permute-start(bf16[272,256]{1,0:T(8,128)(2,1)S(1)} %get-tuple-element.97), channel_id=1, source_target_pairs={{0,16},{8,24},{16,0},{24,8},{1,17},{9,25},{17,1},{25,9},{2,18},{10... | collective-permute-start | bytes 417800 | tf_op jit(solution)/shard_map/ppermute | solution.py:399
  37.3 2.7 %collective-permute-done.12.refs_1_ = bf16[272,256]{1,0:T(8,128)(2,1)S(1)} collective-permute-done((bf16[272,256]{1,0:T(8,128)(2,1)S(1)}, bf16[272,256]{1,0:T(8,128)(2,1)S(1)}, u32[]{:S(2)}, u32[]{:S(2)}) %collective-permute-start.12) | collective-permute-done | bytes 139296 | tf_op jit(solution)/shard_map/ppermute | solution.py:399
  40.1 1.5 %outward.1 = (bf16[256,256]{1,0:T(8,128)(2,1)S(1)}, bf16[256,256]{1,0:T(8,128)(2,1)S(1)}) custom-call(s32[4]{0:T(128)S(1)} %pad_add_fusion.1.info, bf16[2,256,256]{2,1,0:T(8,128)(2,1)S(1)} %get-tuple-element.77.qa_in, bf16[2,256,256]{2,1,0:T(8,128)(2,1)S(1)} %get-tuple-element.69.kb_in.kb, bf16[2,256,256]{2,1,0:T(8,128)(2,1)S(1)} %get-tuple-element.78.v_in, ...), custom_call_target="tpu_custom_call" | custom-call | flops 134217728 | bytes 1703936 | tf_op jit(solution)/shard_map/outward/pallas_call | solution.py:35
  42.5 1.2 %collective-permute-done.13.refs_0_ = bf16[272,256]{1,0:T(8,128)(2,1)S(1)} collective-permute-done((bf16[272,256]{1,0:T(8,128)(2,1)S(1)}, bf16[272,256]{1,0:T(8,128)(2,1)S(1)}, u32[]{:S(2)}, u32[]{:S(2)}) %collective-permute-start.13) | collective-permute-done | bytes 139296 | tf_op jit(solution)/shard_map/ppermute | solution.py:399
  44.6 2.4 %collective-permute-start.15 = (bf16[128,256]{1,0:T(8,128)(2,1)S(1)}, bf16[128,256]{1,0:T(8,128)(2,1)S(1)}, u32[]{:S(2)}, u32[]{:S(2)}) collective-permute-start(bf16[128,256]{1,0:T(8,128)(2,1)S(1)} %get-tuple-element.99), channel_id=1, source_target_pairs={{0,6},{1,7},{2,4},{3,5},{4,2},{5,3},{6,0},{7,1},{8,14},{9,15},{10,... | collective-permute-start | bytes 196616 | tf_op jit(solution)/shard_map/ppermute | solution.py:402
  47.3 1.8 %collective-permute-start.18 = (bf16[128,256]{1,0:T(8,128)(2,1)S(1)}, bf16[128,256]{1,0:T(8,128)(2,1)S(1)}, u32[]{:S(2)}, u32[]{:S(2)}) collective-permute-start(bf16[128,256]{1,0:T(8,128)(2,1)S(1)} %get-tuple-element.103), channel_id=1, source_target_pairs={{0,4},{1,5},{2,6},{3,7},{4,0},{5,1},{6,2},{7,3},{8,12},{9,13},{10,... | collective-permute-start | bytes 196616 | tf_op jit(solution)/shard_map/ppermute | solution.py:402
  49.1 2.0 %collective-permute-done.15.refs_1_ = bf16[128,256]{1,0:T(8,128)(2,1)S(1)} collective-permute-done((bf16[128,256]{1,0:T(8,128)(2,1)S(1)}, bf16[128,256]{1,0:T(8,128)(2,1)S(1)}, u32[]{:S(2)}, u32[]{:S(2)}) %collective-permute-start.15) | collective-permute-done | bytes 65568 | tf_op jit(solution)/shard_map/ppermute | solution.py:402
  51.1 1.6 %result.1 = bf16[256,512]{1,0:T(8,128)(2,1)} custom-call(s32[4]{0:T(128)S(1)} %pad_add_fusion.1.info, bf16[2,256,512]{2,1,0:T(8,128)(2,1)S(1)} %get-tuple-element.83.emb, bf16[256,256]{1,0:T(8,128)(2,1)S(1)} %get-tuple-element.104.att_own, bf16[256,256]{1,0:T(8,128)(2,1)S(1)} %collective-permute-done.16.att_came, bf16[512,512]{1,0:T(8,128)(2,1)S(1)} %get-tuple-element.106.w_out), custom_call_target="tpu_custom_call" | custom-call | flops 134217728 | bytes 1572864 | tf_op jit(solution)/shard_map/result/pallas_call | solution.py:35
  53.3 2.9 %collective-permute-start.21 = (bf16[128,256]{1,0:T(8,128)(2,1)S(1)}, bf16[128,256]{1,0:T(8,128)(2,1)S(1)}, u32[]{:S(2)}, u32[]{:S(2)}) collective-permute-start(bf16[128,256]{1,0:T(8,128)(2,1)S(1)} %add_up.1.refs_0_), channel_id=1, source_target_pairs={{0,6},{1,7},{2,4},{3,5},{4,2},{5,3},{6,0},{7,1},{8,14},{9,15},{10,... | collective-permute-start | bytes 196616 | tf_op jit(solution)/shard_map/ppermute | solution.py:402
  56.3 1.4 %collective-permute-start.19 = (bf16[128,256]{1,0:T(8,128)(2,1)S(1)}, bf16[128,256]{1,0:T(8,128)(2,1)S(1)}, u32[]{:S(2)}, u32[]{:S(2)}) collective-permute-start(bf16[128,256]{1,0:T(8,128)(2,1)S(1)} %add_up.1.refs_0_), channel_id=1, source_target_pairs={{0,2},{1,3},{2,0},{3,1},{4,6},{5,7},{6,4},{7,5},{8,10},{9,11},{10,... | collective-permute-start | bytes 196616 | tf_op jit(solution)/shard_map/ppermute | solution.py:402
  57.7 2.1 %collective-permute-done.21.refs_3_ = bf16[128,256]{1,0:T(8,128)(2,1)S(1)} collective-permute-done((bf16[128,256]{1,0:T(8,128)(2,1)S(1)}, bf16[128,256]{1,0:T(8,128)(2,1)S(1)}, u32[]{:S(2)}, u32[]{:S(2)}) %collective-permute-start.21) | collective-permute-done | bytes 65568 | tf_op jit(solution)/shard_map/ppermute | solution.py:402
  59.8 1.7 %collective-permute-done.20.refs_2_ = bf16[128,256]{1,0:T(8,128)(2,1)S(1)} collective-permute-done((bf16[128,256]{1,0:T(8,128)(2,1)S(1)}, bf16[128,256]{1,0:T(8,128)(2,1)S(1)}, u32[]{:S(2)}, u32[]{:S(2)}) %collective-permute-start.20) | collective-permute-done | bytes 65568 | tf_op jit(solution)/shard_map/ppermute | solution.py:402
  62.9 1.4 %assemble.1 = bf16[512,512]{1,0:T(8,128)(2,1)} custom-call(s32[4]{0:T(128)S(1)} %pad_add_fusion.1.info, bf16[128,256]{1,0:T(8,128)(2,1)S(1)} %add_up.1.refs_0_, bf16[128,256]{1,0:T(8,128)(2,1)S(1)} %collective-permute-done.19.refs_1_, bf16[128,256]{1,0:T(8,128)(2,1)S(1)} %collective-permute-done.20.refs_2_, ...), custom_call_target="tpu_custom_call" | custom-call | flops 262144 | bytes 1048576 | tf_op jit(solution)/shard_map/assemble/pallas_call | solution.py:35
  (58 shorter events, 12.9 us)
Async XLA Ops:
  1.8 7.4 %collective-permute-start.2 = (bf16[256,512]{1,0:T(8,128)(2,1)S(1)}, bf16[256,512]{1,0:T(8,128)(2,1)S(1)}, u32[]{:S(2)}, u32[]{:S(2)}) collective-permute-start(bf16[256,512]{1,0:T(8,128)(2,1)S(1)} %get-tuple-element.57.refs_0_), channel_id=1, source_target_pairs={{0,8},{1,17},{2,10},{3,19},{4,12},{5,21},{6,14},{7,23},{8,0},{9,25... | collective-permute-start | bytes 786440 | tf_op jit(solution)/shard_map/ppermute | solution.py:422
  5.5 6.6 %collective-permute-start = (bf16[256,512]{1,0:T(8,128)(2,1)S(1)}, bf16[256,512]{1,0:T(8,128)(2,1)S(1)}, u32[]{:S(2)}, u32[]{:S(2)}) collective-permute-start(bf16[256,512]{1,0:T(8,128)(2,1)S(1)} %bitcast.11), channel_id=1, source_target_pairs={{0,1},{1,0},{2,3},{3,2},{4,5},{5,4},{6,7},{7,6},{8,9},{9,8},{10,11... | collective-permute-start | bytes 786440 | tf_op jit(solution)/shard_map/ppermute | solution.py:405
  6.0 8.7 %collective-permute-start.3 = (bf16[256,512]{1,0:T(8,128)(2,1)S(1)}, bf16[256,512]{1,0:T(8,128)(2,1)S(1)}, u32[]{:S(2)}, u32[]{:S(2)}) collective-permute-start(bf16[256,512]{1,0:T(8,128)(2,1)S(1)} %get-tuple-element.58.refs_1_), channel_id=1, source_target_pairs={{0,8},{1,17},{2,10},{3,19},{4,12},{5,21},{6,14},{7,23},{8,0},{9,25... | collective-permute-start | bytes 786440 | tf_op jit(solution)/shard_map/ppermute | solution.py:422
  9.1 6.4 %collective-permute-start.4 = (bf16[256,512]{1,0:T(8,128)(2,1)S(1)}, bf16[256,512]{1,0:T(8,128)(2,1)S(1)}, u32[]{:S(2)}, u32[]{:S(2)}) collective-permute-start(bf16[256,512]{1,0:T(8,128)(2,1)S(1)} %collective-permute-done.2.refs_2_), channel_id=1, source_target_pairs={{0,16},{1,9},{2,18},{3,11},{4,20},{5,13},{6,22},{7,15},{8,24},{9,1... | collective-permute-start | bytes 786440 | tf_op jit(solution)/shard_map/ppermute | solution.py:422
  14.7 2.0 %collective-permute-start.6 = (bf16[256,512]{1,0:T(8,128)(2,1)S(1)}, bf16[256,512]{1,0:T(8,128)(2,1)S(1)}, u32[]{:S(2)}, u32[]{:S(2)}) collective-permute-start(bf16[256,512]{1,0:T(8,128)(2,1)S(1)} %collective-permute-done.3.refs_0_), channel_id=1, source_target_pairs={{0,1},{1,0},{2,3},{3,2},{4,5},{5,4},{6,7},{7,6},{8,9},{9,8},{10,11... | collective-permute-start | bytes 786440 | tf_op jit(solution)/shard_map/ppermute | solution.py:405
  14.8 1.9 %collective-permute-start.5 = (bf16[256,512]{1,0:T(8,128)(2,1)S(1)}, bf16[256,512]{1,0:T(8,128)(2,1)S(1)}, u32[]{:S(2)}, u32[]{:S(2)}) collective-permute-start(bf16[256,512]{1,0:T(8,128)(2,1)S(1)} %collective-permute-done.2.refs_2_), channel_id=1, source_target_pairs={{0,1},{1,0},{2,3},{3,2},{4,5},{5,4},{6,7},{7,6},{8,9},{9,8},{10,11... | collective-permute-start | bytes 786440 | tf_op jit(solution)/shard_map/ppermute | solution.py:405
  15.5 1.5 %collective-permute-start.7 = (bf16[256,512]{1,0:T(8,128)(2,1)S(1)}, bf16[256,512]{1,0:T(8,128)(2,1)S(1)}, u32[]{:S(2)}, u32[]{:S(2)}) collective-permute-start(bf16[256,512]{1,0:T(8,128)(2,1)S(1)} %collective-permute-done.4.refs_1_), channel_id=1, source_target_pairs={{0,1},{1,0},{2,3},{3,2},{4,5},{5,4},{6,7},{7,6},{8,9},{9,8},{10,11... | collective-permute-start | bytes 786440 | tf_op jit(solution)/shard_map/ppermute | solution.py:405
  20.2 8.1 %collective-permute-start.10 = (bf16[64,256]{1,0:T(8,128)(2,1)S(1)}, bf16[64,256]{1,0:T(8,128)(2,1)S(1)}, u32[]{:S(2)}, u32[]{:S(2)}) collective-permute-start(bf16[64,256]{1,0:T(8,128)(2,1)S(1)} %get-tuple-element.86), channel_id=1, source_target_pairs={{0,6},{1,7},{2,4},{3,5},{4,2},{5,3},{6,0},{7,1},{8,14},{9,15},{10,... | collective-permute-start | bytes 98312 | tf_op jit(solution)/shard_map/ppermute | solution.py:402
  24.3 4.8 %collective-permute-start.9 = (bf16[64,256]{1,0:T(8,128)(2,1)S(1)}, bf16[64,256]{1,0:T(8,128)(2,1)S(1)}, u32[]{:S(2)}, u32[]{:S(2)}) collective-permute-start(bf16[64,256]{1,0:T(8,128)(2,1)S(1)} %get-tuple-element.86), channel_id=1, source_target_pairs={{0,4},{1,5},{2,6},{3,7},{4,0},{5,1},{6,2},{7,3},{8,12},{9,13},{10,... | collective-permute-start | bytes 98312 | tf_op jit(solution)/shard_map/ppermute | solution.py:402
  24.3 3.9 %collective-permute-start.8 = (bf16[64,256]{1,0:T(8,128)(2,1)S(1)}, bf16[64,256]{1,0:T(8,128)(2,1)S(1)}, u32[]{:S(2)}, u32[]{:S(2)}) collective-permute-start(bf16[64,256]{1,0:T(8,128)(2,1)S(1)} %get-tuple-element.85), channel_id=1, source_target_pairs={{0,2},{1,3},{2,0},{3,1},{4,6},{5,7},{6,4},{7,5},{8,10},{9,11},{10,... | collective-permute-start | bytes 98312 | tf_op jit(solution)/shard_map/ppermute | solution.py:402
  31.3 1.6 %collective-permute-start.11 = (bf16[2,256,256]{2,1,0:T(8,128)(2,1)S(1)}, bf16[2,256,256]{2,1,0:T(8,128)(2,1)S(1)}, u32[]{:S(2)}, u32[]{:S(2)}) collective-permute-start(bf16[2,256,256]{2,1,0:T(8,128)(2,1)S(1)} %get-tuple-element.88), channel_id=1, source_target_pairs={{0,1},{1,0},{2,3},{3,2},{4,5},{5,4},{6,7},{7,6},{8,9},{9,8},{10,11... | collective-permute-start | bytes 786440 | tf_op jit(solution)/shard_map/ppermute | solution.py:405
  33.8 6.3 %collective-permute-start.12 = (bf16[272,256]{1,0:T(8,128)(2,1)S(1)}, bf16[272,256]{1,0:T(8,128)(2,1)S(1)}, u32[]{:S(2)}, u32[]{:S(2)}) collective-permute-start(bf16[272,256]{1,0:T(8,128)(2,1)S(1)} %get-tuple-element.91), channel_id=1, source_target_pairs={{0,8},{8,0},{16,24},{24,16},{1,9},{9,1},{17,25},{25,17},{2,10},{10... | collective-permute-start | bytes 417800 | tf_op jit(solution)/shard_map/ppermute | solution.py:399
  35.3 8.4 %collective-permute-start.13 = (bf16[272,256]{1,0:T(8,128)(2,1)S(1)}, bf16[272,256]{1,0:T(8,128)(2,1)S(1)}, u32[]{:S(2)}, u32[]{:S(2)}) collective-permute-start(bf16[272,256]{1,0:T(8,128)(2,1)S(1)} %get-tuple-element.97), channel_id=1, source_target_pairs={{0,16},{8,24},{16,0},{24,8},{1,17},{9,25},{17,1},{25,9},{2,18},{10... | collective-permute-start | bytes 417800 | tf_op jit(solution)/shard_map/ppermute | solution.py:399
  36.9 6.9 %collective-permute-start.14 = (bf16[272,256]{1,0:T(8,128)(2,1)S(1)}, bf16[272,256]{1,0:T(8,128)(2,1)S(1)}, u32[]{:S(2)}, u32[]{:S(2)}) collective-permute-start(bf16[272,256]{1,0:T(8,128)(2,1)S(1)} %get-tuple-element.98), channel_id=1, source_target_pairs={{0,24},{8,16},{16,8},{24,0},{1,25},{9,17},{17,9},{25,1},{2,26},{10... | collective-permute-start | bytes 417800 | tf_op jit(solution)/shard_map/ppermute | solution.py:399
  42.4 8.6 %collective-permute-start.16 = (bf16[256,256]{1,0:T(8,128)(2,1)S(1)}, bf16[256,256]{1,0:T(8,128)(2,1)S(1)}, u32[]{:S(2)}, u32[]{:S(2)}) collective-permute-start(bf16[256,256]{1,0:T(8,128)(2,1)S(1)} %get-tuple-element.100), channel_id=1, source_target_pairs={{0,1},{1,0},{2,3},{3,2},{4,5},{5,4},{6,7},{7,6},{8,9},{9,8},{10,11... | collective-permute-start | bytes 393224 | tf_op jit(solution)/shard_map/ppermute | solution.py:405
  44.6 6.4 %collective-permute-start.15 = (bf16[128,256]{1,0:T(8,128)(2,1)S(1)}, bf16[128,256]{1,0:T(8,128)(2,1)S(1)}, u32[]{:S(2)}, u32[]{:S(2)}) collective-permute-start(bf16[128,256]{1,0:T(8,128)(2,1)S(1)} %get-tuple-element.99), channel_id=1, source_target_pairs={{0,6},{1,7},{2,4},{3,5},{4,2},{5,3},{6,0},{7,1},{8,14},{9,15},{10,... | collective-permute-start | bytes 196616 | tf_op jit(solution)/shard_map/ppermute | solution.py:402
  47.0 5.7 %collective-permute-start.17 = (bf16[128,256]{1,0:T(8,128)(2,1)S(1)}, bf16[128,256]{1,0:T(8,128)(2,1)S(1)}, u32[]{:S(2)}, u32[]{:S(2)}) collective-permute-start(bf16[128,256]{1,0:T(8,128)(2,1)S(1)} %get-tuple-element.102), channel_id=1, source_target_pairs={{0,2},{1,3},{2,0},{3,1},{4,6},{5,7},{6,4},{7,5},{8,10},{9,11},{10,... | collective-permute-start | bytes 196616 | tf_op jit(solution)/shard_map/ppermute | solution.py:402
  47.3 5.4 %collective-permute-start.18 = (bf16[128,256]{1,0:T(8,128)(2,1)S(1)}, bf16[128,256]{1,0:T(8,128)(2,1)S(1)}, u32[]{:S(2)}, u32[]{:S(2)}) collective-permute-start(bf16[128,256]{1,0:T(8,128)(2,1)S(1)} %get-tuple-element.103), channel_id=1, source_target_pairs={{0,4},{1,5},{2,6},{3,7},{4,0},{5,1},{6,2},{7,3},{8,12},{9,13},{10,... | collective-permute-start | bytes 196616 | tf_op jit(solution)/shard_map/ppermute | solution.py:402
  53.3 6.5 %collective-permute-start.21 = (bf16[128,256]{1,0:T(8,128)(2,1)S(1)}, bf16[128,256]{1,0:T(8,128)(2,1)S(1)}, u32[]{:S(2)}, u32[]{:S(2)}) collective-permute-start(bf16[128,256]{1,0:T(8,128)(2,1)S(1)} %add_up.1.refs_0_), channel_id=1, source_target_pairs={{0,6},{1,7},{2,4},{3,5},{4,2},{5,3},{6,0},{7,1},{8,14},{9,15},{10,... | collective-permute-start | bytes 196616 | tf_op jit(solution)/shard_map/ppermute | solution.py:402
  56.2 5.3 %collective-permute-start.20 = (bf16[128,256]{1,0:T(8,128)(2,1)S(1)}, bf16[128,256]{1,0:T(8,128)(2,1)S(1)}, u32[]{:S(2)}, u32[]{:S(2)}) collective-permute-start(bf16[128,256]{1,0:T(8,128)(2,1)S(1)} %add_up.1.refs_0_), channel_id=1, source_target_pairs={{0,4},{1,5},{2,6},{3,7},{4,0},{5,1},{6,2},{7,3},{8,12},{9,13},{10,... | collective-permute-start | bytes 196616 | tf_op jit(solution)/shard_map/ppermute | solution.py:402
  56.3 5.2 %collective-permute-start.19 = (bf16[128,256]{1,0:T(8,128)(2,1)S(1)}, bf16[128,256]{1,0:T(8,128)(2,1)S(1)}, u32[]{:S(2)}, u32[]{:S(2)}) collective-permute-start(bf16[128,256]{1,0:T(8,128)(2,1)S(1)} %add_up.1.refs_0_), channel_id=1, source_target_pairs={{0,2},{1,3},{2,0},{3,1},{4,6},{5,7},{6,4},{7,5},{8,10},{9,11},{10,... | collective-permute-start | bytes 196616 | tf_op jit(solution)/shard_map/ppermute | solution.py:402
  57.7 4.3 %collective-permute-start.22 = (bf16[128,256]{1,0:T(8,128)(2,1)S(1)}, bf16[128,256]{1,0:T(8,128)(2,1)S(1)}, u32[]{:S(2)}, u32[]{:S(2)}) collective-permute-start(bf16[128,256]{1,0:T(8,128)(2,1)S(1)} %add_up.1.refs_0_), channel_id=1, source_target_pairs={{0,1},{1,0},{2,3},{3,2},{4,5},{5,4},{6,7},{7,6},{8,9},{9,8},{10,11... | collective-permute-start | bytes 196616 | tf_op jit(solution)/shard_map/ppermute | solution.py:405
  59.8 2.2 %collective-permute-start.25 = (bf16[128,256]{1,0:T(8,128)(2,1)S(1)}, bf16[128,256]{1,0:T(8,128)(2,1)S(1)}, u32[]{:S(2)}, u32[]{:S(2)}) collective-permute-start(bf16[128,256]{1,0:T(8,128)(2,1)S(1)} %collective-permute-done.21.refs_3_), channel_id=1, source_target_pairs={{0,1},{1,0},{2,3},{3,2},{4,5},{5,4},{6,7},{7,6},{8,9},{9,8},{10,11... | collective-permute-start | bytes 196616 | tf_op jit(solution)/shard_map/ppermute | solution.py:405
  61.5 1.4 %collective-permute-start.23 = (bf16[128,256]{1,0:T(8,128)(2,1)S(1)}, bf16[128,256]{1,0:T(8,128)(2,1)S(1)}, u32[]{:S(2)}, u32[]{:S(2)}) collective-permute-start(bf16[128,256]{1,0:T(8,128)(2,1)S(1)} %collective-permute-done.19.refs_1_), channel_id=1, source_target_pairs={{0,1},{1,0},{2,3},{3,2},{4,5},{5,4},{6,7},{7,6},{8,9},{9,8},{10,11... | collective-permute-start | bytes 196616 | tf_op jit(solution)/shard_map/ppermute | solution.py:405
  (9 other events, 33.0 us)

commit v6 on v5

--- a/solution.py
+++ b/solution.py
@@ -84,11 +84,23 @@
         yield ref, owner * rows + jnp.where(core == 0, sides[0], sides[1]) * (rows // 2)
 
 
-def chosen_rows(x, column, blocks):
+def chosen_rows(column, blocks):
+    hits = []
     for ref, base in blocks:
         hit = column - base == iota((column.shape[0], ref.shape[0]), 1)
-        x = x + dot(jnp.where(hit, 1.0, 0.0).astype(BF16), ref[...])
-    return x
+        hits.append(jnp.where(hit, 1.0, 0.0).astype(BF16))
+    return dot(jnp.concatenate(hits, 1), jnp.concatenate([ref[...] for ref, _ in blocks], 0))
+
+
+def both(ref):
+    return jnp.concatenate([ref[0], ref[1]], 0)
+
+
+def valid_both(info, length):
+    core, z = info[1], info[2]
+    return jnp.concatenate(
+        [valid_col(info, (2 * z + side) * length, length) for side in (core, 1 - core)], 0
+    )
 
 
 def prepare(
@@ -115,7 +127,7 @@
         slot = jnp.sum(same, axis=0, keepdims=True).astype(jnp.int32)
         where_to = (owner_row ^ mine) * cap + slot
         dest[j : j + 1, :] = where_to
-        x = chosen_rows(jnp.zeros((length, emb.shape[2]), F32), column, blocks)
+        x = chosen_rows(column, blocks)
         emb[j] = x.astype(BF16)
         high = local_row // 32
         line = iota((16, length), 0) - 2 * j
@@ -161,38 +173,35 @@
     blocks = list(held_rows(where_from, parts, info, rows))
     same_head = same_heads(half, size)
     mean_of = jnp.where(same_head, 1.0 / size, 0.0).astype(BF16)
+    x = both(emb_own).astype(F32) + chosen_rows(both(ids_col), blocks)
+    rstd = lax.rsqrt(jnp.mean(x * x, axis=1, keepdims=True) + EPS)
+    normed = (x * rstd * gain[...]).astype(BF16)
+    valid = valid_both(info, length)
+    qr = dot(normed, w_q[:, mine_at])
+    kr = dot(normed, w_k[:, mine_at])
+    v = dot(normed, w_v[:, mine_at]) * valid
+    q_rms = lax.rsqrt(dot((qr * qr).astype(BF16), mean_of) + EPS)
+    k_rms = lax.rsqrt(dot((kr * kr).astype(BF16), mean_of) + EPS)
+    qn = qr * q_rms
+    kn = kr * k_rms * valid
+    up = both(rising)
+    qa = (qn * both(falling) / size).astype(BF16)
+    kb = (kn * up / math.sqrt(size)).astype(BF16)
+    vb = (v * up).astype(BF16)
+    v = v.astype(BF16)
+    qs, ks = q_rms / size, k_rms * (valid / math.sqrt(size))
     totals = [0.0, 0.0]
     for j in range(2):
-        side = core if j == 0 else 1 - core
-        column = ids_col[j]
-        x = chosen_rows(emb_own[j].astype(F32), column, blocks)
-        emb[j] = x.astype(BF16)
-        rstd = lax.rsqrt(jnp.mean(x * x, axis=1, keepdims=True) + EPS)
-        rstd_out[j] = rstd
-        normed = (x * rstd * gain[...]).astype(BF16)
-        valid = valid_col(info, (2 * z + side) * length, length)
-        qr = dot(normed, w_q[:, mine_at])
-        kr = dot(normed, w_k[:, mine_at])
-        v = dot(normed, w_v[:, mine_at]) * valid
-        q_rms = lax.rsqrt(dot((qr * qr).astype(BF16), mean_of) + EPS)
-        k_rms = lax.rsqrt(dot((kr * kr).astype(BF16), mean_of) + EPS)
-        qn = qr * q_rms
-        kn = kr * k_rms * valid
-        qa = (qn * falling[j] / size).astype(BF16)
-        kb = (kn * rising[j] / math.sqrt(size)).astype(BF16)
-        vb_out[j] = (v * rising[j]).astype(BF16)
-        v = v.astype(BF16)
-        v_out[j] = v
-        qa_out[j] = qa
-        kb_out[j] = kb
-        qn_out[j] = qn.astype(BF16)
-        kn_out[j] = kn.astype(BF16)
-        qs_out[j] = q_rms / size
-        ks_out[j] = k_rms * (valid / math.sqrt(size))
-        for n, full in enumerate((dot_tn(kb, v), dot_tn(qa, g[j]))):
+        at = slice(j * length, (j + 1) * length)
+        for n, full in enumerate((dot_tn(kb[at], v[at]), dot_tn(qa[at], g[j]))):
             full = jnp.where(same_head, full, 0.0)
             states[n, j] = full.astype(BF16)
             totals[n] = totals[n] + full
+        for out, value in (
+            (emb, x), (rstd_out, rstd), (v_out, v), (qa_out, qa), (kb_out, kb), (vb_out, vb),
+            (qn_out, qn), (kn_out, kn), (qs_out, qs), (ks_out, ks),
+        ):
+            out[j] = value[at].astype(out.dtype)
 
     def packed(full):
         return sum(full[h * size : (h + 1) * size, :] for h in range(half // size))
@@ -278,12 +287,8 @@
         total = jnp.zeros((length, 1), F32)
         for at in (keep_at, send_at):
             rows = pl.ds(at, half)
-            d_normed = (
-                dot_nt(d_q, w_q[rows, mine_at])
-                + dot_nt(d_k, w_k[rows, mine_at])
-                + dot_nt(d_v, w_v[rows, mine_at])
-            )
-            d_normed = d_normed * gain[:, rows]
+            weights = jnp.concatenate([w[rows, mine_at] for w in (w_q, w_k, w_v)], 1)
+            d_normed = dot_nt(jnp.concatenate([d_q, d_k, d_v], 1), weights) * gain[:, rows]
             part = emb[j, :, rows].astype(F32)
             scaled.append((d_normed, part))
             total = total + jnp.sum(d_normed * part, axis=1, keepdims=True)

time: 64.5 us -> 64 us (level)
  transfers between devices with their start and end apart: 26 -> 26, of which waited for: 15 -> 15; matrix products, arithmetic and copies ran while one was open for 1% -> 1% of each run, Pallas kernels for 14% -> 15%
where the time goes in v6:
time: 64 us; the launch traced here: 63.8 us
  starting transfers between devices  24.7 us (39%)
  Pallas kernels  18 us (28%)
  waiting for transfers between devices  18 us (28%)
  between operations  1.49 us (2%)
  local copies, waits for them, and re-layouts  0.82 us (1%)
  other arithmetic  0.78 us (1%)
    pallas_call x11, Pallas kernels, call(): pl.pallas_call(body, in_specs=[pl.BlockSpec(memory_space=pltpu.SMEM)] + [...  16.9 us
    ppermute x9, starting transfers between devices, over_z(): return lax.ppermute(x, 'ctx', [(i, i ^ 2 * m) for i in range(count)])  13.7 us
    ppermute x9, waiting for transfers between devices, over_z(): return lax.ppermute(x, 'ctx', [(i, i ^ 2 * m) for i in range(count)])  7.32 us
    ppermute x3, starting transfers between devices, from_mask(): lax.ppermute(x, ('table', 'ctx'), [(t * count + c, (t ^ masks[c % 2]) * c...  5.69 us
    ppermute x3, waiting for transfers between devices, over_table(): return lax.ppermute(x, 'table', [(i, i ^ m) for i in range(tables)])  3.98 us
    ppermute x11, waiting for transfers between devices, swap(): return lax.ppermute(x, 'ctx', [(i, i ^ 1) for i in range(count)])  3.96 us
    ppermute x3, starting transfers between devices, over_table(): return lax.ppermute(x, 'table', [(i, i ^ m) for i in range(tables)])  3.55 us
    ppermute x3, waiting for transfers between devices, from_mask(): lax.ppermute(x, ('table', 'ctx'), [(t * count + c, (t ^ masks[c % 2]) * c...  2.78 us
  transfers between devices with their start and end apart: 26, of which 15 were waited for; matrix products, arithmetic and copies ran while one was open for 1% of the time, Pallas kernels for 15%

profile of v6, /device:TPU:0, one launch (start us, length us, event | category | flops | bytes accessed | tf_op | source)
XLA Modules:
  0.0 63.8 jit_solution(14727398124919498268)
XLA Ops:
  0.7 1.1 %pick.1 = (bf16[256,512]{1,0:T(8,128)(2,1)S(1)}, bf16[256,512]{1,0:T(8,128)(2,1)S(1)}) custom-call(bf16[512,512]{1,0:T(8,128)(2,1)} %table.1), custom_call_target="tpu_custom_call" | custom-call | tf_op jit(solution)/shard_map/pick/pallas_call | solution.py:417
  1.8 3.0 %collective-permute-start.2 = (bf16[256,512]{1,0:T(8,128)(2,1)S(1)}, bf16[256,512]{1,0:T(8,128)(2,1)S(1)}, u32[]{:S(2)}, u32[]{:S(2)}) collective-permute-start(bf16[256,512]{1,0:T(8,128)(2,1)S(1)} %get-tuple-element.57.refs_0_), channel_id=1, source_target_pairs={{0,8},{1,17},{2,10},{3,19},{4,12},{5,21},{6,14},{7,23},{8,0},{9,25... | collective-permute-start | bytes 786440 | tf_op jit(solution)/shard_map/ppermute | solution.py:427
  6.6 2.5 %collective-permute-done.2.refs_2_ = bf16[256,512]{1,0:T(8,128)(2,1)S(1)} collective-permute-done((bf16[256,512]{1,0:T(8,128)(2,1)S(1)}, bf16[256,512]{1,0:T(8,128)(2,1)S(1)}, u32[]{:S(2)}, u32[]{:S(2)}) %collective-permute-start.2) | collective-permute-done | bytes 262176 | tf_op jit(solution)/shard_map/ppermute | solution.py:427
  9.1 2.0 %collective-permute-start.4 = (bf16[256,512]{1,0:T(8,128)(2,1)S(1)}, bf16[256,512]{1,0:T(8,128)(2,1)S(1)}, u32[]{:S(2)}, u32[]{:S(2)}) collective-permute-start(bf16[256,512]{1,0:T(8,128)(2,1)S(1)} %collective-permute-done.2.refs_2_), channel_id=1, source_target_pairs={{0,16},{1,9},{2,18},{3,11},{4,20},{5,13},{6,22},{7,15},{8,24},{9,1... | collective-permute-start | bytes 786440 | tf_op jit(solution)/shard_map/ppermute | solution.py:427
  12.8 1.9 %prepare.1 = (bf16[2,256,256]{2,1,0:T(8,128)(2,1)S(1)}, bf16[2,256,256]{2,1,0:T(8,128)(2,1)S(1)}, s32[2,256]{1,0:T(2,128)S(1)}, bf16[4,16,128]{2,1,0:T(8,128)(2,...) custom-call(s32[4]{0:T(128)S(1)} %pad_add_fusion.1.info, ...), custom_call_target="tpu_custom_call" | custom-call | flops 134217728 | bytes 3957760 | tf_op jit(solution)/shard_map/prepare/pallas_call | solution.py:35
  17.1 2.6 %project.1 = (bf16[2,256,512]{2,1,0:T(8,128)(2,1)S(1)}, bf16[2,256,256]{2,1,0:T(8,128)(2,1)S(1)}, bf16[2,256,256]{2,1,0:T(8,128)(2,1)S(1)}, bf16[2,256,256]{2,1,...) custom-call(s32[4]{0:T(128)S(1)} %pad_add_fusion.1.info, ...), custom_call_target="tpu_custom_call" | custom-call | flops 1073741824 | bytes 8460288 | tf_op jit(solution)/shard_map/project/pallas_call | solution.py:35
  19.7 4.2 %collective-permute-start.10 = (bf16[64,256]{1,0:T(8,128)(2,1)S(1)}, bf16[64,256]{1,0:T(8,128)(2,1)S(1)}, u32[]{:S(2)}, u32[]{:S(2)}) collective-permute-start(bf16[64,256]{1,0:T(8,128)(2,1)S(1)} %get-tuple-element.86), channel_id=1, source_target_pairs={{0,6},{1,7},{2,4},{3,5},{4,2},{5,3},{6,0},{7,1},{8,14},{9,15},{10,... | collective-permute-start | bytes 98312 | tf_op jit(solution)/shard_map/ppermute | solution.py:407
  24.5 2.7 %attend.1 = (bf16[2,256,256]{2,1,0:T(8,128)(2,1)S(1)}, bf16[2,256,256]{2,1,0:T(8,128)(2,1)S(1)}, bf16[2,256,256]{2,1,0:T(8,128)(2,1)S(1)}) custom-call(s32[4]{0:T(128)S(1)} %pad_add_fusion.1.info, bf16[2,256,256]{2,1,0:T(8,128)(2,1)S(1)} %get-tuple-element.77.qa_in, bf16[2,256,256]{2,1,0:T(8,128)(2,1)S(1)} %get-tuple-element.69.kb_in.kb, ...), custom_call_target="tpu_custom_call" | custom-call | flops 402653184 | bytes 2883584 | tf_op jit(solution)/shard_map/attend/pallas_call | solution.py:35
  28.7 2.1 %finish.1 = (bf16[256,256]{1,0:T(8,128)(2,1)S(1)}, f32[2,256,256]{2,1,0:T(8,128)S(1)}, bf16[2,256,256]{2,1,0:T(8,128)(2,1)S(1)}) custom-call(s32[4]{0:T(128)S(1)} %pad_add_fusion.1.info, f32[1,256]{1,0:T(1,128)S(1)} %get-tuple-element.59.rate, bf16[2,256,256]{2,1,0:T(8,128)(2,1)S(1)} %get-tuple-element.69.kb_in.kb, ...), custom_call_target="tpu_custom_call" | custom-call | flops 402653184 | bytes 6788096 | tf_op jit(solution)/shard_map/finish/pallas_call | solution.py:35
  30.9 1.5 %collective-permute-done.11.row_came = bf16[2,256,256]{2,1,0:T(8,128)(2,1)S(1)} collective-permute-done((bf16[2,256,256]{2,1,0:T(8,128)(2,1)S(1)}, bf16[2,256,256]{2,1,0:T(8,128)(2,1)S(1)}, u32[]{:S(2)}, u32[]{:S(2)}) %collective-permute-start.11) | collective-permute-done | bytes 262176 | tf_op jit(solution)/shard_map/ppermute | solution.py:410
  33.3 1.6 %collective-permute-start.12 = (bf16[272,256]{1,0:T(8,128)(2,1)S(1)}, bf16[272,256]{1,0:T(8,128)(2,1)S(1)}, u32[]{:S(2)}, u32[]{:S(2)}) collective-permute-start(bf16[272,256]{1,0:T(8,128)(2,1)S(1)} %get-tuple-element.91), channel_id=1, source_target_pairs={{0,8},{8,0},{16,24},{24,16},{1,9},{9,1},{17,25},{25,17},{2,10},{10... | collective-permute-start | bytes 417800 | tf_op jit(solution)/shard_map/ppermute | solution.py:404
  34.9 1.5 %collective-permute-start.13 = (bf16[272,256]{1,0:T(8,128)(2,1)S(1)}, bf16[272,256]{1,0:T(8,128)(2,1)S(1)}, u32[]{:S(2)}, u32[]{:S(2)}) collective-permute-start(bf16[272,256]{1,0:T(8,128)(2,1)S(1)} %get-tuple-element.97), channel_id=1, source_target_pairs={{0,16},{8,24},{16,0},{24,8},{1,17},{9,25},{17,1},{25,9},{2,18},{10... | collective-permute-start | bytes 417800 | tf_op jit(solution)/shard_map/ppermute | solution.py:404
  36.9 2.7 %collective-permute-done.12.refs_1_ = bf16[272,256]{1,0:T(8,128)(2,1)S(1)} collective-permute-done((bf16[272,256]{1,0:T(8,128)(2,1)S(1)}, bf16[272,256]{1,0:T(8,128)(2,1)S(1)}, u32[]{:S(2)}, u32[]{:S(2)}) %collective-permute-start.12) | collective-permute-done | bytes 139296 | tf_op jit(solution)/shard_map/ppermute | solution.py:404
  39.6 1.5 %outward.1 = (bf16[256,256]{1,0:T(8,128)(2,1)S(1)}, bf16[256,256]{1,0:T(8,128)(2,1)S(1)}) custom-call(s32[4]{0:T(128)S(1)} %pad_add_fusion.1.info, bf16[2,256,256]{2,1,0:T(8,128)(2,1)S(1)} %get-tuple-element.77.qa_in, bf16[2,256,256]{2,1,0:T(8,128)(2,1)S(1)} %get-tuple-element.69.kb_in.kb, bf16[2,256,256]{2,1,0:T(8,128)(2,1)S(1)} %get-tuple-element.78.v_in, ...), custom_call_target="tpu_custom_call" | custom-call | flops 134217728 | bytes 1703936 | tf_op jit(solution)/shard_map/outward/pallas_call | solution.py:35
  42.0 1.2 %collective-permute-done.13.refs_0_ = bf16[272,256]{1,0:T(8,128)(2,1)S(1)} collective-permute-done((bf16[272,256]{1,0:T(8,128)(2,1)S(1)}, bf16[272,256]{1,0:T(8,128)(2,1)S(1)}, u32[]{:S(2)}, u32[]{:S(2)}) %collective-permute-start.13) | collective-permute-done | bytes 139296 | tf_op jit(solution)/shard_map/ppermute | solution.py:404
  44.2 2.4 %collective-permute-start.15 = (bf16[128,256]{1,0:T(8,128)(2,1)S(1)}, bf16[128,256]{1,0:T(8,128)(2,1)S(1)}, u32[]{:S(2)}, u32[]{:S(2)}) collective-permute-start(bf16[128,256]{1,0:T(8,128)(2,1)S(1)} %get-tuple-element.99), channel_id=1, source_target_pairs={{0,6},{1,7},{2,4},{3,5},{4,2},{5,3},{6,0},{7,1},{8,14},{9,15},{10,... | collective-permute-start | bytes 196616 | tf_op jit(solution)/shard_map/ppermute | solution.py:407
  46.8 1.8 %collective-permute-start.18 = (bf16[128,256]{1,0:T(8,128)(2,1)S(1)}, bf16[128,256]{1,0:T(8,128)(2,1)S(1)}, u32[]{:S(2)}, u32[]{:S(2)}) collective-permute-start(bf16[128,256]{1,0:T(8,128)(2,1)S(1)} %get-tuple-element.103), channel_id=1, source_target_pairs={{0,4},{1,5},{2,6},{3,7},{4,0},{5,1},{6,2},{7,3},{8,12},{9,13},{10,... | collective-permute-start | bytes 196616 | tf_op jit(solution)/shard_map/ppermute | solution.py:407
  48.6 1.9 %collective-permute-done.15.refs_1_ = bf16[128,256]{1,0:T(8,128)(2,1)S(1)} collective-permute-done((bf16[128,256]{1,0:T(8,128)(2,1)S(1)}, bf16[128,256]{1,0:T(8,128)(2,1)S(1)}, u32[]{:S(2)}, u32[]{:S(2)}) %collective-permute-start.15) | collective-permute-done | bytes 65568 | tf_op jit(solution)/shard_map/ppermute | solution.py:407
  50.5 1.6 %result.1 = bf16[256,512]{1,0:T(8,128)(2,1)} custom-call(s32[4]{0:T(128)S(1)} %pad_add_fusion.1.info, bf16[2,256,512]{2,1,0:T(8,128)(2,1)S(1)} %get-tuple-element.83.emb, bf16[256,256]{1,0:T(8,128)(2,1)S(1)} %get-tuple-element.104.att_own, bf16[256,256]{1,0:T(8,128)(2,1)S(1)} %collective-permute-done.16.att_came, bf16[512,512]{1,0:T(8,128)(2,1)S(1)} %get-tuple-element.106.w_out), custom_call_target="tpu_custom_call" | custom-call | flops 134217728 | bytes 1572864 | tf_op jit(solution)/shard_map/result/pallas_call | solution.py:35
  52.8 3.0 %collective-permute-start.21 = (bf16[128,256]{1,0:T(8,128)(2,1)S(1)}, bf16[128,256]{1,0:T(8,128)(2,1)S(1)}, u32[]{:S(2)}, u32[]{:S(2)}) collective-permute-start(bf16[128,256]{1,0:T(8,128)(2,1)S(1)} %add_up.1.refs_0_), channel_id=1, source_target_pairs={{0,6},{1,7},{2,4},{3,5},{4,2},{5,3},{6,0},{7,1},{8,14},{9,15},{10,... | collective-permute-start | bytes 196616 | tf_op jit(solution)/shard_map/ppermute | solution.py:407
  55.8 1.4 %collective-permute-start.19 = (bf16[128,256]{1,0:T(8,128)(2,1)S(1)}, bf16[128,256]{1,0:T(8,128)(2,1)S(1)}, u32[]{:S(2)}, u32[]{:S(2)}) collective-permute-start(bf16[128,256]{1,0:T(8,128)(2,1)S(1)} %add_up.1.refs_0_), channel_id=1, source_target_pairs={{0,2},{1,3},{2,0},{3,1},{4,6},{5,7},{6,4},{7,5},{8,10},{9,11},{10,... | collective-permute-start | bytes 196616 | tf_op jit(solution)/shard_map/ppermute | solution.py:407
  57.2 2.0 %collective-permute-done.21.refs_3_ = bf16[128,256]{1,0:T(8,128)(2,1)S(1)} collective-permute-done((bf16[128,256]{1,0:T(8,128)(2,1)S(1)}, bf16[128,256]{1,0:T(8,128)(2,1)S(1)}, u32[]{:S(2)}, u32[]{:S(2)}) %collective-permute-start.21) | collective-permute-done | bytes 65568 | tf_op jit(solution)/shard_map/ppermute | solution.py:407
  59.3 1.7 %collective-permute-done.20.refs_2_ = bf16[128,256]{1,0:T(8,128)(2,1)S(1)} collective-permute-done((bf16[128,256]{1,0:T(8,128)(2,1)S(1)}, bf16[128,256]{1,0:T(8,128)(2,1)S(1)}, u32[]{:S(2)}, u32[]{:S(2)}) %collective-permute-start.20) | collective-permute-done | bytes 65568 | tf_op jit(solution)/shard_map/ppermute | solution.py:407
  62.4 1.4 %assemble.1 = bf16[512,512]{1,0:T(8,128)(2,1)} custom-call(s32[4]{0:T(128)S(1)} %pad_add_fusion.1.info, bf16[128,256]{1,0:T(8,128)(2,1)S(1)} %add_up.1.refs_0_, bf16[128,256]{1,0:T(8,128)(2,1)S(1)} %collective-permute-done.19.refs_1_, bf16[128,256]{1,0:T(8,128)(2,1)S(1)} %collective-permute-done.20.refs_2_, ...), custom_call_target="tpu_custom_call" | custom-call | flops 262144 | bytes 1048576 | tf_op jit(solution)/shard_map/assemble/pallas_call | solution.py:35
  (58 shorter events, 12.9 us)
Async XLA Ops:
  1.8 7.4 %collective-permute-start.2 = (bf16[256,512]{1,0:T(8,128)(2,1)S(1)}, bf16[256,512]{1,0:T(8,128)(2,1)S(1)}, u32[]{:S(2)}, u32[]{:S(2)}) collective-permute-start(bf16[256,512]{1,0:T(8,128)(2,1)S(1)} %get-tuple-element.57.refs_0_), channel_id=1, source_target_pairs={{0,8},{1,17},{2,10},{3,19},{4,12},{5,21},{6,14},{7,23},{8,0},{9,25... | collective-permute-start | bytes 786440 | tf_op jit(solution)/shard_map/ppermute | solution.py:427
  5.5 6.6 %collective-permute-start = (bf16[256,512]{1,0:T(8,128)(2,1)S(1)}, bf16[256,512]{1,0:T(8,128)(2,1)S(1)}, u32[]{:S(2)}, u32[]{:S(2)}) collective-permute-start(bf16[256,512]{1,0:T(8,128)(2,1)S(1)} %bitcast.11), channel_id=1, source_target_pairs={{0,1},{1,0},{2,3},{3,2},{4,5},{5,4},{6,7},{7,6},{8,9},{9,8},{10,11... | collective-permute-start | bytes 786440 | tf_op jit(solution)/shard_map/ppermute | solution.py:410
  6.0 8.7 %collective-permute-start.3 = (bf16[256,512]{1,0:T(8,128)(2,1)S(1)}, bf16[256,512]{1,0:T(8,128)(2,1)S(1)}, u32[]{:S(2)}, u32[]{:S(2)}) collective-permute-start(bf16[256,512]{1,0:T(8,128)(2,1)S(1)} %get-tuple-element.58.refs_1_), channel_id=1, source_target_pairs={{0,8},{1,17},{2,10},{3,19},{4,12},{5,21},{6,14},{7,23},{8,0},{9,25... | collective-permute-start | bytes 786440 | tf_op jit(solution)/shard_map/ppermute | solution.py:427
  9.1 6.4 %collective-permute-start.4 = (bf16[256,512]{1,0:T(8,128)(2,1)S(1)}, bf16[256,512]{1,0:T(8,128)(2,1)S(1)}, u32[]{:S(2)}, u32[]{:S(2)}) collective-permute-start(bf16[256,512]{1,0:T(8,128)(2,1)S(1)} %collective-permute-done.2.refs_2_), channel_id=1, source_target_pairs={{0,16},{1,9},{2,18},{3,11},{4,20},{5,13},{6,22},{7,15},{8,24},{9,1... | collective-permute-start | bytes 786440 | tf_op jit(solution)/shard_map/ppermute | solution.py:427
  14.7 2.0 %collective-permute-start.6 = (bf16[256,512]{1,0:T(8,128)(2,1)S(1)}, bf16[256,512]{1,0:T(8,128)(2,1)S(1)}, u32[]{:S(2)}, u32[]{:S(2)}) collective-permute-start(bf16[256,512]{1,0:T(8,128)(2,1)S(1)} %collective-permute-done.3.refs_0_), channel_id=1, source_target_pairs={{0,1},{1,0},{2,3},{3,2},{4,5},{5,4},{6,7},{7,6},{8,9},{9,8},{10,11... | collective-permute-start | bytes 786440 | tf_op jit(solution)/shard_map/ppermute | solution.py:410
  14.8 1.9 %collective-permute-start.5 = (bf16[256,512]{1,0:T(8,128)(2,1)S(1)}, bf16[256,512]{1,0:T(8,128)(2,1)S(1)}, u32[]{:S(2)}, u32[]{:S(2)}) collective-permute-start(bf16[256,512]{1,0:T(8,128)(2,1)S(1)} %collective-permute-done.2.refs_2_), channel_id=1, source_target_pairs={{0,1},{1,0},{2,3},{3,2},{4,5},{5,4},{6,7},{7,6},{8,9},{9,8},{10,11... | collective-permute-start | bytes 786440 | tf_op jit(solution)/shard_map/ppermute | solution.py:410
  15.5 1.5 %collective-permute-start.7 = (bf16[256,512]{1,0:T(8,128)(2,1)S(1)}, bf16[256,512]{1,0:T(8,128)(2,1)S(1)}, u32[]{:S(2)}, u32[]{:S(2)}) collective-permute-start(bf16[256,512]{1,0:T(8,128)(2,1)S(1)} %collective-permute-done.4.refs_1_), channel_id=1, source_target_pairs={{0,1},{1,0},{2,3},{3,2},{4,5},{5,4},{6,7},{7,6},{8,9},{9,8},{10,11... | collective-permute-start | bytes 786440 | tf_op jit(solution)/shard_map/ppermute | solution.py:410
  19.7 8.1 %collective-permute-start.10 = (bf16[64,256]{1,0:T(8,128)(2,1)S(1)}, bf16[64,256]{1,0:T(8,128)(2,1)S(1)}, u32[]{:S(2)}, u32[]{:S(2)}) collective-permute-start(bf16[64,256]{1,0:T(8,128)(2,1)S(1)} %get-tuple-element.86), channel_id=1, source_target_pairs={{0,6},{1,7},{2,4},{3,5},{4,2},{5,3},{6,0},{7,1},{8,14},{9,15},{10,... | collective-permute-start | bytes 98312 | tf_op jit(solution)/shard_map/ppermute | solution.py:407
  23.9 4.8 %collective-permute-start.9 = (bf16[64,256]{1,0:T(8,128)(2,1)S(1)}, bf16[64,256]{1,0:T(8,128)(2,1)S(1)}, u32[]{:S(2)}, u32[]{:S(2)}) collective-permute-start(bf16[64,256]{1,0:T(8,128)(2,1)S(1)} %get-tuple-element.86), channel_id=1, source_target_pairs={{0,4},{1,5},{2,6},{3,7},{4,0},{5,1},{6,2},{7,3},{8,12},{9,13},{10,... | collective-permute-start | bytes 98312 | tf_op jit(solution)/shard_map/ppermute | solution.py:407
  23.9 3.9 %collective-permute-start.8 = (bf16[64,256]{1,0:T(8,128)(2,1)S(1)}, bf16[64,256]{1,0:T(8,128)(2,1)S(1)}, u32[]{:S(2)}, u32[]{:S(2)}) collective-permute-start(bf16[64,256]{1,0:T(8,128)(2,1)S(1)} %get-tuple-element.85), channel_id=1, source_target_pairs={{0,2},{1,3},{2,0},{3,1},{4,6},{5,7},{6,4},{7,5},{8,10},{9,11},{10,... | collective-permute-start | bytes 98312 | tf_op jit(solution)/shard_map/ppermute | solution.py:407
  30.8 1.6 %collective-permute-start.11 = (bf16[2,256,256]{2,1,0:T(8,128)(2,1)S(1)}, bf16[2,256,256]{2,1,0:T(8,128)(2,1)S(1)}, u32[]{:S(2)}, u32[]{:S(2)}) collective-permute-start(bf16[2,256,256]{2,1,0:T(8,128)(2,1)S(1)} %get-tuple-element.88), channel_id=1, source_target_pairs={{0,1},{1,0},{2,3},{3,2},{4,5},{5,4},{6,7},{7,6},{8,9},{9,8},{10,11... | collective-permute-start | bytes 786440 | tf_op jit(solution)/shard_map/ppermute | solution.py:410
  33.3 6.3 %collective-permute-start.12 = (bf16[272,256]{1,0:T(8,128)(2,1)S(1)}, bf16[272,256]{1,0:T(8,128)(2,1)S(1)}, u32[]{:S(2)}, u32[]{:S(2)}) collective-permute-start(bf16[272,256]{1,0:T(8,128)(2,1)S(1)} %get-tuple-element.91), channel_id=1, source_target_pairs={{0,8},{8,0},{16,24},{24,16},{1,9},{9,1},{17,25},{25,17},{2,10},{10... | collective-permute-start | bytes 417800 | tf_op jit(solution)/shard_map/ppermute | solution.py:404
  34.9 8.4 %collective-permute-start.13 = (bf16[272,256]{1,0:T(8,128)(2,1)S(1)}, bf16[272,256]{1,0:T(8,128)(2,1)S(1)}, u32[]{:S(2)}, u32[]{:S(2)}) collective-permute-start(bf16[272,256]{1,0:T(8,128)(2,1)S(1)} %get-tuple-element.97), channel_id=1, source_target_pairs={{0,16},{8,24},{16,0},{24,8},{1,17},{9,25},{17,1},{25,9},{2,18},{10... | collective-permute-start | bytes 417800 | tf_op jit(solution)/shard_map/ppermute | solution.py:404
  36.4 6.9 %collective-permute-start.14 = (bf16[272,256]{1,0:T(8,128)(2,1)S(1)}, bf16[272,256]{1,0:T(8,128)(2,1)S(1)}, u32[]{:S(2)}, u32[]{:S(2)}) collective-permute-start(bf16[272,256]{1,0:T(8,128)(2,1)S(1)} %get-tuple-element.98), channel_id=1, source_target_pairs={{0,24},{8,16},{16,8},{24,0},{1,25},{9,17},{17,9},{25,1},{2,26},{10... | collective-permute-start | bytes 417800 | tf_op jit(solution)/shard_map/ppermute | solution.py:404
  42.0 8.6 %collective-permute-start.16 = (bf16[256,256]{1,0:T(8,128)(2,1)S(1)}, bf16[256,256]{1,0:T(8,128)(2,1)S(1)}, u32[]{:S(2)}, u32[]{:S(2)}) collective-permute-start(bf16[256,256]{1,0:T(8,128)(2,1)S(1)} %get-tuple-element.100), channel_id=1, source_target_pairs={{0,1},{1,0},{2,3},{3,2},{4,5},{5,4},{6,7},{7,6},{8,9},{9,8},{10,11... | collective-permute-start | bytes 393224 | tf_op jit(solution)/shard_map/ppermute | solution.py:410
  44.2 6.4 %collective-permute-start.15 = (bf16[128,256]{1,0:T(8,128)(2,1)S(1)}, bf16[128,256]{1,0:T(8,128)(2,1)S(1)}, u32[]{:S(2)}, u32[]{:S(2)}) collective-permute-start(bf16[128,256]{1,0:T(8,128)(2,1)S(1)} %get-tuple-element.99), channel_id=1, source_target_pairs={{0,6},{1,7},{2,4},{3,5},{4,2},{5,3},{6,0},{7,1},{8,14},{9,15},{10,... | collective-permute-start | bytes 196616 | tf_op jit(solution)/shard_map/ppermute | solution.py:407
  46.5 5.7 %collective-permute-start.17 = (bf16[128,256]{1,0:T(8,128)(2,1)S(1)}, bf16[128,256]{1,0:T(8,128)(2,1)S(1)}, u32[]{:S(2)}, u32[]{:S(2)}) collective-permute-start(bf16[128,256]{1,0:T(8,128)(2,1)S(1)} %get-tuple-element.102), channel_id=1, source_target_pairs={{0,2},{1,3},{2,0},{3,1},{4,6},{5,7},{6,4},{7,5},{8,10},{9,11},{10,... | collective-permute-start | bytes 196616 | tf_op jit(solution)/shard_map/ppermute | solution.py:407
  46.8 5.4 %collective-permute-start.18 = (bf16[128,256]{1,0:T(8,128)(2,1)S(1)}, bf16[128,256]{1,0:T(8,128)(2,1)S(1)}, u32[]{:S(2)}, u32[]{:S(2)}) collective-permute-start(bf16[128,256]{1,0:T(8,128)(2,1)S(1)} %get-tuple-element.103), channel_id=1, source_target_pairs={{0,4},{1,5},{2,6},{3,7},{4,0},{5,1},{6,2},{7,3},{8,12},{9,13},{10,... | collective-permute-start | bytes 196616 | tf_op jit(solution)/shard_map/ppermute | solution.py:407
  52.8 6.5 %collective-permute-start.21 = (bf16[128,256]{1,0:T(8,128)(2,1)S(1)}, bf16[128,256]{1,0:T(8,128)(2,1)S(1)}, u32[]{:S(2)}, u32[]{:S(2)}) collective-permute-start(bf16[128,256]{1,0:T(8,128)(2,1)S(1)} %add_up.1.refs_0_), channel_id=1, source_target_pairs={{0,6},{1,7},{2,4},{3,5},{4,2},{5,3},{6,0},{7,1},{8,14},{9,15},{10,... | collective-permute-start | bytes 196616 | tf_op jit(solution)/shard_map/ppermute | solution.py:407
  55.8 5.3 %collective-permute-start.20 = (bf16[128,256]{1,0:T(8,128)(2,1)S(1)}, bf16[128,256]{1,0:T(8,128)(2,1)S(1)}, u32[]{:S(2)}, u32[]{:S(2)}) collective-permute-start(bf16[128,256]{1,0:T(8,128)(2,1)S(1)} %add_up.1.refs_0_), channel_id=1, source_target_pairs={{0,4},{1,5},{2,6},{3,7},{4,0},{5,1},{6,2},{7,3},{8,12},{9,13},{10,... | collective-permute-start | bytes 196616 | tf_op jit(solution)/shard_map/ppermute | solution.py:407
  55.8 5.2 %collective-permute-start.19 = (bf16[128,256]{1,0:T(8,128)(2,1)S(1)}, bf16[128,256]{1,0:T(8,128)(2,1)S(1)}, u32[]{:S(2)}, u32[]{:S(2)}) collective-permute-start(bf16[128,256]{1,0:T(8,128)(2,1)S(1)} %add_up.1.refs_0_), channel_id=1, source_target_pairs={{0,2},{1,3},{2,0},{3,1},{4,6},{5,7},{6,4},{7,5},{8,10},{9,11},{10,... | collective-permute-start | bytes 196616 | tf_op jit(solution)/shard_map/ppermute | solution.py:407
  57.2 4.3 %collective-permute-start.22 = (bf16[128,256]{1,0:T(8,128)(2,1)S(1)}, bf16[128,256]{1,0:T(8,128)(2,1)S(1)}, u32[]{:S(2)}, u32[]{:S(2)}) collective-permute-start(bf16[128,256]{1,0:T(8,128)(2,1)S(1)} %add_up.1.refs_0_), channel_id=1, source_target_pairs={{0,1},{1,0},{2,3},{3,2},{4,5},{5,4},{6,7},{7,6},{8,9},{9,8},{10,11... | collective-permute-start | bytes 196616 | tf_op jit(solution)/shard_map/ppermute | solution.py:410
  59.3 2.3 %collective-permute-start.25 = (bf16[128,256]{1,0:T(8,128)(2,1)S(1)}, bf16[128,256]{1,0:T(8,128)(2,1)S(1)}, u32[]{:S(2)}, u32[]{:S(2)}) collective-permute-start(bf16[128,256]{1,0:T(8,128)(2,1)S(1)} %collective-permute-done.21.refs_3_), channel_id=1, source_target_pairs={{0,1},{1,0},{2,3},{3,2},{4,5},{5,4},{6,7},{7,6},{8,9},{9,8},{10,11... | collective-permute-start | bytes 196616 | tf_op jit(solution)/shard_map/ppermute | solution.py:410
  61.0 1.4 %collective-permute-start.23 = (bf16[128,256]{1,0:T(8,128)(2,1)S(1)}, bf16[128,256]{1,0:T(8,128)(2,1)S(1)}, u32[]{:S(2)}, u32[]{:S(2)}) collective-permute-start(bf16[128,256]{1,0:T(8,128)(2,1)S(1)} %collective-permute-done.19.refs_1_), channel_id=1, source_target_pairs={{0,1},{1,0},{2,3},{3,2},{4,5},{5,4},{6,7},{7,6},{8,9},{9,8},{10,11... | collective-permute-start | bytes 196616 | tf_op jit(solution)/shard_map/ppermute | solution.py:410
  (9 other events, 33.0 us)

commit v7 on v6

--- a/solution.py
+++ b/solution.py
@@ -254,6 +254,7 @@
     half = kb.shape[2]
     same_head = same_heads(half, size)
     mean_of = jnp.where(same_head, 1.0 / size, 0.0).astype(BF16)
+    mean_all = jnp.full((half, half), 0.5 / half, BF16)
     state = jnp.zeros((size, half), F32)
     back = jnp.zeros((size, half), F32)
     for m in range(1, chips):
@@ -284,15 +285,15 @@
         d_q, d_k, d_v = d_q.astype(BF16), d_k.astype(BF16), (grad_v * valid).astype(BF16)
         rstd = rstd_in[j]
         scaled = []
-        total = jnp.zeros((length, 1), F32)
+        total = 0.0
         for at in (keep_at, send_at):
             rows = pl.ds(at, half)
             weights = jnp.concatenate([w[rows, mine_at] for w in (w_q, w_k, w_v)], 1)
             d_normed = dot_nt(jnp.concatenate([d_q, d_k, d_v], 1), weights) * gain[:, rows]
             part = emb[j, :, rows].astype(F32)
             scaled.append((d_normed, part))
-            total = total + jnp.sum(d_normed * part, axis=1, keepdims=True)
-        pull = total * (rstd * rstd / (2 * half))
+            total = total + d_normed * part
+        pull = dot(total.astype(BF16), mean_all) * (rstd * rstd)
         kept = rstd * (scaled[0][0] - scaled[0][1] * pull)
         row_keep[j] = kept + d_ref[:, pl.ds(keep_at, half)].astype(F32) * valid
         row_send[1 - j] = (rstd * (scaled[1][0] - scaled[1][1] * pull)).astype(BF16)
@@ -352,13 +353,17 @@
     refs[-1][...] = row_sums(rows, cap, refs[:-1])
 
 
-def owner_sum(rows, cap, chips, count, info, early, *refs):
-    came, outs, acc = refs[:count], refs[count : count + chips], refs[count + chips]
-    z = info[2]
+def peer(z, core, masks):
+    return z ^ jnp.where(core == 0, masks[0], masks[1])
+
+
+def owner_sum(rows, cap, masks, count, info, early, *refs):
+    came, outs, acc = refs[:count], refs[count:-1], refs[-1]
+    core, z = info[1], info[2]
     acc[...] = early[...] + row_sums(rows, cap, came)
-    share = rows // chips
-    for m in range(chips):
-        at = pl.multiple_of((z ^ m) * share, share)
+    share = rows // len(masks)
+    for m, pair in enumerate(masks):
+        at = pl.multiple_of(peer(z, core, pair) * share, share)
         outs[m][...] = acc[pl.ds(at, share), :].astype(BF16)
 
 
@@ -369,16 +374,17 @@
     refs[chips][...] = total.astype(BF16)
 
 
-def assemble(chips, share, half, info, *refs):
-    own, other, (out, held, sems) = refs[:chips], refs[chips : 2 * chips], refs[2 * chips :]
+def assemble(masks, share, half, info, *refs):
+    chips = len(masks)
+    own, other, (out, sems) = refs[:chips], refs[chips : 2 * chips], refs[2 * chips :]
     core, z = info[1], info[2]
     copies = []
-    for m in range(chips):
-        rows = pl.ds(pl.multiple_of((z ^ m) * share, share), share)
-        for ref, side in ((own[m], core), (other[m], 1 - core)):
-            held[m, :, pl.ds(pl.multiple_of(side * half, half), half)] = ref[...]
-        copies.append(pltpu.make_async_copy(held.at[m], out.at[rows, :], sems.at[m]))
-        copies[-1].start()
+    for m, pair in enumerate(masks):
+        for n, (ref, side) in enumerate(((own[m], core), (other[m], 1 - core))):
+            rows = pl.ds(pl.multiple_of(peer(z, side, pair) * share, share), share)
+            columns = pl.ds(pl.multiple_of(side * half, half), half)
+            copies.append(pltpu.make_async_copy(ref, out.at[rows, columns], sems.at[2 * m + n]))
+            copies[-1].start()
     for copy in copies:
         copy.wait()
 
@@ -539,10 +545,17 @@
         "outward",
     )
     share = rows // chips
+    each = list(range(1, chips))
+    adding = [(0, 0)] + ([(3, 3), (1, 1), (2, 2)] if chips == 4 else list(zip(each, each)))
+    giving = [(0, 0)] + ([(1, 3), (2, 1), (3, 2)] if chips == 4 else list(zip(each, each)))
+
+    def by_core(x, masks):
+        return lax.ppermute(x, "ctx", [(c, c ^ (2 * masks[c % 2])) for c in range(count)])
+
     early, att_oth = lax.optimization_barrier((early, att_oth))
     att_came = swap(att_oth)
     everything = call(
-        functools.partial(owner_sum, rows, cap, chips, tables - 2),
+        functools.partial(owner_sum, rows, cap, adding, tables - 2),
         info,
         (early, *arrived[1:]),
         [array((share, half), BF16)] * chips,
@@ -551,7 +564,7 @@
         None,
         [pltpu.VMEM((rows, half), F32)],
     )
-    pieces = [over_z(everything[m], m) for m in (*range(chips - 1, chips), *range(1, chips - 1)) if m]
+    pieces = [by_core(x, pair) for x, pair in zip(everything[1:], adding[1:])]
     if pieces:
         pieces[0], att_came = lax.optimization_barrier((pieces[0], att_came))
     (output,) = call(
@@ -573,17 +586,17 @@
         chips * share * half,
         "add_up",
     )
-    own = [summed] + [over_z(summed, m) for m in range(1, chips)]
+    own = [summed] + [by_core(summed, pair) for pair in giving[1:]]
     other = [swap(x) for x in own]
     (table_grad,) = call(
-        functools.partial(assemble, chips, share, half),
+        functools.partial(assemble, giving, share, half),
         info,
         [*own, *other],
         [array((rows, width), BF16)],
         rows * width,
         "assemble",
         pl.ANY,
-        [pltpu.VMEM((chips, share, width), BF16), pltpu.SemaphoreType.DMA((chips,))],
+        [pltpu.SemaphoreType.DMA((2 * chips,))],
     )
     return (output[None], table_grad)
 

time: 64 us -> 64 us (level)
    ppermute x0 -> x6, starting transfers between devices: none -> 8.91 us  [by_core(): lax.ppermute(x, 'ctx', [(c, c ^ 2 * masks[c % 2]) for c in range(count)])]
    ppermute x9 -> x3, starting transfers between devices: 13.7 us -> 4.82 us  [over_z(): return lax.ppermute(x, 'ctx', [(i, i ^ 2 * m) for i in range(count)])]
    ppermute x0 -> x6, waiting for transfers between devices: none -> 5.83 us  [by_core(): lax.ppermute(x, 'ctx', [(c, c ^ 2 * masks[c % 2]) for c in range(count)])]
    ppermute x9 -> x3, waiting for transfers between devices: 7.32 us -> 1.51 us  [over_z(): return lax.ppermute(x, 'ctx', [(i, i ^ 2 * m) for i in range(count)])]
where the time goes in v7:
time: 64 us; the launch traced here: 63.8 us
  starting transfers between devices  24.7 us (39%)
  waiting for transfers between devices  18 us (28%)
  Pallas kernels  17.9 us (28%)
  between operations  1.49 us (2%)
  local copies, waits for them, and re-layouts  0.82 us (1%)
  other arithmetic  0.78 us (1%)
    pallas_call x11, Pallas kernels, call(): pl.pallas_call(body, in_specs=[pl.BlockSpec(memory_space=pltpu.SMEM)] + [...  16.8 us
    ppermute x6, starting transfers between devices, by_core(): lax.ppermute(x, 'ctx', [(c, c ^ 2 * masks[c % 2]) for c in range(count)])  8.91 us
    ppermute x6, waiting for transfers between devices, by_core(): lax.ppermute(x, 'ctx', [(c, c ^ 2 * masks[c % 2]) for c in range(count)])  5.83 us
    ppermute x3, starting transfers between devices, from_mask(): lax.ppermute(x, ('table', 'ctx'), [(t * count + c, (t ^ masks[c % 2]) * c...  5.69 us
    ppermute x3, starting transfers between devices, over_z(): return lax.ppermute(x, 'ctx', [(i, i ^ 2 * m) for i in range(count)])  4.82 us
    ppermute x3, waiting for transfers between devices, over_table(): return lax.ppermute(x, 'table', [(i, i ^ m) for i in range(tables)])  3.97 us
    ppermute x11, waiting for transfers between devices, swap(): return lax.ppermute(x, 'ctx', [(i, i ^ 1) for i in range(count)])  3.96 us
    ppermute x3, starting transfers between devices, over_table(): return lax.ppermute(x, 'table', [(i, i ^ m) for i in range(tables)])  3.55 us
  transfers between devices with their start and end apart: 26, of which 15 were waited for; matrix products, arithmetic and copies ran while one was open for 1% of the time, Pallas kernels for 15%

profile of v7, /device:TPU:0, one launch (start us, length us, event | category | flops | bytes accessed | tf_op | source)
XLA Modules:
  0.0 63.8 jit_solution(5469224204980257023)
XLA Ops:
  0.7 1.1 %pick.1 = (bf16[256,512]{1,0:T(8,128)(2,1)S(1)}, bf16[256,512]{1,0:T(8,128)(2,1)S(1)}) custom-call(bf16[512,512]{1,0:T(8,128)(2,1)} %table.1), custom_call_target="tpu_custom_call" | custom-call | tf_op jit(solution)/shard_map/pick/pallas_call | solution.py:423
  1.8 3.0 %collective-permute-start.2 = (bf16[256,512]{1,0:T(8,128)(2,1)S(1)}, bf16[256,512]{1,0:T(8,128)(2,1)S(1)}, u32[]{:S(2)}, u32[]{:S(2)}) collective-permute-start(bf16[256,512]{1,0:T(8,128)(2,1)S(1)} %get-tuple-element.57.refs_0_), channel_id=1, source_target_pairs={{0,8},{1,17},{2,10},{3,19},{4,12},{5,21},{6,14},{7,23},{8,0},{9,25... | collective-permute-start | bytes 786440 | tf_op jit(solution)/shard_map/ppermute | solution.py:433
  6.6 2.5 %collective-permute-done.2.refs_2_ = bf16[256,512]{1,0:T(8,128)(2,1)S(1)} collective-permute-done((bf16[256,512]{1,0:T(8,128)(2,1)S(1)}, bf16[256,512]{1,0:T(8,128)(2,1)S(1)}, u32[]{:S(2)}, u32[]{:S(2)}) %collective-permute-start.2) | collective-permute-done | bytes 262176 | tf_op jit(solution)/shard_map/ppermute | solution.py:433
  9.1 2.0 %collective-permute-start.4 = (bf16[256,512]{1,0:T(8,128)(2,1)S(1)}, bf16[256,512]{1,0:T(8,128)(2,1)S(1)}, u32[]{:S(2)}, u32[]{:S(2)}) collective-permute-start(bf16[256,512]{1,0:T(8,128)(2,1)S(1)} %collective-permute-done.2.refs_2_), channel_id=1, source_target_pairs={{0,16},{1,9},{2,18},{3,11},{4,20},{5,13},{6,22},{7,15},{8,24},{9,1... | collective-permute-start | bytes 786440 | tf_op jit(solution)/shard_map/ppermute | solution.py:433
  12.8 1.9 %prepare.1 = (bf16[2,256,256]{2,1,0:T(8,128)(2,1)S(1)}, bf16[2,256,256]{2,1,0:T(8,128)(2,1)S(1)}, s32[2,256]{1,0:T(2,128)S(1)}, bf16[4,16,128]{2,1,0:T(8,128)(2,...) custom-call(s32[4]{0:T(128)S(1)} %pad_add_fusion.1.info, ...), custom_call_target="tpu_custom_call" | custom-call | flops 134217728 | bytes 3957760 | tf_op jit(solution)/shard_map/prepare/pallas_call | solution.py:35
  17.1 2.6 %project.1 = (bf16[2,256,512]{2,1,0:T(8,128)(2,1)S(1)}, bf16[2,256,256]{2,1,0:T(8,128)(2,1)S(1)}, bf16[2,256,256]{2,1,0:T(8,128)(2,1)S(1)}, bf16[2,256,256]{2,1,...) custom-call(s32[4]{0:T(128)S(1)} %pad_add_fusion.1.info, ...), custom_call_target="tpu_custom_call" | custom-call | flops 1073741824 | bytes 8460288 | tf_op jit(solution)/shard_map/project/pallas_call | solution.py:35
  19.7 4.2 %collective-permute-start.10 = (bf16[64,256]{1,0:T(8,128)(2,1)S(1)}, bf16[64,256]{1,0:T(8,128)(2,1)S(1)}, u32[]{:S(2)}, u32[]{:S(2)}) collective-permute-start(bf16[64,256]{1,0:T(8,128)(2,1)S(1)} %get-tuple-element.86), channel_id=1, source_target_pairs={{0,6},{1,7},{2,4},{3,5},{4,2},{5,3},{6,0},{7,1},{8,14},{9,15},{10,... | collective-permute-start | bytes 98312 | tf_op jit(solution)/shard_map/ppermute | solution.py:413
  24.5 2.7 %attend.1 = (bf16[2,256,256]{2,1,0:T(8,128)(2,1)S(1)}, bf16[2,256,256]{2,1,0:T(8,128)(2,1)S(1)}, bf16[2,256,256]{2,1,0:T(8,128)(2,1)S(1)}) custom-call(s32[4]{0:T(128)S(1)} %pad_add_fusion.1.info, bf16[2,256,256]{2,1,0:T(8,128)(2,1)S(1)} %get-tuple-element.77.qa_in, bf16[2,256,256]{2,1,0:T(8,128)(2,1)S(1)} %get-tuple-element.69.kb_in.kb, ...), custom_call_target="tpu_custom_call" | custom-call | flops 402653184 | bytes 2883584 | tf_op jit(solution)/shard_map/attend/pallas_call | solution.py:35
  28.7 2.1 %finish.1 = (bf16[256,256]{1,0:T(8,128)(2,1)S(1)}, f32[2,256,256]{2,1,0:T(8,128)S(1)}, bf16[2,256,256]{2,1,0:T(8,128)(2,1)S(1)}) custom-call(s32[4]{0:T(128)S(1)} %pad_add_fusion.1.info, f32[1,256]{1,0:T(1,128)S(1)} %get-tuple-element.59.rate, bf16[2,256,256]{2,1,0:T(8,128)(2,1)S(1)} %get-tuple-element.69.kb_in.kb, ...), custom_call_target="tpu_custom_call" | custom-call | flops 402653184 | bytes 6788096 | tf_op jit(solution)/shard_map/finish/pallas_call | solution.py:35
  30.8 1.5 %collective-permute-done.11.row_came = bf16[2,256,256]{2,1,0:T(8,128)(2,1)S(1)} collective-permute-done((bf16[2,256,256]{2,1,0:T(8,128)(2,1)S(1)}, bf16[2,256,256]{2,1,0:T(8,128)(2,1)S(1)}, u32[]{:S(2)}, u32[]{:S(2)}) %collective-permute-start.11) | collective-permute-done | bytes 262176 | tf_op jit(solution)/shard_map/ppermute | solution.py:416
  33.2 1.5 %collective-permute-start.12 = (bf16[272,256]{1,0:T(8,128)(2,1)S(1)}, bf16[272,256]{1,0:T(8,128)(2,1)S(1)}, u32[]{:S(2)}, u32[]{:S(2)}) collective-permute-start(bf16[272,256]{1,0:T(8,128)(2,1)S(1)} %get-tuple-element.91), channel_id=1, source_target_pairs={{0,8},{8,0},{16,24},{24,16},{1,9},{9,1},{17,25},{25,17},{2,10},{10... | collective-permute-start | bytes 417800 | tf_op jit(solution)/shard_map/ppermute | solution.py:410
  34.8 1.5 %collective-permute-start.13 = (bf16[272,256]{1,0:T(8,128)(2,1)S(1)}, bf16[272,256]{1,0:T(8,128)(2,1)S(1)}, u32[]{:S(2)}, u32[]{:S(2)}) collective-permute-start(bf16[272,256]{1,0:T(8,128)(2,1)S(1)} %get-tuple-element.97), channel_id=1, source_target_pairs={{0,16},{8,24},{16,0},{24,8},{1,17},{9,25},{17,1},{25,9},{2,18},{10... | collective-permute-start | bytes 417800 | tf_op jit(solution)/shard_map/ppermute | solution.py:410
  36.8 2.8 %collective-permute-done.12.refs_1_ = bf16[272,256]{1,0:T(8,128)(2,1)S(1)} collective-permute-done((bf16[272,256]{1,0:T(8,128)(2,1)S(1)}, bf16[272,256]{1,0:T(8,128)(2,1)S(1)}, u32[]{:S(2)}, u32[]{:S(2)}) %collective-permute-start.12) | collective-permute-done | bytes 139296 | tf_op jit(solution)/shard_map/ppermute | solution.py:410
  39.6 1.5 %outward.1 = (bf16[256,256]{1,0:T(8,128)(2,1)S(1)}, bf16[256,256]{1,0:T(8,128)(2,1)S(1)}) custom-call(s32[4]{0:T(128)S(1)} %pad_add_fusion.1.info, bf16[2,256,256]{2,1,0:T(8,128)(2,1)S(1)} %get-tuple-element.77.qa_in, bf16[2,256,256]{2,1,0:T(8,128)(2,1)S(1)} %get-tuple-element.69.kb_in.kb, bf16[2,256,256]{2,1,0:T(8,128)(2,1)S(1)} %get-tuple-element.78.v_in, ...), custom_call_target="tpu_custom_call" | custom-call | flops 134217728 | bytes 1703936 | tf_op jit(solution)/shard_map/outward/pallas_call | solution.py:35
  42.0 1.2 %collective-permute-done.13.refs_0_ = bf16[272,256]{1,0:T(8,128)(2,1)S(1)} collective-permute-done((bf16[272,256]{1,0:T(8,128)(2,1)S(1)}, bf16[272,256]{1,0:T(8,128)(2,1)S(1)}, u32[]{:S(2)}, u32[]{:S(2)}) %collective-permute-start.13) | collective-permute-done | bytes 139296 | tf_op jit(solution)/shard_map/ppermute | solution.py:410
  44.1 2.4 %collective-permute-start.15 = (bf16[128,256]{1,0:T(8,128)(2,1)S(1)}, bf16[128,256]{1,0:T(8,128)(2,1)S(1)}, u32[]{:S(2)}, u32[]{:S(2)}) collective-permute-start(bf16[128,256]{1,0:T(8,128)(2,1)S(1)} %get-tuple-element.99), channel_id=1, source_target_pairs={{0,6},{1,7},{2,4},{3,5},{4,2},{5,3},{6,0},{7,1},{8,14},{9,15},{10,... | collective-permute-start | bytes 196616 | tf_op jit(solution)/shard_map/ppermute | solution.py:553
  46.7 1.8 %collective-permute-start.18 = (bf16[128,256]{1,0:T(8,128)(2,1)S(1)}, bf16[128,256]{1,0:T(8,128)(2,1)S(1)}, u32[]{:S(2)}, u32[]{:S(2)}) collective-permute-start(bf16[128,256]{1,0:T(8,128)(2,1)S(1)} %get-tuple-element.103), channel_id=1, source_target_pairs={{0,4},{1,5},{2,6},{3,7},{4,0},{5,1},{6,2},{7,3},{8,12},{9,13},{10,... | collective-permute-start | bytes 196616 | tf_op jit(solution)/shard_map/ppermute | solution.py:553
  48.5 1.9 %collective-permute-done.15.refs_1_ = bf16[128,256]{1,0:T(8,128)(2,1)S(1)} collective-permute-done((bf16[128,256]{1,0:T(8,128)(2,1)S(1)}, bf16[128,256]{1,0:T(8,128)(2,1)S(1)}, u32[]{:S(2)}, u32[]{:S(2)}) %collective-permute-start.15) | collective-permute-done | bytes 65568 | tf_op jit(solution)/shard_map/ppermute | solution.py:553
  50.5 1.6 %result.1 = bf16[256,512]{1,0:T(8,128)(2,1)} custom-call(s32[4]{0:T(128)S(1)} %pad_add_fusion.1.info, bf16[2,256,512]{2,1,0:T(8,128)(2,1)S(1)} %get-tuple-element.83.emb, bf16[256,256]{1,0:T(8,128)(2,1)S(1)} %get-tuple-element.104.att_own, bf16[256,256]{1,0:T(8,128)(2,1)S(1)} %collective-permute-done.16.att_came, bf16[512,512]{1,0:T(8,128)(2,1)S(1)} %get-tuple-element.106.w_out), custom_call_target="tpu_custom_call" | custom-call | flops 134217728 | bytes 1572864 | tf_op jit(solution)/shard_map/result/pallas_call | solution.py:35
  52.7 2.9 %collective-permute-start.21 = (bf16[128,256]{1,0:T(8,128)(2,1)S(1)}, bf16[128,256]{1,0:T(8,128)(2,1)S(1)}, u32[]{:S(2)}, u32[]{:S(2)}) collective-permute-start(bf16[128,256]{1,0:T(8,128)(2,1)S(1)} %add_up.1.refs_0_), channel_id=1, source_target_pairs={{0,6},{1,5},{2,4},{3,7},{4,2},{5,1},{6,0},{7,3},{8,14},{9,13},{10,... | collective-permute-start | bytes 196616 | tf_op jit(solution)/shard_map/ppermute | solution.py:553
  55.7 1.4 %collective-permute-start.19 = (bf16[128,256]{1,0:T(8,128)(2,1)S(1)}, bf16[128,256]{1,0:T(8,128)(2,1)S(1)}, u32[]{:S(2)}, u32[]{:S(2)}) collective-permute-start(bf16[128,256]{1,0:T(8,128)(2,1)S(1)} %add_up.1.refs_0_), channel_id=1, source_target_pairs={{0,2},{1,7},{2,0},{3,5},{4,6},{5,3},{6,4},{7,1},{8,10},{9,15},{10,... | collective-permute-start | bytes 196616 | tf_op jit(solution)/shard_map/ppermute | solution.py:553
  57.2 2.1 %collective-permute-done.21.refs_3_ = bf16[128,256]{1,0:T(8,128)(2,1)S(1)} collective-permute-done((bf16[128,256]{1,0:T(8,128)(2,1)S(1)}, bf16[128,256]{1,0:T(8,128)(2,1)S(1)}, u32[]{:S(2)}, u32[]{:S(2)}) %collective-permute-start.21) | collective-permute-done | bytes 65568 | tf_op jit(solution)/shard_map/ppermute | solution.py:553
  59.2 1.7 %collective-permute-done.20.refs_2_ = bf16[128,256]{1,0:T(8,128)(2,1)S(1)} collective-permute-done((bf16[128,256]{1,0:T(8,128)(2,1)S(1)}, bf16[128,256]{1,0:T(8,128)(2,1)S(1)}, u32[]{:S(2)}, u32[]{:S(2)}) %collective-permute-start.20) | collective-permute-done | bytes 65568 | tf_op jit(solution)/shard_map/ppermute | solution.py:553
  62.4 1.4 %assemble.1 = bf16[512,512]{1,0:T(8,128)(2,1)} custom-call(s32[4]{0:T(128)S(1)} %pad_add_fusion.1.info, bf16[128,256]{1,0:T(8,128)(2,1)S(1)} %add_up.1.refs_0_, bf16[128,256]{1,0:T(8,128)(2,1)S(1)} %collective-permute-done.19.refs_1_, bf16[128,256]{1,0:T(8,128)(2,1)S(1)} %collective-permute-done.20.refs_2_, ...), custom_call_target="tpu_custom_call" | custom-call | flops 262144 | bytes 1048576 | tf_op jit(solution)/shard_map/assemble/pallas_call | solution.py:35
  (58 shorter events, 13.0 us)
Async XLA Ops:
  1.8 7.4 %collective-permute-start.2 = (bf16[256,512]{1,0:T(8,128)(2,1)S(1)}, bf16[256,512]{1,0:T(8,128)(2,1)S(1)}, u32[]{:S(2)}, u32[]{:S(2)}) collective-permute-start(bf16[256,512]{1,0:T(8,128)(2,1)S(1)} %get-tuple-element.57.refs_0_), channel_id=1, source_target_pairs={{0,8},{1,17},{2,10},{3,19},{4,12},{5,21},{6,14},{7,23},{8,0},{9,25... | collective-permute-start | bytes 786440 | tf_op jit(solution)/shard_map/ppermute | solution.py:433
  5.5 6.6 %collective-permute-start = (bf16[256,512]{1,0:T(8,128)(2,1)S(1)}, bf16[256,512]{1,0:T(8,128)(2,1)S(1)}, u32[]{:S(2)}, u32[]{:S(2)}) collective-permute-start(bf16[256,512]{1,0:T(8,128)(2,1)S(1)} %bitcast.11), channel_id=1, source_target_pairs={{0,1},{1,0},{2,3},{3,2},{4,5},{5,4},{6,7},{7,6},{8,9},{9,8},{10,11... | collective-permute-start | bytes 786440 | tf_op jit(solution)/shard_map/ppermute | solution.py:416
  6.0 8.7 %collective-permute-start.3 = (bf16[256,512]{1,0:T(8,128)(2,1)S(1)}, bf16[256,512]{1,0:T(8,128)(2,1)S(1)}, u32[]{:S(2)}, u32[]{:S(2)}) collective-permute-start(bf16[256,512]{1,0:T(8,128)(2,1)S(1)} %get-tuple-element.58.refs_1_), channel_id=1, source_target_pairs={{0,8},{1,17},{2,10},{3,19},{4,12},{5,21},{6,14},{7,23},{8,0},{9,25... | collective-permute-start | bytes 786440 | tf_op jit(solution)/shard_map/ppermute | solution.py:433
  9.1 6.4 %collective-permute-start.4 = (bf16[256,512]{1,0:T(8,128)(2,1)S(1)}, bf16[256,512]{1,0:T(8,128)(2,1)S(1)}, u32[]{:S(2)}, u32[]{:S(2)}) collective-permute-start(bf16[256,512]{1,0:T(8,128)(2,1)S(1)} %collective-permute-done.2.refs_2_), channel_id=1, source_target_pairs={{0,16},{1,9},{2,18},{3,11},{4,20},{5,13},{6,22},{7,15},{8,24},{9,1... | collective-permute-start | bytes 786440 | tf_op jit(solution)/shard_map/ppermute | solution.py:433
  14.7 2.0 %collective-permute-start.6 = (bf16[256,512]{1,0:T(8,128)(2,1)S(1)}, bf16[256,512]{1,0:T(8,128)(2,1)S(1)}, u32[]{:S(2)}, u32[]{:S(2)}) collective-permute-start(bf16[256,512]{1,0:T(8,128)(2,1)S(1)} %collective-permute-done.3.refs_0_), channel_id=1, source_target_pairs={{0,1},{1,0},{2,3},{3,2},{4,5},{5,4},{6,7},{7,6},{8,9},{9,8},{10,11... | collective-permute-start | bytes 786440 | tf_op jit(solution)/shard_map/ppermute | solution.py:416
  14.8 1.9 %collective-permute-start.5 = (bf16[256,512]{1,0:T(8,128)(2,1)S(1)}, bf16[256,512]{1,0:T(8,128)(2,1)S(1)}, u32[]{:S(2)}, u32[]{:S(2)}) collective-permute-start(bf16[256,512]{1,0:T(8,128)(2,1)S(1)} %collective-permute-done.2.refs_2_), channel_id=1, source_target_pairs={{0,1},{1,0},{2,3},{3,2},{4,5},{5,4},{6,7},{7,6},{8,9},{9,8},{10,11... | collective-permute-start | bytes 786440 | tf_op jit(solution)/shard_map/ppermute | solution.py:416
  15.5 1.5 %collective-permute-start.7 = (bf16[256,512]{1,0:T(8,128)(2,1)S(1)}, bf16[256,512]{1,0:T(8,128)(2,1)S(1)}, u32[]{:S(2)}, u32[]{:S(2)}) collective-permute-start(bf16[256,512]{1,0:T(8,128)(2,1)S(1)} %collective-permute-done.4.refs_1_), channel_id=1, source_target_pairs={{0,1},{1,0},{2,3},{3,2},{4,5},{5,4},{6,7},{7,6},{8,9},{9,8},{10,11... | collective-permute-start | bytes 786440 | tf_op jit(solution)/shard_map/ppermute | solution.py:416
  19.7 8.1 %collective-permute-start.10 = (bf16[64,256]{1,0:T(8,128)(2,1)S(1)}, bf16[64,256]{1,0:T(8,128)(2,1)S(1)}, u32[]{:S(2)}, u32[]{:S(2)}) collective-permute-start(bf16[64,256]{1,0:T(8,128)(2,1)S(1)} %get-tuple-element.86), channel_id=1, source_target_pairs={{0,6},{1,7},{2,4},{3,5},{4,2},{5,3},{6,0},{7,1},{8,14},{9,15},{10,... | collective-permute-start | bytes 98312 | tf_op jit(solution)/shard_map/ppermute | solution.py:413
  23.9 4.8 %collective-permute-start.9 = (bf16[64,256]{1,0:T(8,128)(2,1)S(1)}, bf16[64,256]{1,0:T(8,128)(2,1)S(1)}, u32[]{:S(2)}, u32[]{:S(2)}) collective-permute-start(bf16[64,256]{1,0:T(8,128)(2,1)S(1)} %get-tuple-element.86), channel_id=1, source_target_pairs={{0,4},{1,5},{2,6},{3,7},{4,0},{5,1},{6,2},{7,3},{8,12},{9,13},{10,... | collective-permute-start | bytes 98312 | tf_op jit(solution)/shard_map/ppermute | solution.py:413
  23.9 3.9 %collective-permute-start.8 = (bf16[64,256]{1,0:T(8,128)(2,1)S(1)}, bf16[64,256]{1,0:T(8,128)(2,1)S(1)}, u32[]{:S(2)}, u32[]{:S(2)}) collective-permute-start(bf16[64,256]{1,0:T(8,128)(2,1)S(1)} %get-tuple-element.85), channel_id=1, source_target_pairs={{0,2},{1,3},{2,0},{3,1},{4,6},{5,7},{6,4},{7,5},{8,10},{9,11},{10,... | collective-permute-start | bytes 98312 | tf_op jit(solution)/shard_map/ppermute | solution.py:413
  30.8 1.6 %collective-permute-start.11 = (bf16[2,256,256]{2,1,0:T(8,128)(2,1)S(1)}, bf16[2,256,256]{2,1,0:T(8,128)(2,1)S(1)}, u32[]{:S(2)}, u32[]{:S(2)}) collective-permute-start(bf16[2,256,256]{2,1,0:T(8,128)(2,1)S(1)} %get-tuple-element.88), channel_id=1, source_target_pairs={{0,1},{1,0},{2,3},{3,2},{4,5},{5,4},{6,7},{7,6},{8,9},{9,8},{10,11... | collective-permute-start | bytes 786440 | tf_op jit(solution)/shard_map/ppermute | solution.py:416
  33.2 6.3 %collective-permute-start.12 = (bf16[272,256]{1,0:T(8,128)(2,1)S(1)}, bf16[272,256]{1,0:T(8,128)(2,1)S(1)}, u32[]{:S(2)}, u32[]{:S(2)}) collective-permute-start(bf16[272,256]{1,0:T(8,128)(2,1)S(1)} %get-tuple-element.91), channel_id=1, source_target_pairs={{0,8},{8,0},{16,24},{24,16},{1,9},{9,1},{17,25},{25,17},{2,10},{10... | collective-permute-start | bytes 417800 | tf_op jit(solution)/shard_map/ppermute | solution.py:410
  34.8 8.4 %collective-permute-start.13 = (bf16[272,256]{1,0:T(8,128)(2,1)S(1)}, bf16[272,256]{1,0:T(8,128)(2,1)S(1)}, u32[]{:S(2)}, u32[]{:S(2)}) collective-permute-start(bf16[272,256]{1,0:T(8,128)(2,1)S(1)} %get-tuple-element.97), channel_id=1, source_target_pairs={{0,16},{8,24},{16,0},{24,8},{1,17},{9,25},{17,1},{25,9},{2,18},{10... | collective-permute-start | bytes 417800 | tf_op jit(solution)/shard_map/ppermute | solution.py:410
  36.3 6.9 %collective-permute-start.14 = (bf16[272,256]{1,0:T(8,128)(2,1)S(1)}, bf16[272,256]{1,0:T(8,128)(2,1)S(1)}, u32[]{:S(2)}, u32[]{:S(2)}) collective-permute-start(bf16[272,256]{1,0:T(8,128)(2,1)S(1)} %get-tuple-element.98), channel_id=1, source_target_pairs={{0,24},{8,16},{16,8},{24,0},{1,25},{9,17},{17,9},{25,1},{2,26},{10... | collective-permute-start | bytes 417800 | tf_op jit(solution)/shard_map/ppermute | solution.py:410
  41.9 8.6 %collective-permute-start.16 = (bf16[256,256]{1,0:T(8,128)(2,1)S(1)}, bf16[256,256]{1,0:T(8,128)(2,1)S(1)}, u32[]{:S(2)}, u32[]{:S(2)}) collective-permute-start(bf16[256,256]{1,0:T(8,128)(2,1)S(1)} %get-tuple-element.100), channel_id=1, source_target_pairs={{0,1},{1,0},{2,3},{3,2},{4,5},{5,4},{6,7},{7,6},{8,9},{9,8},{10,11... | collective-permute-start | bytes 393224 | tf_op jit(solution)/shard_map/ppermute | solution.py:416
  44.1 6.4 %collective-permute-start.15 = (bf16[128,256]{1,0:T(8,128)(2,1)S(1)}, bf16[128,256]{1,0:T(8,128)(2,1)S(1)}, u32[]{:S(2)}, u32[]{:S(2)}) collective-permute-start(bf16[128,256]{1,0:T(8,128)(2,1)S(1)} %get-tuple-element.99), channel_id=1, source_target_pairs={{0,6},{1,7},{2,4},{3,5},{4,2},{5,3},{6,0},{7,1},{8,14},{9,15},{10,... | collective-permute-start | bytes 196616 | tf_op jit(solution)/shard_map/ppermute | solution.py:553
  46.4 5.7 %collective-permute-start.17 = (bf16[128,256]{1,0:T(8,128)(2,1)S(1)}, bf16[128,256]{1,0:T(8,128)(2,1)S(1)}, u32[]{:S(2)}, u32[]{:S(2)}) collective-permute-start(bf16[128,256]{1,0:T(8,128)(2,1)S(1)} %get-tuple-element.102), channel_id=1, source_target_pairs={{0,2},{1,3},{2,0},{3,1},{4,6},{5,7},{6,4},{7,5},{8,10},{9,11},{10,... | collective-permute-start | bytes 196616 | tf_op jit(solution)/shard_map/ppermute | solution.py:553
  46.7 5.4 %collective-permute-start.18 = (bf16[128,256]{1,0:T(8,128)(2,1)S(1)}, bf16[128,256]{1,0:T(8,128)(2,1)S(1)}, u32[]{:S(2)}, u32[]{:S(2)}) collective-permute-start(bf16[128,256]{1,0:T(8,128)(2,1)S(1)} %get-tuple-element.103), channel_id=1, source_target_pairs={{0,4},{1,5},{2,6},{3,7},{4,0},{5,1},{6,2},{7,3},{8,12},{9,13},{10,... | collective-permute-start | bytes 196616 | tf_op jit(solution)/shard_map/ppermute | solution.py:553
  52.7 6.5 %collective-permute-start.21 = (bf16[128,256]{1,0:T(8,128)(2,1)S(1)}, bf16[128,256]{1,0:T(8,128)(2,1)S(1)}, u32[]{:S(2)}, u32[]{:S(2)}) collective-permute-start(bf16[128,256]{1,0:T(8,128)(2,1)S(1)} %add_up.1.refs_0_), channel_id=1, source_target_pairs={{0,6},{1,5},{2,4},{3,7},{4,2},{5,1},{6,0},{7,3},{8,14},{9,13},{10,... | collective-permute-start | bytes 196616 | tf_op jit(solution)/shard_map/ppermute | solution.py:553
  55.7 5.3 %collective-permute-start.20 = (bf16[128,256]{1,0:T(8,128)(2,1)S(1)}, bf16[128,256]{1,0:T(8,128)(2,1)S(1)}, u32[]{:S(2)}, u32[]{:S(2)}) collective-permute-start(bf16[128,256]{1,0:T(8,128)(2,1)S(1)} %add_up.1.refs_0_), channel_id=1, source_target_pairs={{0,4},{1,3},{2,6},{3,1},{4,0},{5,7},{6,2},{7,5},{8,12},{9,11},{10,... | collective-permute-start | bytes 196616 | tf_op jit(solution)/shard_map/ppermute | solution.py:553
  55.7 5.2 %collective-permute-start.19 = (bf16[128,256]{1,0:T(8,128)(2,1)S(1)}, bf16[128,256]{1,0:T(8,128)(2,1)S(1)}, u32[]{:S(2)}, u32[]{:S(2)}) collective-permute-start(bf16[128,256]{1,0:T(8,128)(2,1)S(1)} %add_up.1.refs_0_), channel_id=1, source_target_pairs={{0,2},{1,7},{2,0},{3,5},{4,6},{5,3},{6,4},{7,1},{8,10},{9,15},{10,... | collective-permute-start | bytes 196616 | tf_op jit(solution)/shard_map/ppermute | solution.py:553
  57.2 4.3 %collective-permute-start.22 = (bf16[128,256]{1,0:T(8,128)(2,1)S(1)}, bf16[128,256]{1,0:T(8,128)(2,1)S(1)}, u32[]{:S(2)}, u32[]{:S(2)}) collective-permute-start(bf16[128,256]{1,0:T(8,128)(2,1)S(1)} %add_up.1.refs_0_), channel_id=1, source_target_pairs={{0,1},{1,0},{2,3},{3,2},{4,5},{5,4},{6,7},{7,6},{8,9},{9,8},{10,11... | collective-permute-start | bytes 196616 | tf_op jit(solution)/shard_map/ppermute | solution.py:416
  59.2 2.2 %collective-permute-start.25 = (bf16[128,256]{1,0:T(8,128)(2,1)S(1)}, bf16[128,256]{1,0:T(8,128)(2,1)S(1)}, u32[]{:S(2)}, u32[]{:S(2)}) collective-permute-start(bf16[128,256]{1,0:T(8,128)(2,1)S(1)} %collective-permute-done.21.refs_3_), channel_id=1, source_target_pairs={{0,1},{1,0},{2,3},{3,2},{4,5},{5,4},{6,7},{7,6},{8,9},{9,8},{10,11... | collective-permute-start | bytes 196616 | tf_op jit(solution)/shard_map/ppermute | solution.py:416
  61.0 1.4 %collective-permute-start.23 = (bf16[128,256]{1,0:T(8,128)(2,1)S(1)}, bf16[128,256]{1,0:T(8,128)(2,1)S(1)}, u32[]{:S(2)}, u32[]{:S(2)}) collective-permute-start(bf16[128,256]{1,0:T(8,128)(2,1)S(1)} %collective-permute-done.19.refs_1_), channel_id=1, source_target_pairs={{0,1},{1,0},{2,3},{3,2},{4,5},{5,4},{6,7},{7,6},{8,9},{9,8},{10,11... | collective-permute-start | bytes 196616 | tf_op jit(solution)/shard_map/ppermute | solution.py:416
  (9 other events, 33.0 us)

commit v8 on v6

--- a/solution.py
+++ b/solution.py
@@ -40,7 +40,7 @@
         out_specs=[pl.BlockSpec(memory_space=final) if final else here] * len(outs),
         out_shape=outs if final else [pltpu.VMEM(o.shape, o.dtype) for o in outs],
         scratch_shapes=scratch,
-        compiler_params=pltpu.CompilerParams(vmem_limit_bytes=32 * MIB),
+        compiler_params=pltpu.CompilerParams(vmem_limit_bytes=16 * MIB),
         cost_estimate=pl.CostEstimate(flops=flops, bytes_accessed=moved, transcendentals=0),
         name=name,
     )(info, *operands, *away)

time: 64 us -> 64 us (level)
  no operation moved by 1% of the time
where the time goes in v8:
time: 64 us; the launch traced here: 63.8 us
  starting transfers between devices  24.7 us (39%)
  Pallas kernels  18 us (28%)
  waiting for transfers between devices  18 us (28%)
  between operations  1.49 us (2%)
  local copies, waits for them, and re-layouts  0.82 us (1%)
  other arithmetic  0.78 us (1%)
    pallas_call x11, Pallas kernels, call(): pl.pallas_call(body, in_specs=[pl.BlockSpec(memory_space=pltpu.SMEM)] + [...  16.9 us
    ppermute x9, starting transfers between devices, over_z(): return lax.ppermute(x, 'ctx', [(i, i ^ 2 * m) for i in range(count)])  13.7 us
    ppermute x9, waiting for transfers between devices, over_z(): return lax.ppermute(x, 'ctx', [(i, i ^ 2 * m) for i in range(count)])  7.32 us
    ppermute x3, starting transfers between devices, from_mask(): lax.ppermute(x, ('table', 'ctx'), [(t * count + c, (t ^ masks[c % 2]) * c...  5.69 us
    ppermute x3, waiting for transfers between devices, over_table(): return lax.ppermute(x, 'table', [(i, i ^ m) for i in range(tables)])  3.98 us
    ppermute x11, waiting for transfers between devices, swap(): return lax.ppermute(x, 'ctx', [(i, i ^ 1) for i in range(count)])  3.96 us
    ppermute x3, starting transfers between devices, over_table(): return lax.ppermute(x, 'table', [(i, i ^ m) for i in range(tables)])  3.55 us
    ppermute x3, waiting for transfers between devices, from_mask(): lax.ppermute(x, ('table', 'ctx'), [(t * count + c, (t ^ masks[c % 2]) * c...  2.78 us
  transfers between devices with their start and end apart: 26, of which 15 were waited for; matrix products, arithmetic and copies ran while one was open for 1% of the time, Pallas kernels for 15%

profile of v8, /device:TPU:0, one launch (start us, length us, event | category | flops | bytes accessed | tf_op | source)
XLA Modules:
  0.0 63.8 jit_solution(9168997792947084153)
XLA Ops:
  0.7 1.1 %pick.1 = (bf16[256,512]{1,0:T(8,128)(2,1)S(1)}, bf16[256,512]{1,0:T(8,128)(2,1)S(1)}) custom-call(bf16[512,512]{1,0:T(8,128)(2,1)} %table.1), custom_call_target="tpu_custom_call" | custom-call | tf_op jit(solution)/shard_map/pick/pallas_call | solution.py:417
  1.8 3.0 %collective-permute-start.2 = (bf16[256,512]{1,0:T(8,128)(2,1)S(1)}, bf16[256,512]{1,0:T(8,128)(2,1)S(1)}, u32[]{:S(2)}, u32[]{:S(2)}) collective-permute-start(bf16[256,512]{1,0:T(8,128)(2,1)S(1)} %get-tuple-element.57.refs_0_), channel_id=1, source_target_pairs={{0,8},{1,17},{2,10},{3,19},{4,12},{5,21},{6,14},{7,23},{8,0},{9,25... | collective-permute-start | bytes 786440 | tf_op jit(solution)/shard_map/ppermute | solution.py:427
  6.6 2.5 %collective-permute-done.2.refs_2_ = bf16[256,512]{1,0:T(8,128)(2,1)S(1)} collective-permute-done((bf16[256,512]{1,0:T(8,128)(2,1)S(1)}, bf16[256,512]{1,0:T(8,128)(2,1)S(1)}, u32[]{:S(2)}, u32[]{:S(2)}) %collective-permute-start.2) | collective-permute-done | bytes 262176 | tf_op jit(solution)/shard_map/ppermute | solution.py:427
  9.1 2.0 %collective-permute-start.4 = (bf16[256,512]{1,0:T(8,128)(2,1)S(1)}, bf16[256,512]{1,0:T(8,128)(2,1)S(1)}, u32[]{:S(2)}, u32[]{:S(2)}) collective-permute-start(bf16[256,512]{1,0:T(8,128)(2,1)S(1)} %collective-permute-done.2.refs_2_), channel_id=1, source_target_pairs={{0,16},{1,9},{2,18},{3,11},{4,20},{5,13},{6,22},{7,15},{8,24},{9,1... | collective-permute-start | bytes 786440 | tf_op jit(solution)/shard_map/ppermute | solution.py:427
  12.8 1.9 %prepare.1 = (bf16[2,256,256]{2,1,0:T(8,128)(2,1)S(1)}, bf16[2,256,256]{2,1,0:T(8,128)(2,1)S(1)}, s32[2,256]{1,0:T(2,128)S(1)}, bf16[4,16,128]{2,1,0:T(8,128)(2,...) custom-call(s32[4]{0:T(128)S(1)} %pad_add_fusion.1.info, ...), custom_call_target="tpu_custom_call" | custom-call | flops 134217728 | bytes 3957760 | tf_op jit(solution)/shard_map/prepare/pallas_call | solution.py:35
  17.1 2.6 %project.1 = (bf16[2,256,512]{2,1,0:T(8,128)(2,1)S(1)}, bf16[2,256,256]{2,1,0:T(8,128)(2,1)S(1)}, bf16[2,256,256]{2,1,0:T(8,128)(2,1)S(1)}, bf16[2,256,256]{2,1,...) custom-call(s32[4]{0:T(128)S(1)} %pad_add_fusion.1.info, ...), custom_call_target="tpu_custom_call" | custom-call | flops 1073741824 | bytes 8460288 | tf_op jit(solution)/shard_map/project/pallas_call | solution.py:35
  19.7 4.2 %collective-permute-start.10 = (bf16[64,256]{1,0:T(8,128)(2,1)S(1)}, bf16[64,256]{1,0:T(8,128)(2,1)S(1)}, u32[]{:S(2)}, u32[]{:S(2)}) collective-permute-start(bf16[64,256]{1,0:T(8,128)(2,1)S(1)} %get-tuple-element.86), channel_id=1, source_target_pairs={{0,6},{1,7},{2,4},{3,5},{4,2},{5,3},{6,0},{7,1},{8,14},{9,15},{10,... | collective-permute-start | bytes 98312 | tf_op jit(solution)/shard_map/ppermute | solution.py:407
  24.5 2.7 %attend.1 = (bf16[2,256,256]{2,1,0:T(8,128)(2,1)S(1)}, bf16[2,256,256]{2,1,0:T(8,128)(2,1)S(1)}, bf16[2,256,256]{2,1,0:T(8,128)(2,1)S(1)}) custom-call(s32[4]{0:T(128)S(1)} %pad_add_fusion.1.info, bf16[2,256,256]{2,1,0:T(8,128)(2,1)S(1)} %get-tuple-element.77.qa_in, bf16[2,256,256]{2,1,0:T(8,128)(2,1)S(1)} %get-tuple-element.69.kb_in.kb, ...), custom_call_target="tpu_custom_call" | custom-call | flops 402653184 | bytes 2883584 | tf_op jit(solution)/shard_map/attend/pallas_call | solution.py:35
  28.7 2.1 %finish.1 = (bf16[256,256]{1,0:T(8,128)(2,1)S(1)}, f32[2,256,256]{2,1,0:T(8,128)S(1)}, bf16[2,256,256]{2,1,0:T(8,128)(2,1)S(1)}) custom-call(s32[4]{0:T(128)S(1)} %pad_add_fusion.1.info, f32[1,256]{1,0:T(1,128)S(1)} %get-tuple-element.59.rate, bf16[2,256,256]{2,1,0:T(8,128)(2,1)S(1)} %get-tuple-element.69.kb_in.kb, ...), custom_call_target="tpu_custom_call" | custom-call | flops 402653184 | bytes 6788096 | tf_op jit(solution)/shard_map/finish/pallas_call | solution.py:35
  30.9 1.5 %collective-permute-done.11.row_came = bf16[2,256,256]{2,1,0:T(8,128)(2,1)S(1)} collective-permute-done((bf16[2,256,256]{2,1,0:T(8,128)(2,1)S(1)}, bf16[2,256,256]{2,1,0:T(8,128)(2,1)S(1)}, u32[]{:S(2)}, u32[]{:S(2)}) %collective-permute-start.11) | collective-permute-done | bytes 262176 | tf_op jit(solution)/shard_map/ppermute | solution.py:410
  33.3 1.6 %collective-permute-start.12 = (bf16[272,256]{1,0:T(8,128)(2,1)S(1)}, bf16[272,256]{1,0:T(8,128)(2,1)S(1)}, u32[]{:S(2)}, u32[]{:S(2)}) collective-permute-start(bf16[272,256]{1,0:T(8,128)(2,1)S(1)} %get-tuple-element.91), channel_id=1, source_target_pairs={{0,8},{8,0},{16,24},{24,16},{1,9},{9,1},{17,25},{25,17},{2,10},{10... | collective-permute-start | bytes 417800 | tf_op jit(solution)/shard_map/ppermute | solution.py:404
  34.9 1.5 %collective-permute-start.13 = (bf16[272,256]{1,0:T(8,128)(2,1)S(1)}, bf16[272,256]{1,0:T(8,128)(2,1)S(1)}, u32[]{:S(2)}, u32[]{:S(2)}) collective-permute-start(bf16[272,256]{1,0:T(8,128)(2,1)S(1)} %get-tuple-element.97), channel_id=1, source_target_pairs={{0,16},{8,24},{16,0},{24,8},{1,17},{9,25},{17,1},{25,9},{2,18},{10... | collective-permute-start | bytes 417800 | tf_op jit(solution)/shard_map/ppermute | solution.py:404
  36.9 2.7 %collective-permute-done.12.refs_1_ = bf16[272,256]{1,0:T(8,128)(2,1)S(1)} collective-permute-done((bf16[272,256]{1,0:T(8,128)(2,1)S(1)}, bf16[272,256]{1,0:T(8,128)(2,1)S(1)}, u32[]{:S(2)}, u32[]{:S(2)}) %collective-permute-start.12) | collective-permute-done | bytes 139296 | tf_op jit(solution)/shard_map/ppermute | solution.py:404
  39.6 1.5 %outward.1 = (bf16[256,256]{1,0:T(8,128)(2,1)S(1)}, bf16[256,256]{1,0:T(8,128)(2,1)S(1)}) custom-call(s32[4]{0:T(128)S(1)} %pad_add_fusion.1.info, bf16[2,256,256]{2,1,0:T(8,128)(2,1)S(1)} %get-tuple-element.77.qa_in, bf16[2,256,256]{2,1,0:T(8,128)(2,1)S(1)} %get-tuple-element.69.kb_in.kb, bf16[2,256,256]{2,1,0:T(8,128)(2,1)S(1)} %get-tuple-element.78.v_in, ...), custom_call_target="tpu_custom_call" | custom-call | flops 134217728 | bytes 1703936 | tf_op jit(solution)/shard_map/outward/pallas_call | solution.py:35
  42.0 1.2 %collective-permute-done.13.refs_0_ = bf16[272,256]{1,0:T(8,128)(2,1)S(1)} collective-permute-done((bf16[272,256]{1,0:T(8,128)(2,1)S(1)}, bf16[272,256]{1,0:T(8,128)(2,1)S(1)}, u32[]{:S(2)}, u32[]{:S(2)}) %collective-permute-start.13) | collective-permute-done | bytes 139296 | tf_op jit(solution)/shard_map/ppermute | solution.py:404
  44.2 2.4 %collective-permute-start.15 = (bf16[128,256]{1,0:T(8,128)(2,1)S(1)}, bf16[128,256]{1,0:T(8,128)(2,1)S(1)}, u32[]{:S(2)}, u32[]{:S(2)}) collective-permute-start(bf16[128,256]{1,0:T(8,128)(2,1)S(1)} %get-tuple-element.99), channel_id=1, source_target_pairs={{0,6},{1,7},{2,4},{3,5},{4,2},{5,3},{6,0},{7,1},{8,14},{9,15},{10,... | collective-permute-start | bytes 196616 | tf_op jit(solution)/shard_map/ppermute | solution.py:407
  46.8 1.8 %collective-permute-start.18 = (bf16[128,256]{1,0:T(8,128)(2,1)S(1)}, bf16[128,256]{1,0:T(8,128)(2,1)S(1)}, u32[]{:S(2)}, u32[]{:S(2)}) collective-permute-start(bf16[128,256]{1,0:T(8,128)(2,1)S(1)} %get-tuple-element.103), channel_id=1, source_target_pairs={{0,4},{1,5},{2,6},{3,7},{4,0},{5,1},{6,2},{7,3},{8,12},{9,13},{10,... | collective-permute-start | bytes 196616 | tf_op jit(solution)/shard_map/ppermute | solution.py:407
  48.6 1.9 %collective-permute-done.15.refs_1_ = bf16[128,256]{1,0:T(8,128)(2,1)S(1)} collective-permute-done((bf16[128,256]{1,0:T(8,128)(2,1)S(1)}, bf16[128,256]{1,0:T(8,128)(2,1)S(1)}, u32[]{:S(2)}, u32[]{:S(2)}) %collective-permute-start.15) | collective-permute-done | bytes 65568 | tf_op jit(solution)/shard_map/ppermute | solution.py:407
  50.5 1.6 %result.1 = bf16[256,512]{1,0:T(8,128)(2,1)} custom-call(s32[4]{0:T(128)S(1)} %pad_add_fusion.1.info, bf16[2,256,512]{2,1,0:T(8,128)(2,1)S(1)} %get-tuple-element.83.emb, bf16[256,256]{1,0:T(8,128)(2,1)S(1)} %get-tuple-element.104.att_own, bf16[256,256]{1,0:T(8,128)(2,1)S(1)} %collective-permute-done.16.att_came, bf16[512,512]{1,0:T(8,128)(2,1)S(1)} %get-tuple-element.106.w_out), custom_call_target="tpu_custom_call" | custom-call | flops 134217728 | bytes 1572864 | tf_op jit(solution)/shard_map/result/pallas_call | solution.py:35
  52.8 3.0 %collective-permute-start.21 = (bf16[128,256]{1,0:T(8,128)(2,1)S(1)}, bf16[128,256]{1,0:T(8,128)(2,1)S(1)}, u32[]{:S(2)}, u32[]{:S(2)}) collective-permute-start(bf16[128,256]{1,0:T(8,128)(2,1)S(1)} %add_up.1.refs_0_), channel_id=1, source_target_pairs={{0,6},{1,7},{2,4},{3,5},{4,2},{5,3},{6,0},{7,1},{8,14},{9,15},{10,... | collective-permute-start | bytes 196616 | tf_op jit(solution)/shard_map/ppermute | solution.py:407
  55.8 1.4 %collective-permute-start.19 = (bf16[128,256]{1,0:T(8,128)(2,1)S(1)}, bf16[128,256]{1,0:T(8,128)(2,1)S(1)}, u32[]{:S(2)}, u32[]{:S(2)}) collective-permute-start(bf16[128,256]{1,0:T(8,128)(2,1)S(1)} %add_up.1.refs_0_), channel_id=1, source_target_pairs={{0,2},{1,3},{2,0},{3,1},{4,6},{5,7},{6,4},{7,5},{8,10},{9,11},{10,... | collective-permute-start | bytes 196616 | tf_op jit(solution)/shard_map/ppermute | solution.py:407
  57.2 2.0 %collective-permute-done.21.refs_3_ = bf16[128,256]{1,0:T(8,128)(2,1)S(1)} collective-permute-done((bf16[128,256]{1,0:T(8,128)(2,1)S(1)}, bf16[128,256]{1,0:T(8,128)(2,1)S(1)}, u32[]{:S(2)}, u32[]{:S(2)}) %collective-permute-start.21) | collective-permute-done | bytes 65568 | tf_op jit(solution)/shard_map/ppermute | solution.py:407
  59.3 1.7 %collective-permute-done.20.refs_2_ = bf16[128,256]{1,0:T(8,128)(2,1)S(1)} collective-permute-done((bf16[128,256]{1,0:T(8,128)(2,1)S(1)}, bf16[128,256]{1,0:T(8,128)(2,1)S(1)}, u32[]{:S(2)}, u32[]{:S(2)}) %collective-permute-start.20) | collective-permute-done | bytes 65568 | tf_op jit(solution)/shard_map/ppermute | solution.py:407
  62.4 1.4 %assemble.1 = bf16[512,512]{1,0:T(8,128)(2,1)} custom-call(s32[4]{0:T(128)S(1)} %pad_add_fusion.1.info, bf16[128,256]{1,0:T(8,128)(2,1)S(1)} %add_up.1.refs_0_, bf16[128,256]{1,0:T(8,128)(2,1)S(1)} %collective-permute-done.19.refs_1_, bf16[128,256]{1,0:T(8,128)(2,1)S(1)} %collective-permute-done.20.refs_2_, ...), custom_call_target="tpu_custom_call" | custom-call | flops 262144 | bytes 1048576 | tf_op jit(solution)/shard_map/assemble/pallas_call | solution.py:35
  (58 shorter events, 12.9 us)
Async XLA Ops:
  1.8 7.4 %collective-permute-start.2 = (bf16[256,512]{1,0:T(8,128)(2,1)S(1)}, bf16[256,512]{1,0:T(8,128)(2,1)S(1)}, u32[]{:S(2)}, u32[]{:S(2)}) collective-permute-start(bf16[256,512]{1,0:T(8,128)(2,1)S(1)} %get-tuple-element.57.refs_0_), channel_id=1, source_target_pairs={{0,8},{1,17},{2,10},{3,19},{4,12},{5,21},{6,14},{7,23},{8,0},{9,25... | collective-permute-start | bytes 786440 | tf_op jit(solution)/shard_map/ppermute | solution.py:427
  5.5 6.6 %collective-permute-start = (bf16[256,512]{1,0:T(8,128)(2,1)S(1)}, bf16[256,512]{1,0:T(8,128)(2,1)S(1)}, u32[]{:S(2)}, u32[]{:S(2)}) collective-permute-start(bf16[256,512]{1,0:T(8,128)(2,1)S(1)} %bitcast.11), channel_id=1, source_target_pairs={{0,1},{1,0},{2,3},{3,2},{4,5},{5,4},{6,7},{7,6},{8,9},{9,8},{10,11... | collective-permute-start | bytes 786440 | tf_op jit(solution)/shard_map/ppermute | solution.py:410
  6.0 8.7 %collective-permute-start.3 = (bf16[256,512]{1,0:T(8,128)(2,1)S(1)}, bf16[256,512]{1,0:T(8,128)(2,1)S(1)}, u32[]{:S(2)}, u32[]{:S(2)}) collective-permute-start(bf16[256,512]{1,0:T(8,128)(2,1)S(1)} %get-tuple-element.58.refs_1_), channel_id=1, source_target_pairs={{0,8},{1,17},{2,10},{3,19},{4,12},{5,21},{6,14},{7,23},{8,0},{9,25... | collective-permute-start | bytes 786440 | tf_op jit(solution)/shard_map/ppermute | solution.py:427
  9.1 6.4 %collective-permute-start.4 = (bf16[256,512]{1,0:T(8,128)(2,1)S(1)}, bf16[256,512]{1,0:T(8,128)(2,1)S(1)}, u32[]{:S(2)}, u32[]{:S(2)}) collective-permute-start(bf16[256,512]{1,0:T(8,128)(2,1)S(1)} %collective-permute-done.2.refs_2_), channel_id=1, source_target_pairs={{0,16},{1,9},{2,18},{3,11},{4,20},{5,13},{6,22},{7,15},{8,24},{9,1... | collective-permute-start | bytes 786440 | tf_op jit(solution)/shard_map/ppermute | solution.py:427
  14.7 2.0 %collective-permute-start.6 = (bf16[256,512]{1,0:T(8,128)(2,1)S(1)}, bf16[256,512]{1,0:T(8,128)(2,1)S(1)}, u32[]{:S(2)}, u32[]{:S(2)}) collective-permute-start(bf16[256,512]{1,0:T(8,128)(2,1)S(1)} %collective-permute-done.3.refs_0_), channel_id=1, source_target_pairs={{0,1},{1,0},{2,3},{3,2},{4,5},{5,4},{6,7},{7,6},{8,9},{9,8},{10,11... | collective-permute-start | bytes 786440 | tf_op jit(solution)/shard_map/ppermute | solution.py:410
  14.8 1.9 %collective-permute-start.5 = (bf16[256,512]{1,0:T(8,128)(2,1)S(1)}, bf16[256,512]{1,0:T(8,128)(2,1)S(1)}, u32[]{:S(2)}, u32[]{:S(2)}) collective-permute-start(bf16[256,512]{1,0:T(8,128)(2,1)S(1)} %collective-permute-done.2.refs_2_), channel_id=1, source_target_pairs={{0,1},{1,0},{2,3},{3,2},{4,5},{5,4},{6,7},{7,6},{8,9},{9,8},{10,11... | collective-permute-start | bytes 786440 | tf_op jit(solution)/shard_map/ppermute | solution.py:410
  15.5 1.5 %collective-permute-start.7 = (bf16[256,512]{1,0:T(8,128)(2,1)S(1)}, bf16[256,512]{1,0:T(8,128)(2,1)S(1)}, u32[]{:S(2)}, u32[]{:S(2)}) collective-permute-start(bf16[256,512]{1,0:T(8,128)(2,1)S(1)} %collective-permute-done.4.refs_1_), channel_id=1, source_target_pairs={{0,1},{1,0},{2,3},{3,2},{4,5},{5,4},{6,7},{7,6},{8,9},{9,8},{10,11... | collective-permute-start | bytes 786440 | tf_op jit(solution)/shard_map/ppermute | solution.py:410
  19.7 8.1 %collective-permute-start.10 = (bf16[64,256]{1,0:T(8,128)(2,1)S(1)}, bf16[64,256]{1,0:T(8,128)(2,1)S(1)}, u32[]{:S(2)}, u32[]{:S(2)}) collective-permute-start(bf16[64,256]{1,0:T(8,128)(2,1)S(1)} %get-tuple-element.86), channel_id=1, source_target_pairs={{0,6},{1,7},{2,4},{3,5},{4,2},{5,3},{6,0},{7,1},{8,14},{9,15},{10,... | collective-permute-start | bytes 98312 | tf_op jit(solution)/shard_map/ppermute | solution.py:407
  23.9 4.8 %collective-permute-start.9 = (bf16[64,256]{1,0:T(8,128)(2,1)S(1)}, bf16[64,256]{1,0:T(8,128)(2,1)S(1)}, u32[]{:S(2)}, u32[]{:S(2)}) collective-permute-start(bf16[64,256]{1,0:T(8,128)(2,1)S(1)} %get-tuple-element.86), channel_id=1, source_target_pairs={{0,4},{1,5},{2,6},{3,7},{4,0},{5,1},{6,2},{7,3},{8,12},{9,13},{10,... | collective-permute-start | bytes 98312 | tf_op jit(solution)/shard_map/ppermute | solution.py:407
  23.9 3.9 %collective-permute-start.8 = (bf16[64,256]{1,0:T(8,128)(2,1)S(1)}, bf16[64,256]{1,0:T(8,128)(2,1)S(1)}, u32[]{:S(2)}, u32[]{:S(2)}) collective-permute-start(bf16[64,256]{1,0:T(8,128)(2,1)S(1)} %get-tuple-element.85), channel_id=1, source_target_pairs={{0,2},{1,3},{2,0},{3,1},{4,6},{5,7},{6,4},{7,5},{8,10},{9,11},{10,... | collective-permute-start | bytes 98312 | tf_op jit(solution)/shard_map/ppermute | solution.py:407
  30.8 1.6 %collective-permute-start.11 = (bf16[2,256,256]{2,1,0:T(8,128)(2,1)S(1)}, bf16[2,256,256]{2,1,0:T(8,128)(2,1)S(1)}, u32[]{:S(2)}, u32[]{:S(2)}) collective-permute-start(bf16[2,256,256]{2,1,0:T(8,128)(2,1)S(1)} %get-tuple-element.88), channel_id=1, source_target_pairs={{0,1},{1,0},{2,3},{3,2},{4,5},{5,4},{6,7},{7,6},{8,9},{9,8},{10,11... | collective-permute-start | bytes 786440 | tf_op jit(solution)/shard_map/ppermute | solution.py:410
  33.3 6.3 %collective-permute-start.12 = (bf16[272,256]{1,0:T(8,128)(2,1)S(1)}, bf16[272,256]{1,0:T(8,128)(2,1)S(1)}, u32[]{:S(2)}, u32[]{:S(2)}) collective-permute-start(bf16[272,256]{1,0:T(8,128)(2,1)S(1)} %get-tuple-element.91), channel_id=1, source_target_pairs={{0,8},{8,0},{16,24},{24,16},{1,9},{9,1},{17,25},{25,17},{2,10},{10... | collective-permute-start | bytes 417800 | tf_op jit(solution)/shard_map/ppermute | solution.py:404
  34.9 8.4 %collective-permute-start.13 = (bf16[272,256]{1,0:T(8,128)(2,1)S(1)}, bf16[272,256]{1,0:T(8,128)(2,1)S(1)}, u32[]{:S(2)}, u32[]{:S(2)}) collective-permute-start(bf16[272,256]{1,0:T(8,128)(2,1)S(1)} %get-tuple-element.97), channel_id=1, source_target_pairs={{0,16},{8,24},{16,0},{24,8},{1,17},{9,25},{17,1},{25,9},{2,18},{10... | collective-permute-start | bytes 417800 | tf_op jit(solution)/shard_map/ppermute | solution.py:404
  36.4 6.9 %collective-permute-start.14 = (bf16[272,256]{1,0:T(8,128)(2,1)S(1)}, bf16[272,256]{1,0:T(8,128)(2,1)S(1)}, u32[]{:S(2)}, u32[]{:S(2)}) collective-permute-start(bf16[272,256]{1,0:T(8,128)(2,1)S(1)} %get-tuple-element.98), channel_id=1, source_target_pairs={{0,24},{8,16},{16,8},{24,0},{1,25},{9,17},{17,9},{25,1},{2,26},{10... | collective-permute-start | bytes 417800 | tf_op jit(solution)/shard_map/ppermute | solution.py:404
  42.0 8.6 %collective-permute-start.16 = (bf16[256,256]{1,0:T(8,128)(2,1)S(1)}, bf16[256,256]{1,0:T(8,128)(2,1)S(1)}, u32[]{:S(2)}, u32[]{:S(2)}) collective-permute-start(bf16[256,256]{1,0:T(8,128)(2,1)S(1)} %get-tuple-element.100), channel_id=1, source_target_pairs={{0,1},{1,0},{2,3},{3,2},{4,5},{5,4},{6,7},{7,6},{8,9},{9,8},{10,11... | collective-permute-start | bytes 393224 | tf_op jit(solution)/shard_map/ppermute | solution.py:410
  44.2 6.4 %collective-permute-start.15 = (bf16[128,256]{1,0:T(8,128)(2,1)S(1)}, bf16[128,256]{1,0:T(8,128)(2,1)S(1)}, u32[]{:S(2)}, u32[]{:S(2)}) collective-permute-start(bf16[128,256]{1,0:T(8,128)(2,1)S(1)} %get-tuple-element.99), channel_id=1, source_target_pairs={{0,6},{1,7},{2,4},{3,5},{4,2},{5,3},{6,0},{7,1},{8,14},{9,15},{10,... | collective-permute-start | bytes 196616 | tf_op jit(solution)/shard_map/ppermute | solution.py:407
  46.5 5.7 %collective-permute-start.17 = (bf16[128,256]{1,0:T(8,128)(2,1)S(1)}, bf16[128,256]{1,0:T(8,128)(2,1)S(1)}, u32[]{:S(2)}, u32[]{:S(2)}) collective-permute-start(bf16[128,256]{1,0:T(8,128)(2,1)S(1)} %get-tuple-element.102), channel_id=1, source_target_pairs={{0,2},{1,3},{2,0},{3,1},{4,6},{5,7},{6,4},{7,5},{8,10},{9,11},{10,... | collective-permute-start | bytes 196616 | tf_op jit(solution)/shard_map/ppermute | solution.py:407
  46.8 5.4 %collective-permute-start.18 = (bf16[128,256]{1,0:T(8,128)(2,1)S(1)}, bf16[128,256]{1,0:T(8,128)(2,1)S(1)}, u32[]{:S(2)}, u32[]{:S(2)}) collective-permute-start(bf16[128,256]{1,0:T(8,128)(2,1)S(1)} %get-tuple-element.103), channel_id=1, source_target_pairs={{0,4},{1,5},{2,6},{3,7},{4,0},{5,1},{6,2},{7,3},{8,12},{9,13},{10,... | collective-permute-start | bytes 196616 | tf_op jit(solution)/shard_map/ppermute | solution.py:407
  52.8 6.5 %collective-permute-start.21 = (bf16[128,256]{1,0:T(8,128)(2,1)S(1)}, bf16[128,256]{1,0:T(8,128)(2,1)S(1)}, u32[]{:S(2)}, u32[]{:S(2)}) collective-permute-start(bf16[128,256]{1,0:T(8,128)(2,1)S(1)} %add_up.1.refs_0_), channel_id=1, source_target_pairs={{0,6},{1,7},{2,4},{3,5},{4,2},{5,3},{6,0},{7,1},{8,14},{9,15},{10,... | collective-permute-start | bytes 196616 | tf_op jit(solution)/shard_map/ppermute | solution.py:407
  55.8 5.3 %collective-permute-start.20 = (bf16[128,256]{1,0:T(8,128)(2,1)S(1)}, bf16[128,256]{1,0:T(8,128)(2,1)S(1)}, u32[]{:S(2)}, u32[]{:S(2)}) collective-permute-start(bf16[128,256]{1,0:T(8,128)(2,1)S(1)} %add_up.1.refs_0_), channel_id=1, source_target_pairs={{0,4},{1,5},{2,6},{3,7},{4,0},{5,1},{6,2},{7,3},{8,12},{9,13},{10,... | collective-permute-start | bytes 196616 | tf_op jit(solution)/shard_map/ppermute | solution.py:407
  55.8 5.2 %collective-permute-start.19 = (bf16[128,256]{1,0:T(8,128)(2,1)S(1)}, bf16[128,256]{1,0:T(8,128)(2,1)S(1)}, u32[]{:S(2)}, u32[]{:S(2)}) collective-permute-start(bf16[128,256]{1,0:T(8,128)(2,1)S(1)} %add_up.1.refs_0_), channel_id=1, source_target_pairs={{0,2},{1,3},{2,0},{3,1},{4,6},{5,7},{6,4},{7,5},{8,10},{9,11},{10,... | collective-permute-start | bytes 196616 | tf_op jit(solution)/shard_map/ppermute | solution.py:407
  57.2 4.3 %collective-permute-start.22 = (bf16[128,256]{1,0:T(8,128)(2,1)S(1)}, bf16[128,256]{1,0:T(8,128)(2,1)S(1)}, u32[]{:S(2)}, u32[]{:S(2)}) collective-permute-start(bf16[128,256]{1,0:T(8,128)(2,1)S(1)} %add_up.1.refs_0_), channel_id=1, source_target_pairs={{0,1},{1,0},{2,3},{3,2},{4,5},{5,4},{6,7},{7,6},{8,9},{9,8},{10,11... | collective-permute-start | bytes 196616 | tf_op jit(solution)/shard_map/ppermute | solution.py:410
  59.3 2.3 %collective-permute-start.25 = (bf16[128,256]{1,0:T(8,128)(2,1)S(1)}, bf16[128,256]{1,0:T(8,128)(2,1)S(1)}, u32[]{:S(2)}, u32[]{:S(2)}) collective-permute-start(bf16[128,256]{1,0:T(8,128)(2,1)S(1)} %collective-permute-done.21.refs_3_), channel_id=1, source_target_pairs={{0,1},{1,0},{2,3},{3,2},{4,5},{5,4},{6,7},{7,6},{8,9},{9,8},{10,11... | collective-permute-start | bytes 196616 | tf_op jit(solution)/shard_map/ppermute | solution.py:410
  61.0 1.4 %collective-permute-start.23 = (bf16[128,256]{1,0:T(8,128)(2,1)S(1)}, bf16[128,256]{1,0:T(8,128)(2,1)S(1)}, u32[]{:S(2)}, u32[]{:S(2)}) collective-permute-start(bf16[128,256]{1,0:T(8,128)(2,1)S(1)} %collective-permute-done.19.refs_1_), channel_id=1, source_target_pairs={{0,1},{1,0},{2,3},{3,2},{4,5},{5,4},{6,7},{7,6},{8,9},{9,8},{10,11... | collective-permute-start | bytes 196616 | tf_op jit(solution)/shard_map/ppermute | solution.py:410
  (9 other events, 33.0 us)
